TPU v7x, 256 devices: a whole 4x4x8 slice. The times are simulated.
256 devices in a mesh: gx: 32 (over z, x_lo, core), gy: 8 (over y, x_hi).
Axes of the slice: x: 4 (x_hi: 2, x_lo: 2; x = x_hi * 2 + x_lo), y: 4, z: 8, core: 2. Of those that a mesh axis runs over, the one named last changes fastest.
Arguments:
- field: float32 [32, 128, 128, 256], P(None, 'gx', 'gy'), may hold values from -6 to 6
- spec_weight: float32 [2, 32, 32, 32, 32, 32], P(None, None, 'gx', 'gy'), may hold values from -6 to 6
- dw_kernel: float32 [32, 3, 3, 3], replicated, may hold values from -1.25 to 1.25
- point_weight: float32 [32, 32], replicated, may hold values from -1 to 1
- bias: float32 [32], replicated, may hold values from -3 to 3
Outputs:
- evolved: float32 [32, 128, 128, 256], P(None, 'gx', 'gy')
All inputs are finite; a program needn't handle non-finite values.
Results may differ from a plain program's by a relative error of at most 0.00005.
Values sent between devices are 32-bit elements; how exact they have to be, the bound alone decides.
No kernel may reach another device: no remote copies, remote signals or barrier semaphores. Data moves between devices by JAX's collectives and lax.ppermute only.
A program may use at most 128 MiB of HBM per device.

v0:
```python
import jax
import jax.numpy as jnp
from jax import lax
from jax.sharding import PartitionSpec as P

full_turn = 6.283185307179586


def extended(array, sides, width):
    for axis, dim in sides:
        count, length = (lax.axis_size(axis), array.shape[dim])
        up = [(i, (i + 1) % count) for i in range(count)]
        down = [(j, i) for i, j in up]
        last = lax.slice_in_dim(array, length - width, length, axis=dim)
        leading = lax.slice_in_dim(array, 0, width, axis=dim)
        before = lax.ppermute(last, axis, up)
        after = lax.ppermute(leading, axis, down)
        array = jnp.concatenate([before, array, after], axis=dim)
    return array


def kept_index(modes, length):
    index = jnp.arange(modes, dtype=jnp.int32)
    return jnp.where(index < modes // 2, index, index + length - modes)


def phase_table(freqs, positions, length):
    product = freqs[:, None] * positions[None, :] % length
    angle = product.astype(jnp.float32) * (full_turn / length)
    return (jnp.cos(angle), jnp.sin(angle))


def complex_table(cosine, sine_tab, direction):
    upper = jnp.stack([cosine, direction * sine_tab])
    lower = jnp.stack([-direction * sine_tab, cosine])
    return jnp.stack([upper, lower])


def on_device(field, spec_weight, dw_kernel, point_weight, bias):
    exact_mode = lax.Precision.HIGHEST
    chans, rows_x, rows_y, depth = field.shape
    modes = spec_weight.shape[1]
    full_x = rows_x * lax.axis_size("gx")
    full_y = rows_y * lax.axis_size("gy")
    zfreqs = jnp.arange(modes, dtype=jnp.int32)
    zcosine, zsine = phase_table(zfreqs, jnp.arange(depth, dtype=jnp.int32), depth)
    forward_z = jnp.concatenate([zcosine, -zsine], axis=0)
    zspec = jnp.einsum("tz,cxyz->tcxy", forward_z, field, precision=exact_mode).reshape(
        2, modes, chans, rows_x, rows_y
    )
    yfreqs = kept_index(modes, full_y)
    wide = lax.all_to_all(zspec, "gy", split_axis=1, concat_axis=4, tiled=True)
    ycosine, ysine = phase_table(yfreqs, jnp.arange(full_y, dtype=jnp.int32), full_y)
    ytable = complex_table(ycosine, ysine, 1.0)
    yspec = jnp.einsum("srny,rkcxy->snxkc", ytable, wide, precision=exact_mode)
    yspec = yspec.reshape(2, modes, rows_x, -1)
    columns = lax.all_to_all(yspec, "gx", split_axis=1, concat_axis=2, tiled=True)
    xcosine, xsine = phase_table(
        kept_index(modes, full_x), jnp.arange(full_x, dtype=jnp.int32), full_x
    )
    xtable = complex_table(xcosine, xsine, 1.0)
    xspec = jnp.einsum("srma,rnak->snmk", xtable, columns, precision=exact_mode)
    cols_loc = xspec.shape[1]
    xin = xspec.reshape(2, cols_loc, modes, -1, chans)
    weight_re = spec_weight[0]
    weight_im = spec_weight[1]
    stacked = jnp.stack([jnp.stack([weight_re, -weight_im]), jnp.stack([weight_im, weight_re])])
    mixed = jnp.einsum("rnmki,srmnkio->snmko", xin, stacked, precision=exact_mode)
    mixed = mixed.reshape(2, cols_loc, modes, -1)
    xinverse = complex_table(xcosine / full_x, xsine / full_x, -1.0)
    back_x = jnp.einsum("srma,rnmk->snak", xinverse, mixed, precision=exact_mode)
    rows_back = lax.all_to_all(back_x, "gx", split_axis=2, concat_axis=1, tiled=True)
    yinverse = complex_table(ycosine / full_y, ysine / full_y, -1.0)
    tall = jnp.einsum("srnb,rnxk->sbxk", yinverse, rows_back, precision=exact_mode)
    zback = lax.all_to_all(tall, "gy", split_axis=1, concat_axis=3, tiled=True)
    weights_z = jnp.where(zfreqs == 0, 1.0, 2.0).astype(jnp.float32)[:, None] / depth
    backward_z = jnp.stack([weights_z * zcosine, -weights_z * zsine])
    zcells = zback.reshape(2, rows_y, rows_x, modes, chans)
    spectral = jnp.einsum("skz,syxkc->cxyz", backward_z, zcells, precision=exact_mode)
    framed = extended(field, (("gx", 1), ("gy", 2)), 1)
    framed = jnp.concatenate([framed[..., -1:], framed, framed[..., :1]], axis=3)
    conv = jnp.zeros(field.shape, jnp.float32)
    for shift_x in range(3):
        for shift_y in range(3):
            for shift_z in range(3):
                tap = dw_kernel[:, shift_x, shift_y, shift_z][:, None, None, None]
                conv = (
                    conv
                    + tap
                    * framed[
                        :,
                        shift_x : shift_x + rows_x,
                        shift_y : shift_y + rows_y,
                        shift_z : shift_z + depth,
                    ]
                )
    pointwise = jnp.dot(point_weight.T, field.reshape(chans, -1), precision=exact_mode).reshape(
        field.shape
    )
    total = spectral + conv + pointwise + bias[:, None, None, None]
    return jax.nn.gelu(total)


def solution(mesh):
    placed = (P(None, "gx", "gy", None), P(None, None, "gx", "gy", None, None), P(), P(), P())
    return jax.shard_map(
        on_device, mesh=mesh, in_specs=placed, out_specs=P(None, "gx", "gy", None), check_vma=False
    )
```

profile of v0, /device:TPU:1, one launch (start us, length us, event | category | flops | bytes accessed | tf_op | source)
XLA Modules:
  0.0 143.8 jit_solution(5653876701960673272)
XLA Ops:
  0.0 0.1 sine_negate_fusion
  0.2 4.2 %fusion.61 = f32[64,32,4,16]{0,1,3,2:T(8,128)S(1)} fusion(f32[32,256]{1,0:T(8,128)S(1)} %get-tuple-element.53, f32[32,256]{1,0:T(8,128)S(1)} %get-tuple-element.54, f32[32,4,16,256]{3,2,1,0:T(8,128)} %param.5), kind=kOutput, calls=%fused_computation.102 | convolution fusion | flops 402669568 | bytes 2686976 | tf_op jit(solution)/shard_map/tz,cxyz->tcxy/dot_general | solution.py:48
  4.4 1.2 reshape.378
  5.6 2.9 %copy.48 = f32[2,32,32,4,16]{2,4,3,0,1:T(8,128)} copy(f32[2,32,32,4,16]{1,0,2,4,3:T(2,128)S(1)} %reshape.378) | data formatting | bytes 1048576 | tf_op jit(solution)/shard_map/reshape | solution.py:48
  8.5 3.3 %reshape.404 = f32[8,1,16384]{2,1,0:T(1,128)} reshape(f32[32,2,4,16,32]{4,3,2,1,0:T(8,128)} %bitcast.180) | data formatting | bytes 1048576
  11.8 7.5 %all-to-all-start = ((f32[8,1,16384]{2,1,0:T(1,128)}), f32[8,1,16384]{2,1,0:T(1,128)S(1)}, u32[]{:S(2)}, u32[]{:S(2)}) async-start(f32[8,1,16384]{2,1,0:T(1,128)} %reshape.404), calls=%async_computation | async-start | bytes 1048576 | tf_op jit(solution)/shard_map/all_to_all | solution.py:52
  19.3 0.0 copy-start.5
  19.3 1.2 copy.47
  20.5 0.0 copy-start.6
  20.5 1.1 fusion.103
  21.6 1.2 collective-permute-start
  22.7 0.0 collective-permute-start.1
  22.7 0.2 broadcast_multiply_fusion.1
  22.9 0.3 slice.210
  23.2 0.0 copy-start.13
  23.2 1.2 fusion.100
  24.4 0.7 slice_bitcast_fusion.26
  25.0 2.5 %maximum_bitcast_fusion.1 = f32[1,2,32,1,4,32,32]{6,5,4,2,1,3,0:T(8,128)} fusion(f32[1,32,1,4,32,32]{5,4,3,1,0,2:T(8,128)S(1)} %get-tuple-element.52, f32[1,32,1,4,32,32]{5,4,3,1,0,2:T(8,128)S(1)} %get-tuple-element.5), kind=kLoop, calls=%fused_computation.9 | loop fusion | flops 262144 | bytes 2097152 | tf_op jit(solution)/shard_map/stack | solution.py:67
  27.5 2.5 %maximum_bitcast_fusion.2 = f32[1,2,32,1,4,32,32]{6,5,4,2,1,3,0:T(8,128)} fusion(f32[1,32,1,4,32,32]{5,4,3,2,1,0:T(8,128)S(1)} %get-tuple-element.6, f32[1,32,1,4,32,32]{5,4,3,2,1,0:T(8,128)S(1)} %slice.210), kind=kLoop, calls=%fused_computation.10 | loop fusion | flops 262144 | bytes 2097152 | tf_op jit(solution)/shard_map/stack | solution.py:67
  30.0 0.6 maximum_bitcast_fusion.7
  30.7 0.8 sine_multiply_fusion
  31.5 0.0 all-to-all-done
  31.5 0.6 broadcast.504
  32.0 1.9 %reduce = f32[8,16384]{1,0:T(8,128)S(1)} reduce(f32[8,1,16384]{2,1,0:T(1,128)S(1)} %all-to-all-done, f32[]{:T(128)} %broadcast.504), dimensions={1}, to_apply=%all_to_all.40.reduce_sub_computation | reduce | bytes 1048580 | tf_op jit(solution)/shard_map/all_to_all | solution.py:52
  34.0 2.0 %reshape.405 = f32[32,2,4,16,32]{4,3,2,1,0:T(8,128)} reshape(f32[8,16384]{1,0:T(8,128)S(1)} %reduce) | data formatting | bytes 1048576
  36.0 1.8 %copy.50 = f32[2,4,32,4,8,16]{2,5,4,3,1,0:T(8,128)S(1)} copy(f32[2,4,32,4,8,16]{2,5,3,0,1,4:T(8,128)} %bitcast.181) | data formatting | bytes 1048576 | tf_op jit(solution)/shard_map/all_to_all | solution.py:52
  37.8 3.5 %fusion.55 = f32[2,32,4,4,32]{1,4,0,2,3:T(8,128)S(1)} fusion(f32[2,4,32,4,128,1]{2,4,3,1,0,5:T(8,128)S(1)} %bitcast.182, f32[1,2,32,128]{3,2,1,0:T(8,128)S(1)} %get-tuple-element.55, f32[1,2,32,128]{3,2,1,0:T(8,128)S(1)} %get-tuple-element.56), kind=kOutput, calls=%fused_computation.91 | convolution fusion | flops 100679680 | bytes 720896 | tf_op jit(solution)/shard_map/srny,rkcxy->snxkc/dot_general | solution.py:55
  41.3 0.6 copy.88
  41.9 1.0 reshape.401
  42.8 14.5 %all-to-all-start.1 = ((f32[2,32,4,128]{3,2,0,1:T(4,128)}), f32[2,32,4,128]{3,2,0,1:T(4,128)S(1)}, u32[]{:S(2)}, u32[]{:S(2)}) async-start(f32[2,32,4,128]{3,2,0,1:T(4,128)} %reshape.401), calls=%async_computation.1 | async-start | bytes 262144 | tf_op jit(solution)/shard_map/all_to_all | solution.py:57
  57.3 0.0 collective-permute-done
  57.3 1.1 constant_dynamic-update-slice_fusion.2
  58.4 1.2 constant_dynamic-update-slice_fusion.1
  59.6 0.0 collective-permute-done.1
  59.6 1.1 constant_dynamic-update-slice_fusion
  60.7 1.7 %copy-done.2 = f32[32,6,16,256]{3,0,2,1:T(8,128)} copy-done((f32[32,6,16,256]{3,0,2,1:T(8,128)}, f32[32,6,16,256]{3,0,2,1:T(8,128)S(1)}, u32[]{:S(2)}) %copy-start.2) | copy-done | bytes 3145752
  62.5 1.1 collective-permute-start.2
  63.6 4.0 %collective-permute-start.3 = (f32[32,6,1,256]{3,0,2,1:T(8,128)S(1)}, f32[32,6,1,256]{3,0,2,1:T(8,128)S(1)}, u32[]{:S(2)}, u32[]{:S(2)}) collective-permute-start(f32[32,6,1,256]{3,0,2,1:T(8,128)S(1)} %get-tuple-element.12), channel_id=1, source_target_pairs={{1,0},{2,1},{3,2},{4,3},{5,4},{6,5},{7,6},{0,7},{9,8},{10,9},{11,1... | collective-permute-start | bytes 589832 | tf_op jit(solution)/shard_map/ppermute | solution.py:17
  67.7 0.0 all-to-all-done.1
  67.7 0.2 convolution_bitcast_fusion.2
  67.9 0.1 reshape.391
  68.1 7.2 %fusion = f32[32,4,1,2,32,1]{4,2,5,3,1,0:T(1,128)S(1)} fusion(f32[2,32,4,32,1,1]{3,2,1,0,4,5:T(4,128)S(1)} %reshape.391, f32[1,2,32,1,4,32,32]{6,5,4,2,1,3,0:T(8,128)} %maximum_bitcast_fusion.2, f32[1,2,32,1,4,32,32]{6,5,4,2,1,3,0:T(8,128)} %maximum_bitcast_fusion.1), kind=kOutput, calls=%fused_computation.1 | convolution fusion | flops 6815744 | bytes 2162688 | tf_op jit(solution)/shard_map/rnmki,srmnkio->snmko/dot_general | solution.py:68
  75.4 0.1 reshape.393
  75.5 0.3 convolution_bitcast_fusion.1
  75.8 0.8 copy.55
  76.6 8.8 %all-to-all-start.2 = ((f32[2,1,128,128]{3,0,1,2:T(2,128)}), f32[2,1,128,128]{3,0,1,2:T(2,128)S(1)}, u32[]{:S(2)}, u32[]{:S(2)}) async-start(f32[2,1,128,128]{3,0,1,2:T(2,128)} %copy.55), calls=%async_computation.2 | async-start | bytes 262144 | tf_op jit(solution)/shard_map/all_to_all | solution.py:72
  85.4 1.4 slice_bitcast_fusion.25
  86.8 0.0 collective-permute-done.2
  86.8 0.0 collective-permute-done.3
  86.9 4.1 %pad_maximum_fusion.1 = f32[32,6,18,256]{3,0,2,1:T(8,128)} fusion(f32[32,6,1,256]{3,0,2,1:T(8,128)S(1)} %collective-permute-done.3, f32[32,6,16,256]{3,0,2,1:T(8,128)} %copy-done.2, f32[32,6,1,256]{3,0,2,1:T(8,128)S(1)} %collective-permute-done.2), kind=kLoop, calls=%fused_computation.11 | loop fusion | flops 1769472 | bytes 7077888 | tf_op jit(solution)/shard_map/concatenate | solution.py:18
  91.0 3.7 %all-to-all-done.2 = f32[2,1,128,128]{3,0,1,2:T(2,128)S(1)} async-done(((f32[2,1,128,128]{3,0,1,2:T(2,128)}), f32[2,1,128,128]{3,0,1,2:T(2,128)S(1)}, u32[]{:S(2)}, u32[]{:S(2)}) %all-to-all-start.2) | async-done | bytes 131104 | tf_op jit(solution)/shard_map/all_to_all | solution.py:72
  94.7 0.6 convolution_bitcast_fusion
  95.3 1.2 copy.58
  96.5 3.5 %all-to-all-start.3 = ((f32[2,128,4,128]{3,2,0,1:T(4,128)}), f32[2,128,4,128]{3,2,0,1:T(4,128)S(1)}, u32[]{:S(2)}, u32[]{:S(2)}) async-start(f32[2,128,4,128]{3,2,0,1:T(4,128)} %copy.58), calls=%async_computation.3 | async-start | bytes 1048576 | tf_op jit(solution)/shard_map/all_to_all | solution.py:75
  100.0 2.8 %fusion.101 = (f32[32,6,18,1]{3,0,2,1:T(8,128)S(1)}, f32[32,6,18,1]{3,0,2,1:T(8,128)S(1)}) fusion(f32[32,6,18,256]{3,0,2,1:T(8,128)} %pad_maximum_fusion.1), kind=kLoop, calls=%fused_computation.197 | loop fusion | bytes 55296 | tf_op jit(solution)/shard_map/slice | solution.py:81
  102.7 0.2 copy-done.3
  102.9 5.5 %maximum_maximum_fusion = (f32[32,6,18,257]{3,0,2,1:T(8,128)}, f32[32,6,18,257]{3,0,2,1:T(8,128)}) fusion(f32[32,6,1,256]{3,0,2,1:T(8,128)S(1)} %collective-permute-done.3, f32[32,6,16,256]{3,0,2,1:T(8,128)S(1)} %copy-done.3, f32[32,6,1,256]{3,0,2,1:T(8,128)S(1)} %collective-permute-done.2, f32[32,6,18,1]{3,0,2,1:T(8,128)S(1)} %get-tuple-element.9, ...), kind=kLoop, calls=%fused_computation.3 | loop fusion | flops 5329152 | bytes 10672128 | tf_op jit(solution)/shard_map/concatenate | solution.py:81
  108.4 2.3 %all-to-all-done.3 = f32[2,128,4,128]{3,2,0,1:T(4,128)S(1)} async-done(((f32[2,128,4,128]{3,2,0,1:T(4,128)}), f32[2,128,4,128]{3,2,0,1:T(4,128)S(1)}, u32[]{:S(2)}, u32[]{:S(2)}) %all-to-all-start.3) | async-done | bytes 524320 | tf_op jit(solution)/shard_map/all_to_all | solution.py:75
  110.7 0.3 copy.119
  111.0 1.8 %reshape.383 = f32[2,16,4,32,32]{4,3,2,1,0:T(8,128)} reshape(f32[2,16,4,8,128]{4,3,2,1,0:T(8,128)S(1)} %bitcast.183) | data formatting | bytes 1048576 | tf_op jit(solution)/shard_map/reshape | solution.py:78
  113.1 0.0 copy-start.41
  113.1 5.3 %fusion.64 = f32[16,4,32,256,1]{3,2,1,0,4:T(8,128)S(1)} fusion(f32[2,16,4,32,32]{4,3,2,1,0:T(8,128)} %reshape.383, f32[1,32,256]{2,1,0:T(8,128)} %get-tuple-element.57, f32[1,32,256]{2,1,0:T(8,128)} %get-tuple-element.58), kind=kOutput, calls=%fused_computation.107 | convolution fusion | flops 402669568 | bytes 2686976 | tf_op jit(solution)/shard_map/skz,syxkc->cxyz/dot_general | solution.py:79
  118.7 22.6 %fusion.8 = f32[32,4,16,256]{3,0,2,1:T(8,128)S(1)} fusion(f32[32,6,18,257]{3,0,2,1:T(8,128)} %get-tuple-element.8, f32[32,6,1,256]{3,0,2,1:T(8,128)S(1)} %collective-permute-done.3, f32[32,6,16,256]{3,0,2,1:T(8,128)S(1)} %copy-done.4, f32[32,6,18,257]{3,0,2,1:T(8,128)} %get-tuple-element.7, f32[32,1,16,256]{3,0,2,1:T(8,128)} %collective-permute-done.1, ...), kind=kOutput, calls=%fused_computation.23 | convolution fusion | flops 239075328 | bytes 50732544 | tf_op jit(solution)/shard_map/dot_general | solution.py:97
  141.3 2.5 %copy.69 = f32[32,4,16,256]{3,2,1,0:T(8,128)} copy(f32[32,4,16,256]{3,0,2,1:T(8,128)S(1)} %fusion.8) | data formatting | bytes 4194304 | tf_op jit(solution)/shard_map/mul | solution.py:101
  (84 shorter events, 0.3 us)
Async XLA Ops:
  0.0 118.4 %copy-start = (f32[32,32]{1,0:T(8,128)S(1)}, f32[32,32]{1,0:T(8,128)}, u32[]{:S(2)}) copy-start(f32[32,32]{1,0:T(8,128)} %param.8) | copy-start | bytes 12292
  8.5 10.7 %copy-start.1 = (f32[32,4,16,256]{3,2,1,0:T(8,128)S(1)}, f32[32,4,16,256]{3,2,1,0:T(8,128)}, u32[]{:S(2)}) copy-start(f32[32,4,16,256]{3,2,1,0:T(8,128)} %param.5) | copy-start | bytes 6291460
  11.8 19.7 %all-to-all-start = ((f32[8,1,16384]{2,1,0:T(1,128)}), f32[8,1,16384]{2,1,0:T(1,128)S(1)}, u32[]{:S(2)}, u32[]{:S(2)}) async-start(f32[8,1,16384]{2,1,0:T(1,128)} %reshape.404), calls=%async_computation | async-start | bytes 1048576 | tf_op jit(solution)/shard_map/all_to_all | solution.py:52
  19.3 3.6 %copy-start.5 = (f32[2,32,1,4,32,32]{5,4,3,2,1,0:T(8,128)S(1)}, f32[2,32,1,4,32,32]{5,4,3,2,1,0:T(8,128)}, u32[]{:S(2)}) copy-start(f32[2,32,1,4,32,32]{5,4,3,2,1,0:T(8,128)} %param.6) | copy-start | bytes 3145732
  20.5 2.7 %copy-start.6 = (f32[32,4,16,256]{3,0,2,1:T(8,128)}, f32[32,4,16,256]{3,0,2,1:T(8,128)S(1)}, u32[]{:S(2)}) copy-start(f32[32,4,16,256]{3,0,2,1:T(8,128)S(1)} %copy.47) | copy-start | bytes 6291460
  21.6 35.7 %collective-permute-start = (f32[32,1,16,256]{3,0,2,1:T(8,128)}, f32[32,1,16,256]{3,0,2,1:T(8,128)}, u32[]{:S(2)}, u32[]{:S(2)}) collective-permute-start(f32[32,1,16,256]{3,0,2,1:T(8,128)} %get-tuple-element.14), channel_id=1, source_target_pairs={{0,8},{8,16},{16,24},{24,32},{32,40},{40,48},{48,56},{56,64},{64,7... | collective-permute-start | bytes 1572872 | tf_op jit(solution)/shard_map/ppermute | solution.py:16
  22.7 36.9 %collective-permute-start.1 = (f32[32,1,16,256]{3,0,2,1:T(8,128)}, f32[32,1,16,256]{3,0,2,1:T(8,128)}, u32[]{:S(2)}, u32[]{:S(2)}) collective-permute-start(f32[32,1,16,256]{3,0,2,1:T(8,128)} %get-tuple-element.13), channel_id=1, source_target_pairs={{8,0},{16,8},{24,16},{32,24},{40,32},{48,40},{56,48},{64,56},{72,6... | collective-permute-start | bytes 1572872 | tf_op jit(solution)/shard_map/ppermute | solution.py:17
  23.2 1.2 copy-start.13
  30.7 7.1 %copy-start.7 = (f32[1,2,32,128]{3,2,1,0:T(8,128)}, f32[1,2,32,128]{3,2,1,0:T(8,128)S(1)}, u32[]{:S(2)}) copy-start(f32[1,2,32,128]{3,2,1,0:T(8,128)S(1)} %get-tuple-element.55) | copy-start | bytes 98308
  30.7 7.2 %copy-start.9 = (f32[1,2,32,128]{3,2,1,0:T(8,128)}, f32[1,2,32,128]{3,2,1,0:T(8,128)S(1)}, u32[]{:S(2)}) copy-start(f32[1,2,32,128]{3,2,1,0:T(8,128)S(1)} %get-tuple-element.56) | copy-start | bytes 98308
  42.8 24.8 %all-to-all-start.1 = ((f32[2,32,4,128]{3,2,0,1:T(4,128)}), f32[2,32,4,128]{3,2,0,1:T(4,128)S(1)}, u32[]{:S(2)}, u32[]{:S(2)}) async-start(f32[2,32,4,128]{3,2,0,1:T(4,128)} %reshape.401), calls=%async_computation.1 | async-start | bytes 262144 | tf_op jit(solution)/shard_map/all_to_all | solution.py:57
  59.6 8.1 %copy-start.8 = (f32[1,2,32,128]{3,2,1,0:T(8,128)S(1)}, f32[1,2,32,128]{3,2,1,0:T(8,128)}, u32[]{:S(2)}) copy-start(f32[1,2,32,128]{3,2,1,0:T(8,128)} %copy-done.7) | copy-start | bytes 98308
  59.6 8.1 %copy-start.10 = (f32[1,2,32,128]{3,2,1,0:T(8,128)S(1)}, f32[1,2,32,128]{3,2,1,0:T(8,128)}, u32[]{:S(2)}) copy-start(f32[1,2,32,128]{3,2,1,0:T(8,128)} %copy-done.9) | copy-start | bytes 98308
  60.7 1.7 %copy-start.2 = (f32[32,6,16,256]{3,0,2,1:T(8,128)}, f32[32,6,16,256]{3,0,2,1:T(8,128)S(1)}, u32[]{:S(2)}) copy-start(f32[32,6,16,256]{3,0,2,1:T(8,128)S(1)} %constant_dynamic-update-slice_fusion) | copy-start | bytes 9437188
  62.5 24.3 %collective-permute-start.2 = (f32[32,6,1,256]{3,0,2,1:T(8,128)S(1)}, f32[32,6,1,256]{3,0,2,1:T(8,128)S(1)}, u32[]{:S(2)}, u32[]{:S(2)}) collective-permute-start(f32[32,6,1,256]{3,0,2,1:T(8,128)S(1)} %get-tuple-element.11), channel_id=1, source_target_pairs={{0,1},{1,2},{2,3},{3,4},{4,5},{5,6},{6,7},{7,0},{8,9},{9,10},{10,1... | collective-permute-start | bytes 589832 | tf_op jit(solution)/shard_map/ppermute | solution.py:16
  63.6 23.2 %collective-permute-start.3 = (f32[32,6,1,256]{3,0,2,1:T(8,128)S(1)}, f32[32,6,1,256]{3,0,2,1:T(8,128)S(1)}, u32[]{:S(2)}, u32[]{:S(2)}) collective-permute-start(f32[32,6,1,256]{3,0,2,1:T(8,128)S(1)} %get-tuple-element.12), channel_id=1, source_target_pairs={{1,0},{2,1},{3,2},{4,3},{5,4},{6,5},{7,6},{0,7},{9,8},{10,9},{11,1... | collective-permute-start | bytes 589832 | tf_op jit(solution)/shard_map/ppermute | solution.py:17
  68.0 7.4 %copy-start.11 = (f32[1,2,32,128]{3,2,1,0:T(8,128)S(1)}, f32[1,2,32,128]{3,2,1,0:T(8,128)}, u32[]{:S(2)}) copy-start(f32[1,2,32,128]{3,2,1,0:T(8,128)} %get-tuple-element.42) | copy-start | bytes 98308
  68.1 7.4 %copy-start.12 = (f32[1,2,32,128]{3,2,1,0:T(8,128)S(1)}, f32[1,2,32,128]{3,2,1,0:T(8,128)}, u32[]{:S(2)}) copy-start(f32[1,2,32,128]{3,2,1,0:T(8,128)} %get-tuple-element.43) | copy-start | bytes 98308
  76.6 18.1 %all-to-all-start.2 = ((f32[2,1,128,128]{3,0,1,2:T(2,128)}), f32[2,1,128,128]{3,0,1,2:T(2,128)S(1)}, u32[]{:S(2)}, u32[]{:S(2)}) async-start(f32[2,1,128,128]{3,0,1,2:T(2,128)} %copy.55), calls=%async_computation.2 | async-start | bytes 262144 | tf_op jit(solution)/shard_map/all_to_all | solution.py:72
  96.5 14.2 %all-to-all-start.3 = ((f32[2,128,4,128]{3,2,0,1:T(4,128)}), f32[2,128,4,128]{3,2,0,1:T(4,128)S(1)}, u32[]{:S(2)}, u32[]{:S(2)}) async-start(f32[2,128,4,128]{3,2,0,1:T(4,128)} %copy.58), calls=%async_computation.3 | async-start | bytes 1048576 | tf_op jit(solution)/shard_map/all_to_all | solution.py:75
  100.0 3.0 %copy-start.3 = (f32[32,6,16,256]{3,0,2,1:T(8,128)S(1)}, f32[32,6,16,256]{3,0,2,1:T(8,128)}, u32[]{:S(2)}) copy-start(f32[32,6,16,256]{3,0,2,1:T(8,128)} %copy-done.2) | copy-start | bytes 9437188
  112.8 5.6 %copy-start.4 = (f32[32,6,16,256]{3,0,2,1:T(8,128)S(1)}, f32[32,6,16,256]{3,0,2,1:T(8,128)}, u32[]{:S(2)}) copy-start(f32[32,6,16,256]{3,0,2,1:T(8,128)} %copy-done.2) | copy-start | bytes 9437188
  112.8 5.6 %copy-start.14 = (f32[32]{0:T(128)S(1)}, f32[32]{0:T(128)}, u32[]{:S(2)}) copy-start(f32[32]{0:T(128)} %get-tuple-element.15) | copy-start | bytes 388
  112.8 5.6 %copy-start.15 = (f32[32]{0:T(128)S(1)}, f32[32]{0:T(128)}, u32[]{:S(2)}) copy-start(f32[32]{0:T(128)} %get-tuple-element.16) | copy-start | bytes 388
  112.8 5.6 %copy-start.16 = (f32[32]{0:T(128)S(1)}, f32[32]{0:T(128)}, u32[]{:S(2)}) copy-start(f32[32]{0:T(128)} %get-tuple-element.17) | copy-start | bytes 388
  112.8 5.6 %copy-start.17 = (f32[32]{0:T(128)S(1)}, f32[32]{0:T(128)}, u32[]{:S(2)}) copy-start(f32[32]{0:T(128)} %get-tuple-element.18) | copy-start | bytes 388
  112.8 5.6 %copy-start.18 = (f32[32]{0:T(128)S(1)}, f32[32]{0:T(128)}, u32[]{:S(2)}) copy-start(f32[32]{0:T(128)} %get-tuple-element.19) | copy-start | bytes 388
  112.8 5.6 %copy-start.19 = (f32[32]{0:T(128)S(1)}, f32[32]{0:T(128)}, u32[]{:S(2)}) copy-start(f32[32]{0:T(128)} %get-tuple-element.20) | copy-start | bytes 388
  112.8 5.6 %copy-start.20 = (f32[32]{0:T(128)S(1)}, f32[32]{0:T(128)}, u32[]{:S(2)}) copy-start(f32[32]{0:T(128)} %get-tuple-element.21) | copy-start | bytes 388
  112.9 5.6 %copy-start.21 = (f32[32]{0:T(128)S(1)}, f32[32]{0:T(128)}, u32[]{:S(2)}) copy-start(f32[32]{0:T(128)} %get-tuple-element.22) | copy-start | bytes 388
  112.9 5.6 %copy-start.22 = (f32[32]{0:T(128)S(1)}, f32[32]{0:T(128)}, u32[]{:S(2)}) copy-start(f32[32]{0:T(128)} %get-tuple-element.23) | copy-start | bytes 388
  112.9 5.6 %copy-start.23 = (f32[32]{0:T(128)S(1)}, f32[32]{0:T(128)}, u32[]{:S(2)}) copy-start(f32[32]{0:T(128)} %get-tuple-element.24) | copy-start | bytes 388
  112.9 5.6 %copy-start.24 = (f32[32]{0:T(128)S(1)}, f32[32]{0:T(128)}, u32[]{:S(2)}) copy-start(f32[32]{0:T(128)} %get-tuple-element.25) | copy-start | bytes 388
  112.9 5.6 %copy-start.25 = (f32[32]{0:T(128)S(1)}, f32[32]{0:T(128)}, u32[]{:S(2)}) copy-start(f32[32]{0:T(128)} %get-tuple-element.26) | copy-start | bytes 388
  112.9 5.6 %copy-start.26 = (f32[32]{0:T(128)S(1)}, f32[32]{0:T(128)}, u32[]{:S(2)}) copy-start(f32[32]{0:T(128)} %get-tuple-element.27) | copy-start | bytes 388
  112.9 5.6 %copy-start.27 = (f32[32]{0:T(128)S(1)}, f32[32]{0:T(128)}, u32[]{:S(2)}) copy-start(f32[32]{0:T(128)} %get-tuple-element.28) | copy-start | bytes 388
  112.9 5.6 %copy-start.28 = (f32[32]{0:T(128)S(1)}, f32[32]{0:T(128)}, u32[]{:S(2)}) copy-start(f32[32]{0:T(128)} %get-tuple-element.29) | copy-start | bytes 388
  112.9 5.6 %copy-start.29 = (f32[32]{0:T(128)S(1)}, f32[32]{0:T(128)}, u32[]{:S(2)}) copy-start(f32[32]{0:T(128)} %get-tuple-element.30) | copy-start | bytes 388
  112.9 5.6 %copy-start.30 = (f32[32]{0:T(128)S(1)}, f32[32]{0:T(128)}, u32[]{:S(2)}) copy-start(f32[32]{0:T(128)} %get-tuple-element.31) | copy-start | bytes 388
  113.0 5.6 %copy-start.31 = (f32[32]{0:T(128)S(1)}, f32[32]{0:T(128)}, u32[]{:S(2)}) copy-start(f32[32]{0:T(128)} %get-tuple-element.32) | copy-start | bytes 388
  113.0 5.6 %copy-start.32 = (f32[32]{0:T(128)S(1)}, f32[32]{0:T(128)}, u32[]{:S(2)}) copy-start(f32[32]{0:T(128)} %get-tuple-element.33) | copy-start | bytes 388
  113.0 5.6 %copy-start.33 = (f32[32]{0:T(128)S(1)}, f32[32]{0:T(128)}, u32[]{:S(2)}) copy-start(f32[32]{0:T(128)} %get-tuple-element.34) | copy-start | bytes 388
  113.0 5.6 %copy-start.34 = (f32[32]{0:T(128)S(1)}, f32[32]{0:T(128)}, u32[]{:S(2)}) copy-start(f32[32]{0:T(128)} %get-tuple-element.35) | copy-start | bytes 388
  113.0 5.6 %copy-start.35 = (f32[32]{0:T(128)S(1)}, f32[32]{0:T(128)}, u32[]{:S(2)}) copy-start(f32[32]{0:T(128)} %get-tuple-element.36) | copy-start | bytes 388
  113.0 5.6 %copy-start.36 = (f32[32]{0:T(128)S(1)}, f32[32]{0:T(128)}, u32[]{:S(2)}) copy-start(f32[32]{0:T(128)} %get-tuple-element.37) | copy-start | bytes 388
  113.0 5.6 %copy-start.37 = (f32[32]{0:T(128)S(1)}, f32[32]{0:T(128)}, u32[]{:S(2)}) copy-start(f32[32]{0:T(128)} %get-tuple-element.38) | copy-start | bytes 388
  113.0 5.6 %copy-start.38 = (f32[32]{0:T(128)S(1)}, f32[32]{0:T(128)}, u32[]{:S(2)}) copy-start(f32[32]{0:T(128)} %get-tuple-element.39) | copy-start | bytes 388
  113.0 5.6 %copy-start.39 = (f32[32]{0:T(128)S(1)}, f32[32]{0:T(128)}, u32[]{:S(2)}) copy-start(f32[32]{0:T(128)} %get-tuple-element.40) | copy-start | bytes 388
  113.0 5.6 %copy-start.40 = (f32[32]{0:T(128)S(1)}, f32[32]{0:T(128)}, u32[]{:S(2)}) copy-start(f32[32]{0:T(128)} %get-tuple-element.41) | copy-start | bytes 388
  113.1 5.6 %copy-start.41 = (f32[32]{0:T(128)S(1)}, f32[32]{0:T(128)}, u32[]{:S(2)}) copy-start(f32[32]{0:T(128)} %param.9) | copy-start | bytes 388
where the time goes:
time: 144 us
  matrix products  44 us (31%)
  starting transfers between devices  40.6 us (28%)
  local copies, waits for them, and re-layouts  33 us (23%)
  other arithmetic  19.4 us (13%)
  waiting for transfers between devices  6 us (4%)
    dot_general x1, matrix products, on_device(): jnp.dot(point_weight.T, field.reshape(chans, -1), precision=exact_mode)  22.6 us
    all_to_all x1, starting transfers between devices, on_device(): lax.all_to_all(yspec, 'gx', split_axis=1, concat_axis=2, tiled=True)  14.5 us
    unnamed x89, local copies, waits for them, and re-layouts  10.9 us
    all_to_all x1, starting transfers between devices, on_device(): lax.all_to_all(back_x, 'gx', split_axis=2, concat_axis=1, tiled=True)  8.83 us
    all_to_all x1, starting transfers between devices, on_device(): wide = lax.all_to_all(zspec, 'gy', split_axis=1, concat_axis=4, tiled=True)  7.48 us
    dot_general x1, matrix products, on_device(): jnp.einsum('rnmki,srmnkio->snmko', xin, stacked, precision=exact_mode)  7.24 us
    concatenate x1, other arithmetic, on_device(): jnp.concatenate([framed[..., -1:], framed, framed[..., :1]], axis=3)  5.5 us
    dot_general x1, matrix products, on_device(): jnp.einsum('skz,syxkc->cxyz', backward_z, zcells, precision=exact_mode)  5.29 us
  transfers between devices with their start and end apart: 8, of which 2 were waited for; matrix products, arithmetic and copies ran while one was open for 34% of the time, Pallas kernels for 0%

commit v1 on v0

v1 whole, which is shorter than its diff:
```python
import functools

import jax
import jax.numpy as jnp
import numpy as np
from jax import lax
from jax.experimental import pallas as pl
from jax.experimental.pallas import tpu as pltpu
from jax.sharding import PartitionSpec as P

F32 = jnp.float32
BF16 = jnp.bfloat16


def halves(table):
    high = np.asarray(table, np.float32).astype(BF16)
    low = (np.asarray(table, np.float64) - high.astype(np.float64)).astype(BF16)
    return high, low


def kept(modes, length):
    index = np.arange(modes)
    return np.where(index < modes // 2, index, index + length - modes)


def angles(freqs, length):
    product = np.outer(freqs, np.arange(length)) % length
    turn = 2.0 * np.pi * product / length
    return np.cos(turn), np.sin(turn)


def tables(modes, full_x, full_y, depth):
    zc, zs = angles(np.arange(modes), depth)
    fz = np.stack([zc, -zs], axis=1).reshape(2 * modes, depth)
    weight = np.where(np.arange(modes) == 0, 1.0, 2.0)[:, None] / depth
    iz = np.stack([weight * zc, -weight * zs], axis=1).reshape(2 * modes, depth)
    yc, ys = angles(kept(modes, full_y), full_y)
    fy = np.block([[yc, ys], [-ys, yc]])
    iy = np.block([[yc.T, -ys.T], [ys.T, yc.T]]) / full_y
    xc, xs = angles(kept(modes, full_x), full_x)
    fx = np.concatenate(
        [np.stack([xc, xs], axis=2), np.stack([-xs, xc], axis=2)], axis=0
    ).reshape(2 * modes, 2 * full_x)
    ix = np.stack(
        [np.concatenate([xc.T, -xs.T], axis=1), np.concatenate([xs.T, xc.T], axis=1)]
    ) / full_x
    ix = ix.reshape(2, full_x // 4, 4, 2 * modes).transpose(2, 0, 1, 3)
    ix = ix.reshape(2 * full_x, 2 * modes)
    return {"fz": fz, "iz": iz, "fy": fy, "iy": iy, "fx": fx, "ix": ix}


def split(value):
    high = value.astype(BF16)
    return high, (value - high.astype(F32)).astype(BF16)


def mm(a, b):
    return jnp.dot(a, b, preferred_element_type=F32)


def mm_nt(a, b):
    return lax.dot_general(a, b, (((1,), (1,)), ((), ())), preferred_element_type=F32)


def mm_tn(a, b):
    return lax.dot_general(a, b, (((0,), (0,)), ((), ())), preferred_element_type=F32)


def table_dot(high_ref, low_ref, data):
    high, low = split(data)
    return mm(high_ref[...], high) + mm(high_ref[...], low) + mm(low_ref[...], high)


def forward_z(left_ref, right_ref, th_ref, tl_ref, out_ref, first_ref, middle_ref, last_ref):
    sides = [left_ref.reshape(1024, 128), right_ref.reshape(1024, 128)]
    both = jnp.concatenate([th_ref[...], tl_ref[...]], axis=0)
    for y in range(8):
        parts = [
            jnp.concatenate([side[pl.ds(x * 8 + y, 32, stride=32), :] for side in sides], axis=1)
            for x in range(4)
        ]
        first_ref[y] = parts[0]
        middle_ref[0, y] = parts[1]
        middle_ref[1, y] = parts[2]
        last_ref[y] = parts[3]
        high, low = split(jnp.concatenate(parts, axis=0))
        wide = mm_nt(both, high)
        total = wide[:64] + wide[64:] + mm_nt(th_ref[...], low)
        out_ref[:, y] = total.reshape(8, 8, 128)


def forward_y(data_ref, th_ref, tl_ref, out_ref):
    rows = data_ref.reshape(1024, 128)
    results = []
    for k in range(4):
        parts = [rows[pl.ds(2 * k + part, 128, stride=8), :] for part in range(2)]
        results.append(table_dot(th_ref, tl_ref, jnp.concatenate(parts, axis=0)))
    out = out_ref.reshape(256, 128)
    for x in range(4):
        tile = jnp.concatenate([r[:, 32 * x : 32 * x + 32] for r in results], axis=1)
        for part in range(2):
            out[pl.ds(2 * x + part, 32, stride=8), :] = tile[32 * part : 32 * part + 32]


def middle(data_ref, weight_ref, fh_ref, fl_ref, ih_ref, il_ref, out_ref):
    spec = table_dot(fh_ref, fl_ref, data_ref[...].reshape(256, 128))
    spec_re, spec_im = spec[:32], spec[32:]
    lane = lax.broadcasted_iota(jnp.int32, (32, 128), 1)
    group = lane - lax.rem(lane, 32)
    mixed_re = jnp.zeros((32, 128), F32)
    mixed_im = jnp.zeros((32, 128), F32)
    for c in range(32):
        index = group + c
        in_re = jnp.take_along_axis(spec_re, index, axis=1)
        in_im = jnp.take_along_axis(spec_im, index, axis=1)
        w_re, w_im = weight_ref[0, c], weight_ref[1, c]
        mixed_re = mixed_re + (in_re * w_re - in_im * w_im)
        mixed_im = mixed_im + (in_re * w_im + in_im * w_re)
    back = table_dot(ih_ref, il_ref, jnp.concatenate([mixed_re, mixed_im], axis=0))
    out = out_ref.reshape(256, 128)
    for k in range(4):
        tile = jnp.concatenate(
            [back[64 * x : 64 * x + 64, 32 * k : 32 * k + 32] for x in range(4)], axis=1
        )
        for part in range(2):
            out[pl.ds(2 * k + part, 32, stride=8), :] = tile[32 * part : 32 * part + 32]


def inverse_y(data_ref, th_ref, tl_ref, out_ref):
    rows = data_ref.reshape(256, 128)
    out = out_ref.reshape(1024, 128)
    for k in range(4):
        parts = [rows[pl.ds(2 * k + part, 32, stride=8), :] for part in range(2)]
        result = table_dot(th_ref, tl_ref, jnp.concatenate(parts, axis=0))
        for part in range(2):
            out[pl.ds(2 * k + part, 128, stride=8), :] = result[128 * part : 128 * part + 128]


def final(data_ref, base_ref, th_ref, tl_ref, out_ref):
    rows = out_ref.reshape(1024, 128)
    table = jnp.concatenate([th_ref[...], th_ref[...], tl_ref[...]], axis=0)
    for y in range(8):
        high, low = split(data_ref[:, y].reshape(64, 128))
        stacked = jnp.concatenate([high, low, high], axis=0)
        spectral = mm_tn(stacked, table)
        for x in range(4):
            value = spectral[32 * x : 32 * x + 32] + base_ref[x, y]
            rows[pl.ds(x * 8 + y, 32, stride=32), :] = jax.nn.gelu(value)


def weights(data_ref, out_ref):
    def body(c, carry):
        for part in range(2):
            for k in range(4):
                start = (part * 128 + k) * 32 + c
                block = data_ref[pl.ds(start, 32, stride=128), :]
                out_ref[part, c, :, 32 * k : 32 * k + 32] = block
        return carry

    lax.fori_loop(0, 32, body, 0)


def local(
    first_ref, middle_ref, last_ref, before_ref, after_ref, left_ref, right_ref,
    tap_ref, ph_ref, pl_ref, bias_ref, out_ref, frame, sems
):
    moves = [
        (before_ref, frame.at[0, pl.ds(1, 16)]),
        (first_ref, frame.at[1, pl.ds(1, 16)]),
        (middle_ref, frame.at[pl.ds(2, 2), pl.ds(1, 16)]),
        (last_ref, frame.at[4, pl.ds(1, 16)]),
        (after_ref, frame.at[5, pl.ds(1, 16)]),
        (left_ref, frame.at[:, 0]),
        (right_ref, frame.at[:, 17]),
    ]
    copies = [
        pltpu.make_async_copy(src, dst, sems.at[i]) for i, (src, dst) in enumerate(moves)
    ]
    for copy in copies:
        copy.start()
    for copy in copies:
        copy.wait()
    point = jnp.concatenate([ph_ref[...], pl_ref[...], ph_ref[...]], axis=1)
    bias = jnp.concatenate([bias_ref[...]] * 4, axis=0)

    def pointwise(y, carry):
        data = frame[1:5, y + 1].reshape(128, 256)
        high, low = split(data)
        value = mm(point, jnp.concatenate([high, high, low], axis=0)) + bias
        out_ref[:, y] = value.reshape(4, 32, 256)
        return carry

    lax.fori_loop(0, 16, pointwise, 0)
    lane = lax.broadcasted_iota(jnp.int32, (8, 256), 1)
    for tile in range(4):
        chans = pl.ds(8 * tile, 8)
        taps = tap_ref[chans, :]
        taps = [
            jnp.broadcast_to(taps[:, i : i + 1], (8, 256)) for i in range(27)
        ]

        def row(y, carry):
            for x in range(4):
                sums = [None, None, None]
                for a in range(3):
                    for b in range(3):
                        cell = frame[x + a, y + b, chans, :]
                        for e in range(3):
                            term = taps[9 * a + 3 * b + e] * cell
                            sums[e] = term if sums[e] is None else sums[e] + term
                total = sums[1] + pltpu.roll(sums[0], 1, 1) + pltpu.roll(sums[2], 255, 1)
                out_ref[x, y, chans, :] = out_ref[x, y, chans, :] + total
            return carry

        lax.fori_loop(0, 16, row, 0)


VMEM = pl.BlockSpec(memory_space=pltpu.VMEM)
ANY = pl.BlockSpec(memory_space=pl.ANY)


def call(body, shapes, count, **kw):
    single = not isinstance(shapes, list)
    out_shape = [jax.ShapeDtypeStruct(s, F32) for s in ([shapes] if single else shapes)]
    kw.setdefault("in_specs", [VMEM] * count)
    kw.setdefault("out_specs", [VMEM] * len(out_shape))
    if single:
        out_shape = out_shape[0]
        if isinstance(kw["out_specs"], list):
            kw["out_specs"] = kw["out_specs"][0]
    return pl.pallas_call(body, out_shape=out_shape, name=body.__name__, **kw)


def shifted(axis, value, step):
    count = lax.axis_size(axis)
    return lax.ppermute(value, axis, [(i, (i + step) % count) for i in range(count)])


def exchange(value, axis):
    return lax.all_to_all(value, axis, split_axis=0, concat_axis=0, tiled=True)


def on_device(field, spec_weight, dw_kernel, point_weight, bias):
    tab = {
        name: tuple(jnp.asarray(half) for half in halves(value))
        for name, value in tables(32, 128, 128, 256).items()
    }
    whole = lambda *shape: pl.BlockSpec(shape, lambda i: (0,) * len(shape))
    zchunks, first, mid, last = call(
        forward_z,
        [(8, 16, 8, 128), (16, 32, 256), (2, 16, 32, 256), (16, 32, 256)],
        4,
        grid=(2,),
        in_specs=[
            pl.BlockSpec((128, 8, 128), lambda i: (0, i, 0)),
            pl.BlockSpec((128, 8, 128), lambda i: (0, i, 1)),
            whole(64, 256),
            whole(64, 256),
        ],
        out_specs=[
            pl.BlockSpec((8, 8, 8, 128), lambda i: (0, i, 0, 0)),
            pl.BlockSpec((8, 32, 256), lambda i: (i, 0, 0)),
            pl.BlockSpec((2, 8, 32, 256), lambda i: (0, i, 0, 0)),
            pl.BlockSpec((8, 32, 256), lambda i: (i, 0, 0)),
        ],
    )(field.reshape(128, 16, 256), field.reshape(128, 16, 256), *tab["fz"])
    zall = exchange(zchunks, "gy")
    before = shifted("gx", last, 1)
    after = shifted("gx", first, -1)
    packed = call(weights, (2, 32, 32, 128), 1)(spec_weight.reshape(8192, 32))
    ychunks = call(forward_y, (32, 8, 128), 3)(zall, *tab["fy"])
    yall = exchange(ychunks, "gx")
    rows = [before[None], first[None], mid, last[None], after[None]]
    top = jnp.concatenate([r[:, 15] for r in rows], axis=0)
    bottom = jnp.concatenate([r[:, 0] for r in rows], axis=0)
    left = shifted("gy", top, 1)
    right = shifted("gy", bottom, -1)
    xchunks = call(middle, (32, 8, 128), 6)(yall, packed, *tab["fx"], *tab["ix"])
    xall = exchange(xchunks, "gx")
    blocks = jnp.kron(jnp.eye(4, dtype=F32), point_weight.T)
    point_high = blocks.astype(BF16)
    point_low = (blocks - lax.reduce_precision(blocks, 8, 7)).astype(BF16)
    base = call(
        local,
        (4, 16, 32, 256),
        11,
        in_specs=[ANY] * 7 + [VMEM] * 4,
        scratch_shapes=[pltpu.VMEM((6, 18, 32, 256), F32), pltpu.SemaphoreType.DMA((7,))],
    )(
        first, mid, last, before, after, left, right,
        dw_kernel.reshape(32, 27), point_high, point_low, bias.reshape(32, 1),
    )
    back = call(inverse_y, (8, 16, 8, 128), 3)(xall, *tab["iy"])
    ball = exchange(back, "gy")
    out = call(
        final,
        (128, 16, 256),
        4,
        grid=(2, 2),
        in_specs=[
            pl.BlockSpec((8, 8, 8, 128), lambda i, j: (0, i, 0, 0)),
            pl.BlockSpec((4, 8, 32, 128), lambda i, j: (0, i, 0, j)),
            pl.BlockSpec((64, 128), lambda i, j: (0, j)),
            pl.BlockSpec((64, 128), lambda i, j: (0, j)),
        ],
        out_specs=pl.BlockSpec((128, 8, 128), lambda i, j: (0, i, j)),
    )(ball, base, *tab["iz"])
    return out.reshape(field.shape)


def solution(mesh):
    placed = (P(None, "gx", "gy", None), P(None, None, "gx", "gy", None, None), P(), P(), P())
    return jax.shard_map(
        on_device, mesh=mesh, in_specs=placed, out_specs=P(None, "gx", "gy", None), check_vma=False
    )
```

time: 144 us -> 123 us (0.85)
  matrix products: 44 us -> 0 us
  Pallas kernels: 0 us -> 40.4 us
  local copies, waits for them, and re-layouts: 33 us -> 7.67 us
  waiting for transfers between devices: 6 us -> 29.9 us
  other arithmetic: 19.4 us -> 0.75 us
  starting transfers between devices: 40.6 us -> 43.2 us
    dot_general x8 -> x0, matrix products: 44 us -> none  [the longest x1 22.6 us: on_device(): jnp.dot(point_weight.T, field.reshape(chans, -1), precision=exact_mode)]
    pallas_call x0 -> x7, Pallas kernels: none -> 40.4 us  [the longest x1 15.1 us: on_device(): call(local, (4, 16, 32, 256), 11, in_specs=[ANY] * 7 + [VMEM] * 4, scratc...]
    ppermute x4, waiting for transfers between devices: 0.01 us -> 12.9 us  [shifted(): lax.ppermute(value, axis, [(i, (i + step) % count) for i in range(count)])]
    all_to_all x4, waiting for transfers between devices: 5.99 us -> 17 us  [exchange(): return lax.all_to_all(value, axis, split_axis=0, concat_axis=0, tiled=True)]
    concatenate x2 -> x0, other arithmetic: 9.62 us -> none  [the longest x1 5.5 us: on_device(): jnp.concatenate([framed[..., -1:], framed, framed[..., :1]], axis=3)]
    reshape x5 -> x3, local copies, waits for them, and re-layouts: 7.4 us -> 1.37 us  [the longest x2 0.69 us: on_device(): dw_kernel.reshape(32, 27)]
    another operation x3 -> x0, other arithmetic: 5.65 us -> none  [the longest x2 5.01 us: on_device(): jnp.stack([jnp.stack([weight_re, -weight_im]), jnp.stack([weight_im, weig...]
    unnamed x89 -> x26, local copies, waits for them, and re-layouts: 10.9 us -> 6.06 us
  transfers between devices with their start and end apart: 8 -> 8, of which waited for: 2 -> 4; matrix products, arithmetic and copies ran while one was open for 34% -> 4% of each run, Pallas kernels for 0% -> 25%
where the time goes in v1:
time: 123 us; the launch traced here: 122 us
  starting transfers between devices  43.2 us (35%)
  Pallas kernels  40.4 us (33%)
  waiting for transfers between devices  29.9 us (24%)
  local copies, waits for them, and re-layouts  7.67 us (6%)
    all_to_all x4, starting transfers between devices, exchange(): return lax.all_to_all(value, axis, split_axis=0, concat_axis=0, tiled=True)  37 us
    all_to_all x4, waiting for transfers between devices, exchange(): return lax.all_to_all(value, axis, split_axis=0, concat_axis=0, tiled=True)  17 us
    pallas_call x1, Pallas kernels, on_device(): call(local, (4, 16, 32, 256), 11, in_specs=[ANY] * 7 + [VMEM] * 4, scratc...  15.1 us
    ppermute x4, waiting for transfers between devices, shifted(): lax.ppermute(value, axis, [(i, (i + step) % count) for i in range(count)])  12.9 us
    pallas_call x1, Pallas kernels, on_device(): packed = call(weights, (2, 32, 32, 128), 1)(spec_weight.reshape(8192, 32))  8.7 us
    ppermute x4, starting transfers between devices, shifted(): lax.ppermute(value, axis, [(i, (i + step) % count) for i in range(count)])  6.25 us
    unnamed x26, local copies, waits for them, and re-layouts  6.06 us
    pallas_call x1, Pallas kernels, on_device(): call(final, (128, 16, 256), 4, grid=(2, 2), in_specs=[pl.BlockSpec((8, 8,...  5.27 us
  transfers between devices with their start and end apart: 8, of which 4 were waited for; matrix products, arithmetic and copies ran while one was open for 4% of the time, Pallas kernels for 25%

profile of v1, /device:TPU:1, one launch (start us, length us, event | category | flops | bytes accessed | tf_op | source)
XLA Modules:
  0.0 122.1 jit_solution(7118077599916083989)
XLA Ops:
  0.0 0.0 copy-start.9
  0.0 4.1 %forward_z.1 = (f32[8,16,8,128]{3,2,1,0:T(8,128)}, f32[16,32,256]{2,1,0:T(8,128)}, f32[2,16,32,256]{3,2,1,0:T(8,128)}, f32[16,32,256]{2,1,0:T(8,128)}) custom-call(f32[128,16,256]{2,1,0:T(8,128)} %bitcast.51, f32[128,16,256]{2,1,0:T(8,128)} %bitcast.52, bf16[64,256]{1,0:T(8,128)(2,1)} %constant.24.clone.th_ref, bf16[64,256]{1,0:T(8,128)(2,1)} %constant.25.clone.tl_ref), custom_call_target="tpu_custom_call" | custom-call | tf_op jit(solution)/shard_map/forward_z/pallas_call | solution.py:249
  4.1 0.0 copy-start.8
  4.1 0.0 copy-start.10
  4.1 7.6 %all-to-all-start = ((f32[8,16,8,128]{3,2,1,0:T(8,128)}), f32[8,16,8,128]{3,2,1,0:T(8,128)S(1)}, u32[]{:S(2)}, u32[]{:S(2)}) async-start(f32[8,16,8,128]{3,2,1,0:T(8,128)} %get-tuple-element.9), calls=%async_computation | async-start | bytes 1048576 | tf_op jit(solution)/shard_map/all_to_all | solution.py:240
  11.8 1.2 collective-permute-start
  12.9 0.0 collective-permute-start.1
  12.9 0.0 copy-done.9
  12.9 0.1 copy.25
  13.0 9.4 %all-to-all-done.data_ref = f32[8,16,8,128]{3,2,1,0:T(8,128)S(1)} async-done(((f32[8,16,8,128]{3,2,1,0:T(8,128)}), f32[8,16,8,128]{3,2,1,0:T(8,128)S(1)}, u32[]{:S(2)}, u32[]{:S(2)}) %all-to-all-start) | async-done | bytes 524320 | tf_op jit(solution)/shard_map/all_to_all | solution.py:240
  22.4 0.0 copy-start.1
  22.4 0.8 copy-done.1
  23.2 2.1 %forward_y.1 = f32[32,8,128]{2,1,0:T(8,128)} custom-call(f32[8,16,8,128]{3,2,1,0:T(8,128)} %copy-done.1, bf16[64,256]{1,0:T(8,128)(2,1)} %constant.28.clone.th_ref, bf16[64,256]{1,0:T(8,128)(2,1)} %constant.29.clone.tl_ref), custom_call_target="tpu_custom_call" | custom-call | tf_op jit(solution)/shard_map/forward_y/pallas_call | solution.py:271
  25.3 17.6 %all-to-all-start.1 = ((f32[32,8,128]{2,1,0:T(8,128)}), f32[32,8,128]{2,1,0:T(8,128)S(1)}, u32[]{:S(2)}, u32[]{:S(2)}) async-start(f32[32,8,128]{2,1,0:T(8,128)} %forward_y.1), calls=%async_computation.1 | async-start | bytes 262144 | tf_op jit(solution)/shard_map/all_to_all | solution.py:240
  42.9 0.1 broadcast_multiply_fusion
  43.0 0.0 copy-done.8
  43.0 0.7 copy.26.tap_ref
  43.7 0.0 copy-done.10
  43.7 0.7 copy.27.bias_ref
  44.4 0.2 mul.27
  44.5 8.7 %weights.1.weight_ref = f32[2,32,32,128]{3,2,1,0:T(8,128)} custom-call(f32[8192,32]{1,0:T(8,128)} %bitcast.53), custom_call_target="tpu_custom_call" | custom-call | tf_op jit(solution)/shard_map/weights/pallas_call | solution.py:270
  53.2 0.0 collective-permute-done.before_ref
  53.2 0.0 copy-start.2
  53.3 0.0 all-to-all-done.1.data_ref
  53.3 0.0 copy-start.4
  53.3 0.7 copy-done.4
  53.9 3.1 %middle.1 = f32[32,8,128]{2,1,0:T(8,128)} custom-call(f32[32,8,128]{2,1,0:T(8,128)} %copy-done.4, f32[2,32,32,128]{3,2,1,0:T(8,128)} %weights.1.weight_ref, bf16[64,256]{1,0:T(8,128)(2,1)} %constant.32.clone.fh_ref, bf16[64,256]{1,0:T(8,128)(2,1)} %constant.33.clone.fl_ref, bf16[256,64]{1,0:T(8,128)(2,1)} %constant.34.clone.ih_ref, ...), custom_call_target="tpu_custom_call" | custom-call | tf_op jit(solution)/shard_map/middle/pallas_call | solution.py:278
  57.0 8.3 %all-to-all-start.2 = ((f32[32,8,128]{2,1,0:T(8,128)}), f32[32,8,128]{2,1,0:T(8,128)S(1)}, u32[]{:S(2)}, u32[]{:S(2)}) async-start(f32[32,8,128]{2,1,0:T(8,128)} %middle.1), calls=%async_computation.2 | async-start | bytes 262144 | tf_op jit(solution)/shard_map/all_to_all | solution.py:240
  65.3 0.8 fusion.5
  66.1 0.9 fusion.1
  67.0 7.6 %all-to-all-done.2.data_ref = f32[32,8,128]{2,1,0:T(8,128)S(1)} async-done(((f32[32,8,128]{2,1,0:T(8,128)}), f32[32,8,128]{2,1,0:T(8,128)S(1)}, u32[]{:S(2)}, u32[]{:S(2)}) %all-to-all-start.2) | async-done | bytes 131104 | tf_op jit(solution)/shard_map/all_to_all | solution.py:240
  74.5 0.0 copy-start.5
  74.5 0.6 copy-done.5
  75.2 2.1 %inverse_y.1 = f32[8,16,8,128]{3,2,1,0:T(8,128)} custom-call(f32[32,8,128]{2,1,0:T(8,128)} %copy-done.5, bf16[256,64]{1,0:T(8,128)(2,1)} %constant.30.clone.th_ref, bf16[256,64]{1,0:T(8,128)(2,1)} %constant.31.clone.tl_ref), custom_call_target="tpu_custom_call" | custom-call | tf_op jit(solution)/shard_map/inverse_y/pallas_call | solution.py:293
  77.3 3.5 %all-to-all-start.3 = ((f32[8,16,8,128]{3,2,1,0:T(8,128)}), f32[8,16,8,128]{3,2,1,0:T(8,128)S(1)}, u32[]{:S(2)}, u32[]{:S(2)}) async-start(f32[8,16,8,128]{3,2,1,0:T(8,128)} %inverse_y.1), calls=%async_computation.3 | async-start | bytes 1048576 | tf_op jit(solution)/shard_map/all_to_all | solution.py:240
  80.8 0.8 fusion.4
  81.6 0.0 copy-done.2
  81.6 0.0 collective-permute-done.1.after_ref
  81.6 0.0 copy-start.3
  81.6 5.1 %collective-permute-start.3 = (f32[6,32,256]{2,1,0:T(8,128)S(1)}, f32[6,32,256]{2,1,0:T(8,128)S(1)}, u32[]{:S(2)}, u32[]{:S(2)}) collective-permute-start(f32[6,32,256]{2,1,0:T(8,128)S(1)} %get-tuple-element.15), channel_id=1, source_target_pairs={{0,7},{1,0},{2,1},{3,2},{4,3},{5,4},{6,5},{7,6},{8,15},{9,8},{10,9... | collective-permute-start | bytes 589832 | tf_op jit(solution)/shard_map/ppermute | solution.py:236
  86.7 0.0 collective-permute-start.2
  86.7 0.6 fusion
  87.3 6.5 %collective-permute-done.3.right_ref = f32[6,32,256]{2,1,0:T(8,128)S(1)} collective-permute-done((f32[6,32,256]{2,1,0:T(8,128)S(1)}, f32[6,32,256]{2,1,0:T(8,128)S(1)}, u32[]{:S(2)}, u32[]{:S(2)}) %collective-permute-start.3) | collective-permute-done | bytes 196640 | tf_op jit(solution)/shard_map/ppermute | solution.py:236
  93.9 0.0 copy-start.6
  93.9 6.4 %collective-permute-done.2.left_ref = f32[6,32,256]{2,1,0:T(8,128)S(1)} collective-permute-done((f32[6,32,256]{2,1,0:T(8,128)S(1)}, f32[6,32,256]{2,1,0:T(8,128)S(1)}, u32[]{:S(2)}, u32[]{:S(2)}) %collective-permute-start.2) | collective-permute-done | bytes 196640 | tf_op jit(solution)/shard_map/ppermute | solution.py:236
  100.2 0.0 copy-start.7
  100.2 0.0 copy-done.3
  100.2 0.0 copy-done.6
  100.2 0.7 copy-done.7
  100.9 15.1 %local.1.base_ref = f32[4,16,32,256]{3,2,1,0:T(8,128)} custom-call(f32[16,32,256]{2,1,0:T(8,128)} %get-tuple-element.10.first_ref, f32[2,16,32,256]{3,2,1,0:T(8,128)} %get-tuple-element.11.middle_ref, f32[16,32,256]{2,1,0:T(8,128)} %get-tuple-element.12.last_ref, f32[16,32,256]{2,1,0:T(8,128)} %copy-done.2, f32[16,32,256]{2,1,0:T(8,128)} %copy-done.3, ...), custom_call_target="tpu_custom_call" | custom-call | tf_op jit(solution)/shard_map/local/pallas_call | solution.py:283
  116.0 0.0 all-to-all-done.3.data_ref
  116.0 0.0 copy-start
  116.0 0.8 copy-done
  116.8 5.3 %final.1 = f32[128,16,256]{2,1,0:T(8,128)} custom-call(f32[8,16,8,128]{3,2,1,0:T(8,128)} %copy-done, f32[4,16,32,256]{3,2,1,0:T(8,128)} %local.1.base_ref, bf16[64,256]{1,0:T(8,128)(2,1)} %constant.26.clone.th_ref, bf16[64,256]{1,0:T(8,128)(2,1)} %constant.27.clone.tl_ref), custom_call_target="tpu_custom_call" | custom-call | tf_op jit(solution)/shard_map/final/pallas_call | solution.py:295
  (4 shorter events, 0.0 us)
Async XLA Ops:
  0.0 12.9 %copy-start.9 = (f32[32,32]{1,0:T(8,128)S(1)}, f32[32,32]{1,0:T(8,128)}, u32[]{:S(2)}) copy-start(f32[32,32]{1,0:T(8,128)} %param.20) | copy-start | bytes 12292
  4.1 38.9 %copy-start.8 = (f32[32,3,3,3]{0,3,2,1:T(4,128)S(1)}, f32[32,3,3,3]{0,3,2,1:T(4,128)}, u32[]{:S(2)}) copy-start(f32[32,3,3,3]{0,3,2,1:T(4,128)} %param.19) | copy-start | bytes 10372
  4.1 39.6 %copy-start.10 = (f32[32]{0:T(128)S(1)}, f32[32]{0:T(128)}, u32[]{:S(2)}) copy-start(f32[32]{0:T(128)} %param.21) | copy-start | bytes 388
  4.1 18.3 %all-to-all-start = ((f32[8,16,8,128]{3,2,1,0:T(8,128)}), f32[8,16,8,128]{3,2,1,0:T(8,128)S(1)}, u32[]{:S(2)}, u32[]{:S(2)}) async-start(f32[8,16,8,128]{3,2,1,0:T(8,128)} %get-tuple-element.9), calls=%async_computation | async-start | bytes 1048576 | tf_op jit(solution)/shard_map/all_to_all | solution.py:240
  11.8 41.5 %collective-permute-start = (f32[16,32,256]{2,1,0:T(8,128)}, f32[16,32,256]{2,1,0:T(8,128)S(1)}, u32[]{:S(2)}, u32[]{:S(2)}) collective-permute-start(f32[16,32,256]{2,1,0:T(8,128)} %get-tuple-element.12.last_ref), channel_id=1, source_target_pairs={{0,8},{8,16},{16,24},{24,32},{32,40},{40,48},{48,56},{56,64},{64,7... | collective-permute-start | bytes 1572872 | tf_op jit(solution)/shard_map/ppermute | solution.py:236
  12.9 68.7 %collective-permute-start.1 = (f32[16,32,256]{2,1,0:T(8,128)}, f32[16,32,256]{2,1,0:T(8,128)S(1)}, u32[]{:S(2)}, u32[]{:S(2)}) collective-permute-start(f32[16,32,256]{2,1,0:T(8,128)} %get-tuple-element.10.first_ref), channel_id=1, source_target_pairs={{0,248},{8,0},{16,8},{24,16},{32,24},{40,32},{48,40},{56,48},{64,5... | collective-permute-start | bytes 1572872 | tf_op jit(solution)/shard_map/ppermute | solution.py:236
  22.4 0.8 copy-start.1
  25.3 28.0 %all-to-all-start.1 = ((f32[32,8,128]{2,1,0:T(8,128)}), f32[32,8,128]{2,1,0:T(8,128)S(1)}, u32[]{:S(2)}, u32[]{:S(2)}) async-start(f32[32,8,128]{2,1,0:T(8,128)} %forward_y.1), calls=%async_computation.1 | async-start | bytes 262144 | tf_op jit(solution)/shard_map/all_to_all | solution.py:240
  53.2 28.3 %copy-start.2 = (f32[16,32,256]{2,1,0:T(8,128)}, f32[16,32,256]{2,1,0:T(8,128)S(1)}, u32[]{:S(2)}) copy-start(f32[16,32,256]{2,1,0:T(8,128)S(1)} %collective-permute-done.before_ref) | copy-start | bytes 1572868
  53.3 0.7 copy-start.4
  57.0 17.5 %all-to-all-start.2 = ((f32[32,8,128]{2,1,0:T(8,128)}), f32[32,8,128]{2,1,0:T(8,128)S(1)}, u32[]{:S(2)}, u32[]{:S(2)}) async-start(f32[32,8,128]{2,1,0:T(8,128)} %middle.1), calls=%async_computation.2 | async-start | bytes 262144 | tf_op jit(solution)/shard_map/all_to_all | solution.py:240
  74.5 0.7 copy-start.5
  77.3 38.7 %all-to-all-start.3 = ((f32[8,16,8,128]{3,2,1,0:T(8,128)}), f32[8,16,8,128]{3,2,1,0:T(8,128)S(1)}, u32[]{:S(2)}, u32[]{:S(2)}) async-start(f32[8,16,8,128]{3,2,1,0:T(8,128)} %inverse_y.1), calls=%async_computation.3 | async-start | bytes 1048576 | tf_op jit(solution)/shard_map/all_to_all | solution.py:240
  81.6 18.7 %copy-start.3 = (f32[16,32,256]{2,1,0:T(8,128)}, f32[16,32,256]{2,1,0:T(8,128)S(1)}, u32[]{:S(2)}) copy-start(f32[16,32,256]{2,1,0:T(8,128)S(1)} %collective-permute-done.1.after_ref) | copy-start | bytes 1572868
  81.6 12.3 %collective-permute-start.3 = (f32[6,32,256]{2,1,0:T(8,128)S(1)}, f32[6,32,256]{2,1,0:T(8,128)S(1)}, u32[]{:S(2)}, u32[]{:S(2)}) collective-permute-start(f32[6,32,256]{2,1,0:T(8,128)S(1)} %get-tuple-element.15), channel_id=1, source_target_pairs={{0,7},{1,0},{2,1},{3,2},{4,3},{5,4},{6,5},{7,6},{8,15},{9,8},{10,9... | collective-permute-start | bytes 589832 | tf_op jit(solution)/shard_map/ppermute | solution.py:236
  86.7 13.5 %collective-permute-start.2 = (f32[6,32,256]{2,1,0:T(8,128)S(1)}, f32[6,32,256]{2,1,0:T(8,128)S(1)}, u32[]{:S(2)}, u32[]{:S(2)}) collective-permute-start(f32[6,32,256]{2,1,0:T(8,128)S(1)} %get-tuple-element.16), channel_id=1, source_target_pairs={{0,1},{1,2},{2,3},{3,4},{4,5},{5,6},{6,7},{7,0},{8,9},{9,10},{10,1... | collective-permute-start | bytes 589832 | tf_op jit(solution)/shard_map/ppermute | solution.py:236
  93.9 6.4 %copy-start.6 = (f32[6,32,256]{2,1,0:T(8,128)}, f32[6,32,256]{2,1,0:T(8,128)S(1)}, u32[]{:S(2)}) copy-start(f32[6,32,256]{2,1,0:T(8,128)S(1)} %collective-permute-done.3.right_ref) | copy-start | bytes 589828
  100.2 0.7 copy-start.7
  116.0 0.8 copy-start

commit v2 on v1

--- a/solution.py
+++ b/solution.py
@@ -136,99 +136,194 @@
             out[pl.ds(2 * k + part, 128, stride=8), :] = result[128 * part : 128 * part + 128]
 
 
-def final(data_ref, base_ref, th_ref, tl_ref, out_ref):
-    rows = out_ref.reshape(1024, 128)
+def final(data_ref, base_ref, th_ref, tl_ref, out_ref, held, sems):
     table = jnp.concatenate([th_ref[...], th_ref[...], tl_ref[...]], axis=0)
-    for y in range(8):
-        high, low = split(data_ref[:, y].reshape(64, 128))
-        stacked = jnp.concatenate([high, low, high], axis=0)
-        spectral = mm_tn(stacked, table)
-        for x in range(4):
-            value = spectral[32 * x : 32 * x + 32] + base_ref[x, y]
-            rows[pl.ds(x * 8 + y, 32, stride=32), :] = jax.nn.gelu(value)
-
-
-def weights(data_ref, out_ref):
+    copies = []
+    for half in range(2):
+        slots = [held.at[half, side] for side in range(2)]
+        rows = [slot.reshape(1024, 128) for slot in slots]
+        for y in range(8):
+            high, low = split(data_ref[:, 8 * half + y].reshape(64, 128))
+            stacked = jnp.concatenate([high, low, high], axis=0)
+            spectral = mm_tn(stacked, table)
+            for x in range(4):
+                value = spectral[32 * x : 32 * x + 32] + base_ref[x, 8 * half + y]
+                value = jax.nn.gelu(value)
+                for side in range(2):
+                    rows[side][pl.ds(x * 8 + y, 32, stride=32), :] = value[
+                        :, 128 * side : 128 * side + 128
+                    ]
+        for side in range(2):
+            copy = pltpu.make_async_copy(
+                slots[side],
+                out_ref.at[:, pl.ds(8 * half, 8), pl.ds(128 * side, 128)],
+                sems.at[half, side],
+            )
+            copy.start()
+            copies.append(copy)
+    for copy in copies:
+        copy.wait()
+
+
+def weights(data_ref, out_ref, held, sem):
+    copy = pltpu.make_async_copy(data_ref, held.at[:, pl.ds(0, 128), :], sem)
+    copy.start()
+    copy.wait()
+    rows = held.reshape(64 * 136, 32)
+
     def body(c, carry):
         for part in range(2):
             for k in range(4):
-                start = (part * 128 + k) * 32 + c
-                block = data_ref[pl.ds(start, 32, stride=128), :]
+                start = part * 32 * 136 + 32 * k + c
+                block = rows[pl.ds(start, 32, stride=136), :]
                 out_ref[part, c, :, 32 * k : 32 * k + 32] = block
         return carry
 
     lax.fori_loop(0, 32, body, 0)
 
 
-def local(
-    first_ref, middle_ref, last_ref, before_ref, after_ref, left_ref, right_ref,
-    tap_ref, ph_ref, pl_ref, bias_ref, out_ref, frame, sems
+def shift_sum(sums):
+    whole = [jnp.concatenate(pair, axis=1) for pair in sums]
+    return whole[1] + pltpu.roll(whole[0], 1, 1) + pltpu.roll(whole[2], 255, 1)
+
+
+def tap_rows(tap_ref, chans, wanted):
+    taps = tap_ref[chans, :]
+    return {i: jnp.broadcast_to(taps[:, i : i + 1], (8, 128)) for i in wanted}
+
+
+def add_taps(sums, taps, first, cells):
+    for e in range(3):
+        for side in range(2):
+            term = taps[first + e] * cells[side]
+            old = sums[e][side]
+            sums[e][side] = term if old is None else old + term
+
+
+def own_cells(
+    first_ref, middle_ref, last_ref, tap_ref, ph_ref, pl_ref, bias_ref, out_ref, frame, sems
 ):
     moves = [
-        (before_ref, frame.at[0, pl.ds(1, 16)]),
-        (first_ref, frame.at[1, pl.ds(1, 16)]),
-        (middle_ref, frame.at[pl.ds(2, 2), pl.ds(1, 16)]),
-        (last_ref, frame.at[4, pl.ds(1, 16)]),
-        (after_ref, frame.at[5, pl.ds(1, 16)]),
-        (left_ref, frame.at[:, 0]),
-        (right_ref, frame.at[:, 17]),
+        (first_ref, frame.at[0, pl.ds(1, 16)]),
+        (middle_ref, frame.at[pl.ds(1, 2), pl.ds(1, 16)]),
+        (last_ref, frame.at[3, pl.ds(1, 16)]),
     ]
     copies = [
         pltpu.make_async_copy(src, dst, sems.at[i]) for i, (src, dst) in enumerate(moves)
     ]
     for copy in copies:
         copy.start()
+    frame[:, 0] = jnp.zeros((4, 32, 256), F32)
+    frame[:, 17] = jnp.zeros((4, 32, 256), F32)
     for copy in copies:
         copy.wait()
     point = jnp.concatenate([ph_ref[...], pl_ref[...], ph_ref[...]], axis=1)
     bias = jnp.concatenate([bias_ref[...]] * 4, axis=0)
 
     def pointwise(y, carry):
-        data = frame[1:5, y + 1].reshape(128, 256)
+        data = frame[:, y + 1].reshape(128, 256)
         high, low = split(data)
         value = mm(point, jnp.concatenate([high, high, low], axis=0)) + bias
         out_ref[:, y] = value.reshape(4, 32, 256)
         return carry
 
     lax.fori_loop(0, 16, pointwise, 0)
-    lane = lax.broadcasted_iota(jnp.int32, (8, 256), 1)
     for tile in range(4):
         chans = pl.ds(8 * tile, 8)
-        taps = tap_ref[chans, :]
-        taps = [
-            jnp.broadcast_to(taps[:, i : i + 1], (8, 256)) for i in range(27)
-        ]
+        taps = tap_rows(tap_ref, chans, range(27))
 
         def row(y, carry):
             for x in range(4):
-                sums = [None, None, None]
+                sums = [[None, None] for _ in range(3)]
                 for a in range(3):
+                    if not 0 <= x + a - 1 < 4:
+                        continue
                     for b in range(3):
-                        cell = frame[x + a, y + b, chans, :]
-                        for e in range(3):
-                            term = taps[9 * a + 3 * b + e] * cell
-                            sums[e] = term if sums[e] is None else sums[e] + term
-                total = sums[1] + pltpu.roll(sums[0], 1, 1) + pltpu.roll(sums[2], 255, 1)
-                out_ref[x, y, chans, :] = out_ref[x, y, chans, :] + total
+                        cells = [
+                            frame[x + a - 1, y + b, chans, 128 * side : 128 * side + 128]
+                            for side in range(2)
+                        ]
+                        add_taps(sums, taps, 9 * a + 3 * b, cells)
+                out_ref[x, y, chans, :] = out_ref[x, y, chans, :] + shift_sum(sums)
             return carry
 
         lax.fori_loop(0, 16, row, 0)
+
+
+def edge_cells(
+    base_ref, before_ref, after_ref, left_ref, right_ref, tap_ref, out_ref, frame, sems
+):
+    moves = [
+        (before_ref, frame.at[0, pl.ds(1, 16)]),
+        (left_ref.at[0], frame.at[0, 0]),
+        (right_ref.at[0], frame.at[0, 17]),
+        (after_ref, frame.at[1, pl.ds(1, 16)]),
+        (left_ref.at[5], frame.at[1, 0]),
+        (right_ref.at[5], frame.at[1, 17]),
+    ]
+    copies = [
+        pltpu.make_async_copy(src, dst, sems.at[i]) for i, (src, dst) in enumerate(moves)
+    ]
+    for copy in copies:
+        copy.start()
+    for tile in range(4):
+        chans = pl.ds(8 * tile, 8)
+        for edge, source in enumerate((left_ref, right_ref)):
+            b = 2 * edge
+            y = 15 * edge
+            taps = tap_rows(
+                tap_ref, chans, [9 * a + 3 * b + e for a in range(3) for e in range(3)]
+            )
+            for x in range(4):
+                sums = [[None, None] for _ in range(3)]
+                for a in range(3):
+                    if not 0 <= x + a - 1 < 4:
+                        continue
+                    cells = [
+                        source[x + a, chans, 128 * side : 128 * side + 128]
+                        for side in range(2)
+                    ]
+                    add_taps(sums, taps, 9 * a + 3 * b, cells)
+                out_ref[x, y, chans, :] = base_ref[x, y, chans, :] + shift_sum(sums)
+    for copy in copies:
+        copy.wait()
+    for tile in range(4):
+        chans = pl.ds(8 * tile, 8)
+        for edge in range(2):
+            a, x = 2 * edge, 3 * edge
+            taps = tap_rows(tap_ref, chans, range(9 * a, 9 * a + 9))
+
+            def row(y, carry):
+                sums = [[None, None] for _ in range(3)]
+                for b in range(3):
+                    cells = [
+                        frame[edge, y + b, chans, 128 * side : 128 * side + 128]
+                        for side in range(2)
+                    ]
+                    add_taps(sums, taps, 9 * a + 3 * b, cells)
+                out_ref[x, y, chans, :] = out_ref[x, y, chans, :] + shift_sum(sums)
+                return carry
+
+            lax.fori_loop(0, 16, row, 0, unroll=2)
 
 
 VMEM = pl.BlockSpec(memory_space=pltpu.VMEM)
 ANY = pl.BlockSpec(memory_space=pl.ANY)
 
 
-def call(body, shapes, count, **kw):
-    single = not isinstance(shapes, list)
-    out_shape = [jax.ShapeDtypeStruct(s, F32) for s in ([shapes] if single else shapes)]
-    kw.setdefault("in_specs", [VMEM] * count)
+def call(body, shapes, inputs, **kw):
+    out_shape = [shape if kind is None else kind(shape, F32) for shape, kind in shapes]
+    kw.setdefault("in_specs", [VMEM] * inputs)
     kw.setdefault("out_specs", [VMEM] * len(out_shape))
-    if single:
-        out_shape = out_shape[0]
-        if isinstance(kw["out_specs"], list):
-            kw["out_specs"] = kw["out_specs"][0]
     return pl.pallas_call(body, out_shape=out_shape, name=body.__name__, **kw)
+
+
+def near(value):
+    return pltpu.with_memory_space_constraint(value, pltpu.VMEM)
+
+
+def after_all(value, *others):
+    return lax.optimization_barrier((value, *others))[0]
 
 
 def shifted(axis, value, step):
@@ -246,9 +341,16 @@
         for name, value in tables(32, 128, 128, 256).items()
     }
     whole = lambda *shape: pl.BlockSpec(shape, lambda i: (0,) * len(shape))
+    plain, kept_near = jax.ShapeDtypeStruct, pltpu.VMEM
+    cells = field.reshape(128, 16, 256)
     zchunks, first, mid, last = call(
         forward_z,
-        [(8, 16, 8, 128), (16, 32, 256), (2, 16, 32, 256), (16, 32, 256)],
+        [
+            ((8, 16, 8, 128), plain),
+            ((16, 32, 256), plain),
+            ((2, 16, 32, 256), plain),
+            ((16, 32, 256), plain),
+        ],
         4,
         grid=(2,),
         in_specs=[
@@ -263,48 +365,71 @@
             pl.BlockSpec((2, 8, 32, 256), lambda i: (0, i, 0, 0)),
             pl.BlockSpec((8, 32, 256), lambda i: (i, 0, 0)),
         ],
-    )(field.reshape(128, 16, 256), field.reshape(128, 16, 256), *tab["fz"])
+    )(cells, cells, *tab["fz"])
+
     zall = exchange(zchunks, "gy")
-    before = shifted("gx", last, 1)
-    after = shifted("gx", first, -1)
-    packed = call(weights, (2, 32, 32, 128), 1)(spec_weight.reshape(8192, 32))
-    ychunks = call(forward_y, (32, 8, 128), 3)(zall, *tab["fy"])
+    (packed,) = call(
+        weights,
+        [((2, 32, 32, 128), kept_near)],
+        1,
+        in_specs=[ANY],
+        scratch_shapes=[pltpu.VMEM((64, 136, 32), F32), pltpu.SemaphoreType.DMA],
+    )(after_all(spec_weight.reshape(64, 128, 32), zchunks))
+    zall, packed = lax.optimization_barrier((zall, packed))
+    (ychunks,) = call(forward_y, [((32, 8, 128), plain)], 3)(near(zall), *tab["fy"])
+
     yall = exchange(ychunks, "gx")
+    edge_first, edge_last, _ = lax.optimization_barrier((first, last, ychunks))
+    before = shifted("gx", edge_last, 1)
+    after = shifted("gx", edge_first, -1)
+    blocks = jnp.kron(jnp.eye(4, dtype=F32), point_weight.T)
+    point_high = blocks.astype(BF16)
+    point_low = (blocks - lax.reduce_precision(blocks, 8, 7)).astype(BF16)
+    taps = dw_kernel.reshape(32, 27)
+    (base,) = call(
+        own_cells,
+        [((4, 16, 32, 256), kept_near)],
+        7,
+        in_specs=[ANY] * 3 + [VMEM] * 4,
+        scratch_shapes=[pltpu.VMEM((4, 18, 32, 256), F32), pltpu.SemaphoreType.DMA((3,))],
+    )(
+        after_all(first, ychunks), mid, last,
+        taps, point_high, point_low, bias.reshape(32, 1),
+    )
+    yall, base = lax.optimization_barrier((yall, base))
+    (xchunks,) = call(middle, [((32, 8, 128), plain)], 6)(
+        near(yall), near(packed), *tab["fx"], *tab["ix"]
+    )
+
+    xall = exchange(xchunks, "gx")
+    before, after, _ = lax.optimization_barrier((before, after, xchunks))
     rows = [before[None], first[None], mid, last[None], after[None]]
     top = jnp.concatenate([r[:, 15] for r in rows], axis=0)
     bottom = jnp.concatenate([r[:, 0] for r in rows], axis=0)
     left = shifted("gy", top, 1)
     right = shifted("gy", bottom, -1)
-    xchunks = call(middle, (32, 8, 128), 6)(yall, packed, *tab["fx"], *tab["ix"])
-    xall = exchange(xchunks, "gx")
-    blocks = jnp.kron(jnp.eye(4, dtype=F32), point_weight.T)
-    point_high = blocks.astype(BF16)
-    point_low = (blocks - lax.reduce_precision(blocks, 8, 7)).astype(BF16)
-    base = call(
-        local,
-        (4, 16, 32, 256),
-        11,
-        in_specs=[ANY] * 7 + [VMEM] * 4,
-        scratch_shapes=[pltpu.VMEM((6, 18, 32, 256), F32), pltpu.SemaphoreType.DMA((7,))],
-    )(
-        first, mid, last, before, after, left, right,
-        dw_kernel.reshape(32, 27), point_high, point_low, bias.reshape(32, 1),
-    )
-    back = call(inverse_y, (8, 16, 8, 128), 3)(xall, *tab["iy"])
+    (back,) = call(inverse_y, [((8, 16, 8, 128), plain)], 3)(near(xall), *tab["iy"])
+
     ball = exchange(back, "gy")
-    out = call(
+    left, right, _ = lax.optimization_barrier((left, right, back))
+    (base,) = call(
+        edge_cells,
+        [((4, 16, 32, 256), kept_near)],
+        6,
+        in_specs=[VMEM] + [ANY] * 2 + [VMEM] * 3,
+        scratch_shapes=[pltpu.VMEM((2, 18, 32, 256), F32), pltpu.SemaphoreType.DMA((6,))],
+        input_output_aliases={0: 0},
+    )(near(base), before, after, near(left), near(right), taps)
+    ball, base = lax.optimization_barrier((ball, base))
+    (out,) = call(
         final,
-        (128, 16, 256),
+        [((128, 16, 256), plain)],
         4,
-        grid=(2, 2),
-        in_specs=[
-            pl.BlockSpec((8, 8, 8, 128), lambda i, j: (0, i, 0, 0)),
-            pl.BlockSpec((4, 8, 32, 128), lambda i, j: (0, i, 0, j)),
-            pl.BlockSpec((64, 128), lambda i, j: (0, j)),
-            pl.BlockSpec((64, 128), lambda i, j: (0, j)),
+        out_specs=[ANY],
+        scratch_shapes=[
+            pltpu.VMEM((2, 2, 128, 8, 128), F32), pltpu.SemaphoreType.DMA((2, 2)),
         ],
-        out_specs=pl.BlockSpec((128, 8, 128), lambda i, j: (0, i, j)),
-    )(ball, base, *tab["iz"])
+    )(near(ball), near(base), *tab["iz"])
     return out.reshape(field.shape)
 
 

time: 123 us -> 111 us (0.902)
  blocking collectives: 0 us -> 18.9 us
  waiting for transfers between devices: 29.9 us -> 13.5 us
  starting transfers between devices: 43.2 us -> 28.3 us
    all_to_all x0 -> x1, blocking collectives: none -> 18.9 us  [exchange(): return lax.all_to_all(value, axis, split_axis=0, concat_axis=0, tiled=True)]
    all_to_all x4 -> x3, starting transfers between devices: 37 us -> 21.5 us  [exchange(): return lax.all_to_all(value, axis, split_axis=0, concat_axis=0, tiled=True)]
    all_to_all x4 -> x3, waiting for transfers between devices: 17 us -> 5.04 us  [exchange(): return lax.all_to_all(value, axis, split_axis=0, concat_axis=0, tiled=True)]
    ppermute x4, waiting for transfers between devices: 12.9 us -> 8.49 us  [shifted(): lax.ppermute(value, axis, [(i, (i + step) % count) for i in range(count)])]
    pallas_call x7 -> x8, Pallas kernels: 40.4 us -> 40 us  [the longest x1 12.7 us: on_device(): call(own_cells, [((4, 16, 32, 256), kept_near)], 7, in_specs=[ANY] * 3 +...]
    unnamed x26 -> x14, local copies, waits for them, and re-layouts: 6.06 us -> 6.15 us
  transfers between devices with their start and end apart: 8 -> 7, of which waited for: 4 -> 3; matrix products, arithmetic and copies ran while one was open for 4% -> 6% of each run, Pallas kernels for 25% -> 28%
where the time goes in v2:
time: 111 us; the launch traced here: 110 us
  Pallas kernels  40 us (36%)
  starting transfers between devices  28.3 us (25%)
  blocking collectives  18.9 us (17%)
  waiting for transfers between devices  13.5 us (12%)
  local copies, waits for them, and re-layouts  8.54 us (8%)
    all_to_all x3, starting transfers between devices, exchange(): return lax.all_to_all(value, axis, split_axis=0, concat_axis=0, tiled=True)  21.5 us
    all_to_all x1, blocking collectives, exchange(): return lax.all_to_all(value, axis, split_axis=0, concat_axis=0, tiled=True)  18.9 us
    pallas_call x1, Pallas kernels, on_device(): call(own_cells, [((4, 16, 32, 256), kept_near)], 7, in_specs=[ANY] * 3 +...  12.7 us
    ppermute x4, waiting for transfers between devices, shifted(): lax.ppermute(value, axis, [(i, (i + step) % count) for i in range(count)])  8.49 us
    pallas_call x1, Pallas kernels, on_device(): call(edge_cells, [((4, 16, 32, 256), kept_near)], 6, in_specs=[VMEM] + [A...  7.39 us
    ppermute x4, starting transfers between devices, shifted(): lax.ppermute(value, axis, [(i, (i + step) % count) for i in range(count)])  6.8 us
    unnamed x14, local copies, waits for them, and re-layouts  6.15 us
    pallas_call x1, Pallas kernels, on_device(): call(weights, [((2, 32, 32, 128), kept_near)], 1, in_specs=[ANY], scratch...  5.52 us
  transfers between devices with their start and end apart: 7, of which 3 were waited for; matrix products, arithmetic and copies ran while one was open for 6% of the time, Pallas kernels for 28%

profile of v2, /device:TPU:1, one launch (start us, length us, event | category | flops | bytes accessed | tf_op | source)
XLA Modules:
  0.0 110.1 jit_solution(11023804515002972871)
XLA Ops:
  0.0 4.1 %forward_z.1 = (f32[8,16,8,128]{3,2,1,0:T(8,128)}, f32[16,32,256]{2,1,0:T(8,128)}, f32[2,16,32,256]{3,2,1,0:T(8,128)}, f32[16,32,256]{2,1,0:T(8,128)}) custom-call(f32[128,16,256]{2,1,0:T(8,128)} %bitcast.51, f32[128,16,256]{2,1,0:T(8,128)} %bitcast.52, bf16[64,256]{1,0:T(8,128)(2,1)} %constant.24.clone.th_ref, bf16[64,256]{1,0:T(8,128)(2,1)} %constant.25.clone.tl_ref), custom_call_target="tpu_custom_call" | custom-call | tf_op jit(solution)/shard_map/forward_z/pallas_call | solution.py:346
  4.1 7.5 %all-to-all-start = ((f32[8,16,8,128]{3,2,1,0:T(8,128)}), f32[8,16,8,128]{3,2,1,0:T(8,128)S(1)}, u32[]{:S(2)}, u32[]{:S(2)}) async-start(f32[8,16,8,128]{3,2,1,0:T(8,128)} %get-tuple-element.23), calls=%async_computation | async-start | bytes 1048576 | tf_op jit(solution)/shard_map/all_to_all | solution.py:335
  11.6 0.0 copy-start.3
  11.6 0.0 copy-start.2
  11.6 0.0 copy-start.4
  11.6 5.5 %weights.1.weight_ref = f32[2,32,32,128]{3,2,1,0:T(8,128)S(1)} custom-call(f32[64,128,32]{2,1,0:T(8,128)} %bitcast.53), custom_call_target="tpu_custom_call" | custom-call | tf_op jit(solution)/shard_map/weights/pallas_call | solution.py:371
  17.2 0.0 copy-done.3
  17.2 0.1 copy.24
  17.2 5.0 %all-to-all-done.data_ref = f32[8,16,8,128]{3,2,1,0:T(8,128)S(1)} async-done(((f32[8,16,8,128]{3,2,1,0:T(8,128)}), f32[8,16,8,128]{3,2,1,0:T(8,128)S(1)}, u32[]{:S(2)}, u32[]{:S(2)}) %all-to-all-start) | async-done | bytes 524320 | tf_op jit(solution)/shard_map/all_to_all | solution.py:335
  22.3 1.8 %forward_y.1 = f32[32,8,128]{2,1,0:T(8,128)} custom-call(f32[8,16,8,128]{3,2,1,0:T(8,128)S(1)} %all-to-all-done.data_ref, bf16[64,256]{1,0:T(8,128)(2,1)} %constant.28.clone.th_ref, bf16[64,256]{1,0:T(8,128)(2,1)} %constant.29.clone.tl_ref), custom_call_target="tpu_custom_call" | custom-call | tf_op jit(solution)/shard_map/forward_y/pallas_call | solution.py:379
  24.1 10.5 %all-to-all-start.1 = ((f32[32,8,128]{2,1,0:T(8,128)}), f32[32,8,128]{2,1,0:T(8,128)S(1)}, u32[]{:S(2)}, u32[]{:S(2)}) async-start(f32[32,8,128]{2,1,0:T(8,128)} %forward_y.1), calls=%async_computation.1 | async-start | bytes 262144 | tf_op jit(solution)/shard_map/all_to_all | solution.py:335
  34.6 1.7 %collective-permute-start = (f32[16,32,256]{2,1,0:T(8,128)}, f32[16,32,256]{2,1,0:T(8,128)}, u32[]{:S(2)}, u32[]{:S(2)}) collective-permute-start(f32[16,32,256]{2,1,0:T(8,128)} %get-tuple-element.33.last_ref), channel_id=1, source_target_pairs={{0,8},{8,16},{16,24},{24,32},{32,40},{40,48},{48,56},{56,64},{64,7... | collective-permute-start | bytes 1572872 | tf_op jit(solution)/shard_map/ppermute | solution.py:331
  36.3 0.0 collective-permute-start.1
  36.3 0.1 broadcast_multiply_fusion
  36.4 0.2 mul.27
  36.6 0.0 copy-done.2
  36.6 0.7 copy.25.tap_ref
  37.3 0.0 copy-done.4
  37.3 0.7 copy.26.bias_ref
  38.0 0.6 fusion
  38.6 12.7 %own_cells.1.base_ref = f32[4,16,32,256]{3,2,1,0:T(8,128)S(1)} custom-call(f32[16,32,256]{2,1,0:T(8,128)} %get-tuple-element.34.first_ref, f32[2,16,32,256]{3,2,1,0:T(8,128)} %get-tuple-element.28.middle_ref, f32[16,32,256]{2,1,0:T(8,128)} %get-tuple-element.33.last_ref, f32[32,27]{1,0:T(8,128)} %copy.25.tap_ref, bf16[128,128]{1,0:T(8,128)(2,1)} %get-tuple-element.52.ph_ref, ...), custom_call_target="tpu_custom_call" | custom-call | tf_op jit(solution)/shard_map/own_cells/pallas_call | solution.py:389
  51.3 0.0 copy-start
  51.3 1.3 %copy-done = f32[4,16,32,256]{3,2,1,0:T(8,128)} copy-done((f32[4,16,32,256]{3,2,1,0:T(8,128)}, f32[4,16,32,256]{3,2,1,0:T(8,128)S(1)}, u32[]{:S(2)}) %copy-start) | copy-done | bytes 2097176
  52.6 0.0 all-to-all-done.1.data_ref
  52.6 2.7 %middle.1 = f32[32,8,128]{2,1,0:T(8,128)} custom-call(f32[32,8,128]{2,1,0:T(8,128)S(1)} %all-to-all-done.1.data_ref, f32[2,32,32,128]{3,2,1,0:T(8,128)S(1)} %weights.1.weight_ref, bf16[64,256]{1,0:T(8,128)(2,1)} %constant.32.clone.fh_ref, bf16[64,256]{1,0:T(8,128)(2,1)} %constant.33.clone.fl_ref, bf16[256,64]{1,0:T(8,128)(2,1)} %constant.34.clone.ih_ref, ...), custom_call_target="tpu_custom_call" | custom-call | tf_op jit(solution)/shard_map/middle/pallas_call | solution.py:400
  55.3 18.9 %all_to_all.20.data_ref = f32[32,8,128]{2,1,0:T(8,128)S(1)} all-to-all(f32[32,8,128]{2,1,0:T(8,128)} %middle.1), channel_id=1, replica_groups=mesh['gx'=32,'gy'=8] {'gx'}, dimensions={0} | all-to-all | bytes 262144 | tf_op jit(solution)/shard_map/all_to_all | solution.py:335
  74.2 2.0 %inverse_y.1 = f32[8,16,8,128]{3,2,1,0:T(8,128)} custom-call(f32[32,8,128]{2,1,0:T(8,128)S(1)} %all_to_all.20.data_ref, bf16[256,64]{1,0:T(8,128)(2,1)} %constant.30.clone.th_ref, bf16[256,64]{1,0:T(8,128)(2,1)} %constant.31.clone.tl_ref), custom_call_target="tpu_custom_call" | custom-call | tf_op jit(solution)/shard_map/inverse_y/pallas_call | solution.py:411
  76.2 3.5 %all-to-all-start.3 = ((f32[8,16,8,128]{3,2,1,0:T(8,128)}), f32[8,16,8,128]{3,2,1,0:T(8,128)S(1)}, u32[]{:S(2)}, u32[]{:S(2)}) async-start(f32[8,16,8,128]{3,2,1,0:T(8,128)} %inverse_y.1), calls=%async_computation.3 | async-start | bytes 1048576 | tf_op jit(solution)/shard_map/all_to_all | solution.py:335
  79.7 0.0 collective-permute-done.before_ref
  79.7 0.0 collective-permute-done.1.after_ref
  79.7 0.8 fusion.6
  80.5 0.8 fusion.5
  81.3 0.9 fusion.1
  82.1 0.8 fusion.4
  82.9 0.8 fusion.3
  83.7 2.9 %collective-permute-start.2 = (f32[6,32,256]{2,1,0:T(8,128)S(1)}, f32[6,32,256]{2,1,0:T(8,128)S(1)}, u32[]{:S(2)}, u32[]{:S(2)}) collective-permute-start(f32[6,32,256]{2,1,0:T(8,128)S(1)} %get-tuple-element.44), channel_id=1, source_target_pairs={{0,1},{1,2},{2,3},{3,4},{4,5},{5,6},{6,7},{7,0},{8,9},{9,10},{10,1... | collective-permute-start | bytes 589832 | tf_op jit(solution)/shard_map/ppermute | solution.py:331
  86.6 2.2 %collective-permute-start.3 = (f32[6,32,256]{2,1,0:T(8,128)S(1)}, f32[6,32,256]{2,1,0:T(8,128)S(1)}, u32[]{:S(2)}, u32[]{:S(2)}) collective-permute-start(f32[6,32,256]{2,1,0:T(8,128)S(1)} %get-tuple-element.43), channel_id=1, source_target_pairs={{0,7},{1,0},{2,1},{3,2},{4,3},{5,4},{6,5},{7,6},{8,15},{9,8},{10,9... | collective-permute-start | bytes 589832 | tf_op jit(solution)/shard_map/ppermute | solution.py:331
  88.8 6.1 %collective-permute-done.2.left_ref = f32[6,32,256]{2,1,0:T(8,128)S(1)} collective-permute-done((f32[6,32,256]{2,1,0:T(8,128)S(1)}, f32[6,32,256]{2,1,0:T(8,128)S(1)}, u32[]{:S(2)}, u32[]{:S(2)}) %collective-permute-start.2) | collective-permute-done | bytes 196640 | tf_op jit(solution)/shard_map/ppermute | solution.py:331
  94.9 2.4 %collective-permute-done.3.right_ref = f32[6,32,256]{2,1,0:T(8,128)S(1)} collective-permute-done((f32[6,32,256]{2,1,0:T(8,128)S(1)}, f32[6,32,256]{2,1,0:T(8,128)S(1)}, u32[]{:S(2)}, u32[]{:S(2)}) %collective-permute-start.3) | collective-permute-done | bytes 196640 | tf_op jit(solution)/shard_map/ppermute | solution.py:331
  97.3 0.0 copy-start.1
  97.3 1.6 %copy-done.1 = f32[4,16,32,256]{3,2,1,0:T(8,128)S(1)} copy-done((f32[4,16,32,256]{3,2,1,0:T(8,128)S(1)}, f32[4,16,32,256]{3,2,1,0:T(8,128)}, u32[]{:S(2)}) %copy-start.1) | copy-done | bytes 2097176
  98.9 7.4 %edge_cells.1.base_ref = f32[4,16,32,256]{3,2,1,0:T(8,128)S(1)} custom-call(f32[4,16,32,256]{3,2,1,0:T(8,128)S(1)} %copy-done.1, f32[16,32,256]{2,1,0:T(8,128)} %collective-permute-done.before_ref, f32[16,32,256]{2,1,0:T(8,128)} %collective-permute-done.1.after_ref, ...), custom_call_target="tpu_custom_call", output_to_operand_aliasing={{}: (0, {})} | custom-call | tf_op jit(solution)/shard_map/edge_cells/pallas_call | solution.py:415
  106.3 0.0 all-to-all-done.3.data_ref
  106.3 3.8 %final.1 = f32[128,16,256]{2,1,0:T(8,128)} custom-call(f32[8,16,8,128]{3,2,1,0:T(8,128)S(1)} %all-to-all-done.3.data_ref, f32[4,16,32,256]{3,2,1,0:T(8,128)S(1)} %edge_cells.1.base_ref, bf16[64,256]{1,0:T(8,128)(2,1)} %constant.26.clone.th_ref, bf16[64,256]{1,0:T(8,128)(2,1)} %constant.27.clone.tl_ref), custom_call_target="tpu_custom_call" | custom-call | tf_op jit(solution)/shard_map/final/pallas_call | solution.py:424
  (2 shorter events, 0.0 us)
Async XLA Ops:
  4.1 18.2 %all-to-all-start = ((f32[8,16,8,128]{3,2,1,0:T(8,128)}), f32[8,16,8,128]{3,2,1,0:T(8,128)S(1)}, u32[]{:S(2)}, u32[]{:S(2)}) async-start(f32[8,16,8,128]{3,2,1,0:T(8,128)} %get-tuple-element.23), calls=%async_computation | async-start | bytes 1048576 | tf_op jit(solution)/shard_map/all_to_all | solution.py:335
  11.6 5.6 %copy-start.3 = (f32[32,32]{1,0:T(8,128)S(1)}, f32[32,32]{1,0:T(8,128)}, u32[]{:S(2)}) copy-start(f32[32,32]{1,0:T(8,128)} %param.20) | copy-start | bytes 12292
  11.6 25.0 %copy-start.2 = (f32[32,3,3,3]{0,3,2,1:T(4,128)S(1)}, f32[32,3,3,3]{0,3,2,1:T(4,128)}, u32[]{:S(2)}) copy-start(f32[32,3,3,3]{0,3,2,1:T(4,128)} %param.19) | copy-start | bytes 10372
  11.6 25.7 %copy-start.4 = (f32[32]{0:T(128)S(1)}, f32[32]{0:T(128)}, u32[]{:S(2)}) copy-start(f32[32]{0:T(128)} %param.21) | copy-start | bytes 388
  24.1 28.5 %all-to-all-start.1 = ((f32[32,8,128]{2,1,0:T(8,128)}), f32[32,8,128]{2,1,0:T(8,128)S(1)}, u32[]{:S(2)}, u32[]{:S(2)}) async-start(f32[32,8,128]{2,1,0:T(8,128)} %forward_y.1), calls=%async_computation.1 | async-start | bytes 262144 | tf_op jit(solution)/shard_map/all_to_all | solution.py:335
  34.6 45.1 %collective-permute-start = (f32[16,32,256]{2,1,0:T(8,128)}, f32[16,32,256]{2,1,0:T(8,128)}, u32[]{:S(2)}, u32[]{:S(2)}) collective-permute-start(f32[16,32,256]{2,1,0:T(8,128)} %get-tuple-element.33.last_ref), channel_id=1, source_target_pairs={{0,8},{8,16},{16,24},{24,32},{32,40},{40,48},{48,56},{56,64},{64,7... | collective-permute-start | bytes 1572872 | tf_op jit(solution)/shard_map/ppermute | solution.py:331
  36.3 43.4 %collective-permute-start.1 = (f32[16,32,256]{2,1,0:T(8,128)}, f32[16,32,256]{2,1,0:T(8,128)}, u32[]{:S(2)}, u32[]{:S(2)}) collective-permute-start(f32[16,32,256]{2,1,0:T(8,128)} %get-tuple-element.34.first_ref), channel_id=1, source_target_pairs={{0,248},{8,0},{16,8},{24,16},{32,24},{40,32},{48,40},{56,48},{64,5... | collective-permute-start | bytes 1572872 | tf_op jit(solution)/shard_map/ppermute | solution.py:331
  51.3 1.3 %copy-start = (f32[4,16,32,256]{3,2,1,0:T(8,128)}, f32[4,16,32,256]{3,2,1,0:T(8,128)S(1)}, u32[]{:S(2)}) copy-start(f32[4,16,32,256]{3,2,1,0:T(8,128)S(1)} %own_cells.1.base_ref) | copy-start | bytes 6291460
  76.2 30.1 %all-to-all-start.3 = ((f32[8,16,8,128]{3,2,1,0:T(8,128)}), f32[8,16,8,128]{3,2,1,0:T(8,128)S(1)}, u32[]{:S(2)}, u32[]{:S(2)}) async-start(f32[8,16,8,128]{3,2,1,0:T(8,128)} %inverse_y.1), calls=%async_computation.3 | async-start | bytes 1048576 | tf_op jit(solution)/shard_map/all_to_all | solution.py:335
  83.7 11.2 %collective-permute-start.2 = (f32[6,32,256]{2,1,0:T(8,128)S(1)}, f32[6,32,256]{2,1,0:T(8,128)S(1)}, u32[]{:S(2)}, u32[]{:S(2)}) collective-permute-start(f32[6,32,256]{2,1,0:T(8,128)S(1)} %get-tuple-element.44), channel_id=1, source_target_pairs={{0,1},{1,2},{2,3},{3,4},{4,5},{5,6},{6,7},{7,0},{8,9},{9,10},{10,1... | collective-permute-start | bytes 589832 | tf_op jit(solution)/shard_map/ppermute | solution.py:331
  86.6 10.7 %collective-permute-start.3 = (f32[6,32,256]{2,1,0:T(8,128)S(1)}, f32[6,32,256]{2,1,0:T(8,128)S(1)}, u32[]{:S(2)}, u32[]{:S(2)}) collective-permute-start(f32[6,32,256]{2,1,0:T(8,128)S(1)} %get-tuple-element.43), channel_id=1, source_target_pairs={{0,7},{1,0},{2,1},{3,2},{4,3},{5,4},{6,5},{7,6},{8,15},{9,8},{10,9... | collective-permute-start | bytes 589832 | tf_op jit(solution)/shard_map/ppermute | solution.py:331
  97.3 1.6 %copy-start.1 = (f32[4,16,32,256]{3,2,1,0:T(8,128)S(1)}, f32[4,16,32,256]{3,2,1,0:T(8,128)}, u32[]{:S(2)}) copy-start(f32[4,16,32,256]{3,2,1,0:T(8,128)} %copy-done) | copy-start | bytes 6291460

commit v3 on v1

v3 whole, which is shorter than its diff:
```python
import functools

import jax
import jax.numpy as jnp
import numpy as np
from jax import lax
from jax.experimental import pallas as pl
from jax.experimental.pallas import tpu as pltpu
from jax.sharding import PartitionSpec as P

F32 = jnp.float32
BF16 = jnp.bfloat16


def halves(table):
    high = np.asarray(table, np.float32).astype(BF16)
    low = (np.asarray(table, np.float64) - high.astype(np.float64)).astype(BF16)
    return high, low


def kept(modes, length):
    index = np.arange(modes)
    return np.where(index < modes // 2, index, index + length - modes)


def angles(freqs, length):
    product = np.outer(freqs, np.arange(length)) % length
    turn = 2.0 * np.pi * product / length
    return np.cos(turn), np.sin(turn)


def tables(modes, full_x, full_y, depth):
    zc, zs = angles(np.arange(modes), depth)
    fz = np.stack([zc, -zs], axis=1).reshape(2 * modes, depth)
    weight = np.where(np.arange(modes) == 0, 1.0, 2.0)[:, None] / depth
    iz = np.stack([weight * zc, -weight * zs], axis=1).reshape(2 * modes, depth)
    yc, ys = angles(kept(modes, full_y), full_y)
    fy = np.block([[yc, ys], [-ys, yc]])
    iy = np.block([[yc.T, -ys.T], [ys.T, yc.T]]) / full_y
    xc, xs = angles(kept(modes, full_x), full_x)
    fx = np.concatenate(
        [np.stack([xc, xs], axis=2), np.stack([-xs, xc], axis=2)], axis=0
    ).reshape(2 * modes, 2 * full_x)
    ix = np.stack(
        [np.concatenate([xc.T, -xs.T], axis=1), np.concatenate([xs.T, xc.T], axis=1)]
    ) / full_x
    ix = ix.reshape(2, full_x // 4, 4, 2 * modes).transpose(2, 0, 1, 3)
    ix = ix.reshape(2 * full_x, 2 * modes)
    return {"fz": fz, "iz": iz, "fy": fy, "iy": iy, "fx": fx, "ix": ix}


def split(value):
    high = value.astype(BF16)
    return high, (value - high.astype(F32)).astype(BF16)


def mm(a, b):
    return jnp.dot(a, b, preferred_element_type=F32)


def mm_nt(a, b):
    return lax.dot_general(a, b, (((1,), (1,)), ((), ())), preferred_element_type=F32)


def mm_tn(a, b):
    return lax.dot_general(a, b, (((0,), (0,)), ((), ())), preferred_element_type=F32)


def table_dot(high_ref, low_ref, data):
    high, low = split(data)
    return mm(high_ref[...], high) + mm(high_ref[...], low) + mm(low_ref[...], high)


def forward_z(
    cells_ref, th_ref, tl_ref, out_ref, first_ref, middle_ref, last_ref, held, ready, sems, done
):
    copies = []
    for half in range(2):
        for side in range(2):
            copy = pltpu.make_async_copy(
                cells_ref.at[:, pl.ds(8 * half, 8), pl.ds(128 * side, 128)],
                held.at[half, side],
                sems.at[half, side],
            )
            copy.start()
            copies.append(copy)
    both = jnp.concatenate([th_ref[...], tl_ref[...]], axis=0)
    results = []
    for half in range(2):
        for side in range(2):
            copies[2 * half + side].wait()
        sides = [held.at[half, side].reshape(1024, 128) for side in range(2)]
        for row in range(8):
            y = 8 * half + row
            parts = [
                jnp.concatenate(
                    [side[pl.ds(x * 8 + row, 32, stride=32), :] for side in sides], axis=1
                )
                for x in range(4)
            ]
            first_ref[y] = parts[0]
            middle_ref[0, y] = parts[1]
            middle_ref[1, y] = parts[2]
            last_ref[y] = parts[3]
            high, low = split(jnp.concatenate(parts, axis=0))
            wide = mm_nt(both, high)
            total = wide[:64] + wide[64:] + mm_nt(th_ref[...], low)
            ready[:, y] = total.reshape(8, 8, 128)
        result = pltpu.make_async_copy(
            ready.at[:, pl.ds(8 * half, 8)], out_ref.at[:, pl.ds(8 * half, 8)], done.at[half]
        )
        result.start()
        results.append(result)
    for result in results:
        result.wait()


def forward_y(data_ref, th_ref, tl_ref, out_ref):
    rows = data_ref.reshape(1024, 128)
    results = []
    for k in range(4):
        parts = [rows[pl.ds(2 * k + part, 128, stride=8), :] for part in range(2)]
        results.append(table_dot(th_ref, tl_ref, jnp.concatenate(parts, axis=0)))
    out = out_ref.reshape(256, 128)
    for x in range(4):
        tile = jnp.concatenate([r[:, 32 * x : 32 * x + 32] for r in results], axis=1)
        for part in range(2):
            out[pl.ds(2 * x + part, 32, stride=8), :] = tile[32 * part : 32 * part + 32]


def middle(data_ref, weight_ref, fh_ref, fl_ref, ih_ref, il_ref, out_ref):
    spec = table_dot(fh_ref, fl_ref, data_ref[...].reshape(256, 128))
    spec_re, spec_im = spec[:32], spec[32:]
    lane = lax.broadcasted_iota(jnp.int32, (32, 128), 1)
    group = lane - lax.rem(lane, 32)
    mixed_re = jnp.zeros((32, 128), F32)
    mixed_im = jnp.zeros((32, 128), F32)
    for c in range(32):
        index = group + c
        in_re = jnp.take_along_axis(spec_re, index, axis=1)
        in_im = jnp.take_along_axis(spec_im, index, axis=1)
        w_re, w_im = weight_ref[0, c], weight_ref[1, c]
        mixed_re = mixed_re + (in_re * w_re - in_im * w_im)
        mixed_im = mixed_im + (in_re * w_im + in_im * w_re)
    back = table_dot(ih_ref, il_ref, jnp.concatenate([mixed_re, mixed_im], axis=0))
    out = out_ref.reshape(256, 128)
    for k in range(4):
        tile = jnp.concatenate(
            [back[64 * x : 64 * x + 64, 32 * k : 32 * k + 32] for x in range(4)], axis=1
        )
        for part in range(2):
            out[pl.ds(2 * k + part, 32, stride=8), :] = tile[32 * part : 32 * part + 32]


def inverse_y(data_ref, th_ref, tl_ref, out_ref):
    rows = data_ref.reshape(256, 128)
    out = out_ref.reshape(1024, 128)
    for k in range(4):
        parts = [rows[pl.ds(2 * k + part, 32, stride=8), :] for part in range(2)]
        result = table_dot(th_ref, tl_ref, jnp.concatenate(parts, axis=0))
        for part in range(2):
            out[pl.ds(2 * k + part, 128, stride=8), :] = result[128 * part : 128 * part + 128]


def final(data_ref, low_ref, high_ref, th_ref, tl_ref, out_ref, held, sems):
    table = jnp.concatenate([th_ref[...], th_ref[...], tl_ref[...]], axis=0)
    copies = []
    for half in range(2):
        slots = [held.at[half, side] for side in range(2)]
        rows = [slot.reshape(1024, 128) for slot in slots]
        for y in range(8):
            high, low = split(data_ref[:, 8 * half + y].reshape(64, 128))
            stacked = jnp.concatenate([high, low, high], axis=0)
            spectral = mm_tn(stacked, table)
            for x in range(4):
                value = spectral[32 * x : 32 * x + 32] + (low_ref, high_ref)[half][x, y]
                value = jax.nn.gelu(value)
                for side in range(2):
                    rows[side][pl.ds(x * 8 + y, 32, stride=32), :] = value[
                        :, 128 * side : 128 * side + 128
                    ]
        for side in range(2):
            copy = pltpu.make_async_copy(
                slots[side],
                out_ref.at[:, pl.ds(8 * half, 8), pl.ds(128 * side, 128)],
                sems.at[half, side],
            )
            copy.start()
            copies.append(copy)
    for copy in copies:
        copy.wait()


def weights(data_ref, out_ref):
    rows = out_ref.reshape(2048, 128)

    def body(m, carry):
        for part in range(2):
            tile = jnp.concatenate(
                [data_ref[32 * part + m, 32 * k : 32 * k + 32, :] for k in range(4)], axis=1
            )
            rows[pl.ds(1024 * part + m, 32, stride=32), :] = tile
        return carry

    lax.fori_loop(0, 32, body, 0, unroll=4)


def rims(before_ref, first_ref, middle_ref, last_ref, after_ref, top_ref, bottom_ref, sems):
    rows = [before_ref, first_ref, middle_ref.at[0], middle_ref.at[1], last_ref, after_ref]
    copies = [
        pltpu.make_async_copy(row.at[y], out_ref.at[i], sems.at[side, i])
        for side, (out_ref, y) in enumerate(((bottom_ref, 0), (top_ref, 15)))
        for i, row in enumerate(rows)
    ]
    for copy in copies:
        copy.start()
    for copy in copies:
        copy.wait()


def shift_sum(sums):
    whole = [jnp.concatenate(pair, axis=1) for pair in sums]
    return whole[1] + pltpu.roll(whole[0], 1, 1) + pltpu.roll(whole[2], 255, 1)


def add_taps(sums, tap_ref, chans, first, load):
    cells = [load(slice(128 * side, 128 * side + 128)) for side in range(2)]
    for e in range(3):
        tap = tap_ref[first + e, chans, :]
        for side in range(2):
            term = tap * cells[side]
            old = sums[e][side]
            sums[e][side] = term if old is None else old + term


def own_lines(half, planes, tap_ref, ph_ref, pl_ref, bias_ref, out_ref):
    point = jnp.concatenate([ph_ref[...], pl_ref[...], ph_ref[...]], axis=1)
    bias = jnp.concatenate([bias_ref[...]] * 4, axis=0)

    def line(row, shifts):
        y = row + 8 * half
        data = jnp.concatenate([plane[y] for plane in planes], axis=0)
        high, low = split(data)
        value = mm(point, jnp.concatenate([high, high, low], axis=0)) + bias
        for tile in range(4):
            chans = slice(8 * tile, 8 * tile + 8)
            for x in range(4):
                sums = [[None, None] for _ in range(3)]
                for a in range(max(0, 1 - x), min(3, 5 - x)):
                    plane = planes[x + a - 1]
                    for b in shifts:
                        load = lambda lanes: plane[y + b - 1, chans, lanes]
                        add_taps(sums, tap_ref, chans, 9 * a + 3 * b, load)
                own = 32 * x + 8 * tile
                out_ref[x, row, chans, :] = value[own : own + 8] + shift_sum(sums)

    def body(row, carry):
        line(row, (0, 1, 2))
        return carry

    if half == 0:
        line(0, (1, 2))
        lax.fori_loop(1, 8, body, 0)
    else:
        lax.fori_loop(0, 7, body, 0)
        line(7, (0, 1))


def own_cells_low(
    first_ref, middle_ref, last_ref, dw_ref, ph_ref, pl_ref, bias_ref, out_ref, tap_ref
):
    for i in range(27):
        tap_ref[i] = jnp.broadcast_to(dw_ref[:, i : i + 1], (32, 128))
    planes = [first_ref, middle_ref.at[0], middle_ref.at[1], last_ref]
    own_lines(0, planes, tap_ref, ph_ref, pl_ref, bias_ref, out_ref)


def own_cells_high(
    first_ref, middle_ref, last_ref, tap_ref, ph_ref, pl_ref, bias_ref, out_ref
):
    planes = [first_ref, middle_ref.at[0], middle_ref.at[1], last_ref]
    own_lines(1, planes, tap_ref, ph_ref, pl_ref, bias_ref, out_ref)


def edge_cells(
    low_ref, high_ref, before_ref, after_ref, left_ref, right_ref, tap_ref, out_low_ref, out_high_ref
):
    for tile in range(4):
        chans = slice(8 * tile, 8 * tile + 8)
        for b, y, source, base_ref, out_ref in (
            (0, 0, left_ref, low_ref, out_low_ref),
            (2, 7, right_ref, high_ref, out_high_ref),
        ):
            for x in range(4):
                sums = [[None, None] for _ in range(3)]
                for a in range(max(0, 1 - x), min(3, 5 - x)):
                    load = lambda lanes: source[x + a, chans, lanes]
                    add_taps(sums, tap_ref, chans, 9 * a + 3 * b, load)
                out_ref[x, y, chans, :] = base_ref[x, y, chans, :] + shift_sum(sums)

    def line(out_ref, row, before_rows, after_rows):
        for a, x, rows in ((0, 0, before_rows), (2, 3, after_rows)):
            for tile in range(4):
                chans = slice(8 * tile, 8 * tile + 8)
                sums = [[None, None] for _ in range(3)]
                for b in range(3):
                    plane, at = rows[b]
                    load = lambda lanes: plane[at, chans, lanes]
                    add_taps(sums, tap_ref, chans, 9 * a + 3 * b, load)
                out_ref[x, row, chans, :] = out_ref[x, row, chans, :] + shift_sum(sums)

    def near_rows(plane, edge, y):
        low = (left_ref, edge) if y == 0 else (plane, y - 1)
        high = (right_ref, edge) if y == 15 else (plane, y + 1)
        return [low, (plane, y), high]

    for half, out_ref in enumerate((out_low_ref, out_high_ref)):

        def body(row, carry):
            y = row + 8 * half
            both = ([(plane, y + b - 1) for b in range(3)] for plane in (before_ref, after_ref))
            line(out_ref, row, *both)
            return carry

        lax.fori_loop(1 - half, 8 - half, body, 0)
        y = 15 * half
        line(out_ref, 7 * half, near_rows(before_ref, 0, y), near_rows(after_ref, 5, y))


VMEM = pl.BlockSpec(memory_space=pltpu.VMEM)
ANY = pl.BlockSpec(memory_space=pl.ANY)
HBM = pl.BlockSpec(memory_space=pltpu.HBM)


def call(body, shapes, inputs, microseconds=0, **kw):
    out_shape = [shape if kind is None else kind(shape, F32) for shape, kind in shapes]
    kw.setdefault("in_specs", [VMEM] * inputs)
    kw.setdefault("out_specs", [VMEM] * len(out_shape))
    kw["compiler_params"] = pltpu.CompilerParams(vmem_limit_bytes=16 * 2**20)
    kw["cost_estimate"] = pl.CostEstimate(
        flops=1_000_000_000 * microseconds, transcendentals=0, bytes_accessed=0
    )
    return pl.pallas_call(body, out_shape=out_shape, name=body.__name__, **kw)


def near(value):
    return pltpu.with_memory_space_constraint(value, pltpu.VMEM)


def after_all(value, *others):
    return lax.optimization_barrier((value, *others))[0]


def shifted(axis, value, step):
    count = lax.axis_size(axis)
    return lax.ppermute(value, axis, [(i, (i + step) % count) for i in range(count)])


def exchange(value, axis):
    return lax.all_to_all(value, axis, split_axis=0, concat_axis=0, tiled=True)


def on_device(field, spec_weight, dw_kernel, point_weight, bias):
    tab = {
        name: tuple(near(jnp.asarray(half)) for half in halves(value))
        for name, value in tables(32, 128, 128, 256).items()
    }
    plain, kept_near = jax.ShapeDtypeStruct, pltpu.VMEM
    dma = pltpu.SemaphoreType.DMA

    far = functools.partial(pltpu.with_memory_space_constraint, memory_space=pltpu.HBM)
    cells = far(field.reshape(128, 16, 256))
    zchunks, first, mid, last = call(
        forward_z,
        [
            ((8, 16, 8, 128), plain),
            ((16, 32, 256), kept_near),
            ((2, 16, 32, 256), kept_near),
            ((16, 32, 256), kept_near),
        ],
        3,
        in_specs=[HBM] + [VMEM] * 2,
        out_specs=[ANY] + [VMEM] * 3,
        scratch_shapes=[
            pltpu.VMEM((2, 2, 128, 8, 128), F32),
            pltpu.VMEM((8, 16, 8, 128), F32),
            dma((2, 2)),
            dma((2,)),
        ],
    )(cells, *tab["fz"])

    blocks = jnp.kron(jnp.eye(4, dtype=F32), point_weight.T)
    point_high = blocks.astype(BF16)
    point_low = (blocks - lax.reduce_precision(blocks, 8, 7)).astype(BF16)
    shared = (point_high, point_low, bias.reshape(32, 1))
    own_rows = tuple(near(rows) for rows in (first, mid, last))

    zall = exchange(zchunks, "gy")
    (packed,) = call(weights, [((2, 32, 32, 128), plain)], 1, 3)(
        near(after_all(spec_weight.reshape(64, 128, 32), zchunks))
    )
    base_low, taps = call(
        own_cells_low, [((4, 8, 32, 256), plain), ((27, 32, 128), plain)], 7, 3
    )(*own_rows, dw_kernel.reshape(32, 27), *shared)
    zall, packed, base_low = lax.optimization_barrier((zall, packed, base_low))
    (ychunks,) = call(forward_y, [((32, 8, 128), plain)], 3)(near(zall), *tab["fy"])

    yall = exchange(ychunks, "gx")
    first, last, taps, _ = lax.optimization_barrier((first, last, taps, ychunks))
    before = shifted("gx", last, 1)
    after = shifted("gx", first, -1)
    (base_high,) = call(own_cells_high, [((4, 8, 32, 256), plain)], 7, 8)(
        *own_rows, near(taps), *shared
    )
    yall, base_high = lax.optimization_barrier((yall, base_high))
    (xchunks,) = call(middle, [((32, 8, 128), plain)], 6)(
        near(yall), near(packed), *tab["fx"], *tab["ix"]
    )

    xall = exchange(xchunks, "gx")
    before, after, _ = lax.optimization_barrier((before, after, xchunks))
    top, bottom = call(
        rims,
        [((6, 32, 256), plain)] * 2,
        5,
        in_specs=[ANY] * 5,
        out_specs=[ANY] * 2,
        scratch_shapes=[dma((2, 6))],
    )(before, first, mid, last, after)
    left = shifted("gy", top, 1)
    right = shifted("gy", bottom, -1)
    xall, top, bottom = lax.optimization_barrier((xall, top, bottom))
    (back,) = call(inverse_y, [((8, 16, 8, 128), plain)], 3)(near(xall), *tab["iy"])

    ball = exchange(back, "gy")
    left, right, _ = lax.optimization_barrier((left, right, back))
    base_low, base_high = call(
        edge_cells,
        [((4, 8, 32, 256), kept_near)] * 2,
        7,
        40,
        input_output_aliases={0: 0, 1: 1},
    )(*(near(value) for value in (base_low, base_high, before, after, left, right, taps)))
    ball, base_low, base_high = lax.optimization_barrier((ball, base_low, base_high))
    (out,) = call(
        final,
        [((128, 16, 256), plain)],
        5,
        out_specs=[ANY],
        scratch_shapes=[pltpu.VMEM((2, 2, 128, 8, 128), F32), dma((2, 2))],
    )(near(ball), near(base_low), near(base_high), *tab["iz"])
    return out.reshape(field.shape)


def solution(mesh):
    placed = (P(None, "gx", "gy", None), P(None, None, "gx", "gy", None, None), P(), P(), P())
    return jax.shard_map(
        on_device, mesh=mesh, in_specs=placed, out_specs=P(None, "gx", "gy", None), check_vma=False
    )
```

time: 123 us -> 85.9 us (0.70)
  waiting for transfers between devices: 29.9 us -> 7.67 us
  Pallas kernels: 40.4 us -> 25.1 us
  local copies, waits for them, and re-layouts: 7.67 us -> 16.2 us
  starting transfers between devices: 43.2 us -> 35.4 us
    pallas_call x7 -> x10, Pallas kernels: 40.4 us -> 25.1 us  [the longest x1 5.18 us: on_device(): call(rims, [((6, 32, 256), plain)] * 2, 5, in_specs=[ANY] * 5, out_specs=...]
    ppermute x4, waiting for transfers between devices: 12.9 us -> 1.61 us  [shifted(): lax.ppermute(value, axis, [(i, (i + step) % count) for i in range(count)])]
    all_to_all x4, waiting for transfers between devices: 17 us -> 6.05 us  [exchange(): return lax.all_to_all(value, axis, split_axis=0, concat_axis=0, tiled=True)]
    unnamed x26 -> x62, local copies, waits for them, and re-layouts: 6.06 us -> 15.8 us
    all_to_all x4, starting transfers between devices: 37 us -> 28.5 us  [exchange(): return lax.all_to_all(value, axis, split_axis=0, concat_axis=0, tiled=True)]
  transfers between devices with their start and end apart: 8 -> 8, of which waited for: 4 -> 5; matrix products, arithmetic and copies ran while one was open for 4% -> 1% of each run, Pallas kernels for 25% -> 20%
where the time goes in v3:
time: 85.9 us; the launch traced here: 84.6 us
  starting transfers between devices  35.4 us (41%)
  Pallas kernels  25.1 us (29%)
  local copies, waits for them, and re-layouts  16.2 us (19%)
  waiting for transfers between devices  7.67 us (9%)
    all_to_all x4, starting transfers between devices, exchange(): return lax.all_to_all(value, axis, split_axis=0, concat_axis=0, tiled=True)  28.5 us
    unnamed x62, local copies, waits for them, and re-layouts  15.8 us
    ppermute x4, starting transfers between devices, shifted(): lax.ppermute(value, axis, [(i, (i + step) % count) for i in range(count)])  6.87 us
    all_to_all x4, waiting for transfers between devices, exchange(): return lax.all_to_all(value, axis, split_axis=0, concat_axis=0, tiled=True)  6.05 us
    pallas_call x1, Pallas kernels, on_device(): call(rims, [((6, 32, 256), plain)] * 2, 5, in_specs=[ANY] * 5, out_specs=...  5.18 us
    pallas_call x1, Pallas kernels, on_device(): call(forward_z, [((8, 16, 8, 128), plain), ((16, 32, 256), kept_near), ((...  3.77 us
    pallas_call x1, Pallas kernels, on_device(): call(edge_cells, [((4, 8, 32, 256), kept_near)] * 2, 7, 40, input_output_...  3.13 us
    pallas_call x1, Pallas kernels, on_device(): call(final, [((128, 16, 256), plain)], 5, out_specs=[ANY], scratch_shapes...  3.08 us
  transfers between devices with their start and end apart: 8, of which 5 were waited for; matrix products, arithmetic and copies ran while one was open for 1% of the time, Pallas kernels for 20%

profile of v3, /device:TPU:1, one launch (start us, length us, event | category | flops | bytes accessed | tf_op | source)
XLA Modules:
  0.0 84.6 jit_solution(11293296421213458024)
XLA Ops:
  0.0 0.8 copy-done.16
  0.8 0.8 copy-done.17
  1.5 3.8 %forward_z.1 = (f32[8,16,8,128]{3,2,1,0:T(8,128)}, f32[16,32,256]{2,1,0:T(8,128)S(1)}, f32[2,16,32,256]{3,2,1,0:T(8,128)S(1)}, f32[16,32,256]{2,1,0:T(8,128)S(1)}) custom-call(f32[128,16,256]{2,1,0:T(8,128)} %bitcast.8, bf16[64,256]{1,0:T(8,128)(2,1)S(1)} %copy-done.16, bf16[64,256]{1,0:T(8,128)(2,1)S(1)} %copy-done.17), custom_call_target="tpu_custom_call" | custom-call | tf_op jit(solution)/shard_map/forward_z/pallas_call | solution.py:373
  5.3 0.0 copy-start.6
  5.3 7.5 %all-to-all-start = ((f32[8,16,8,128]{3,2,1,0:T(8,128)}), f32[8,16,8,128]{3,2,1,0:T(8,128)S(1)}, u32[]{:S(2)}, u32[]{:S(2)}) async-start(f32[8,16,8,128]{3,2,1,0:T(8,128)} %get-tuple-element.32), calls=%async_computation | async-start | bytes 1048576 | tf_op jit(solution)/shard_map/all_to_all | solution.py:360
  12.8 0.0 copy-done.29
  12.8 0.1 copy.24
  12.9 0.1 broadcast_multiply_fusion
  13.0 0.2 mul.27
  13.2 0.0 copy-done.30
  13.2 0.1 copy.26.bias_ref
  13.3 0.0 copy-done.28
  13.3 0.1 copy.25.dw_ref
  13.4 0.0 copy-done.6
  13.4 2.2 %copy-done.22 = f32[2,32,1,4,32,32]{5,4,3,2,1,0:T(8,128)S(1)} copy-done((f32[2,32,1,4,32,32]{5,4,3,2,1,0:T(8,128)S(1)}, f32[2,32,1,4,32,32]{5,4,3,2,1,0:T(8,128)}, u32[]{:S(2)}) %copy-start.22) | copy-done | bytes 1048600
  15.6 1.9 %weights.1.weight_ref = f32[2,32,32,128]{3,2,1,0:T(8,128)S(1)} custom-call(f32[64,128,32]{2,1,0:T(8,128)S(1)} %bitcast.7), custom_call_target="tpu_custom_call" | custom-call | flops 3000000000 | tf_op jit(solution)/shard_map/weights/pallas_call | solution.py:399
  17.5 0.0 copy-done.7
  17.5 0.0 copy-start.20
  17.5 0.0 copy-start.21
  17.5 2.1 %own_cells_low.1 = (f32[4,8,32,256]{3,2,1,0:T(8,128)S(1)}, f32[27,32,128]{2,1,0:T(8,128)S(1)}) custom-call(f32[16,32,256]{2,1,0:T(8,128)S(1)} %get-tuple-element.44.first_ref, f32[2,16,32,256]{3,2,1,0:T(8,128)S(1)} %get-tuple-element.35.middle_ref, f32[16,32,256]{2,1,0:T(8,128)S(1)} %copy-done.7, f32[32,27]{1,0:T(8,128)S(1)} %copy.25.dw_ref, ...), custom_call_target="tpu_custom_call" | custom-call | flops 3000000000 | tf_op jit(solution)/shard_map/own_cells_low/pallas_call | solution.py:402
  19.6 0.0 copy-start
  19.6 1.0 %copy-done = f32[4,8,32,256]{3,2,1,0:T(8,128)} copy-done((f32[4,8,32,256]{3,2,1,0:T(8,128)}, f32[4,8,32,256]{3,2,1,0:T(8,128)S(1)}, u32[]{:S(2)}) %copy-start) | copy-done | bytes 1048600
  20.6 0.8 copy-done.25
  21.4 2.1 %all-to-all-done.data_ref = f32[8,16,8,128]{3,2,1,0:T(8,128)S(1)} async-done(((f32[8,16,8,128]{3,2,1,0:T(8,128)}), f32[8,16,8,128]{3,2,1,0:T(8,128)S(1)}, u32[]{:S(2)}, u32[]{:S(2)}) %all-to-all-start) | async-done | bytes 524320 | tf_op jit(solution)/shard_map/all_to_all | solution.py:360
  23.5 0.0 copy-done.20
  23.5 0.0 copy-done.21
  23.5 1.0 %forward_y.1 = f32[32,8,128]{2,1,0:T(8,128)} custom-call(f32[8,16,8,128]{3,2,1,0:T(8,128)S(1)} %all-to-all-done.data_ref, bf16[64,256]{1,0:T(8,128)(2,1)S(1)} %copy-done.20, bf16[64,256]{1,0:T(8,128)(2,1)S(1)} %copy-done.21), custom_call_target="tpu_custom_call" | custom-call | tf_op jit(solution)/shard_map/forward_y/pallas_call | solution.py:406
  24.5 10.5 %all-to-all-start.1 = ((f32[32,8,128]{2,1,0:T(8,128)}), f32[32,8,128]{2,1,0:T(8,128)S(1)}, u32[]{:S(2)}, u32[]{:S(2)}) async-start(f32[32,8,128]{2,1,0:T(8,128)} %forward_y.1), calls=%async_computation.1 | async-start | bytes 262144 | tf_op jit(solution)/shard_map/all_to_all | solution.py:360
  35.0 1.7 %collective-permute-start = (f32[16,32,256]{2,1,0:T(8,128)}, f32[16,32,256]{2,1,0:T(8,128)}, u32[]{:S(2)}, u32[]{:S(2)}) collective-permute-start(f32[16,32,256]{2,1,0:T(8,128)} %copy-done.6), channel_id=1, source_target_pairs={{0,8},{8,16},{16,24},{24,32},{32,40},{40,48},{48,56},{56,64},{64,7... | collective-permute-start | bytes 1572872 | tf_op jit(solution)/shard_map/ppermute | solution.py:356
  36.7 0.0 collective-permute-start.1
  36.8 1.1 %copy-done.8 = f32[16,32,256]{2,1,0:T(8,128)S(1)} copy-done((f32[16,32,256]{2,1,0:T(8,128)S(1)}, f32[16,32,256]{2,1,0:T(8,128)}, u32[]{:S(2)}) %copy-start.8) | copy-done | bytes 524312
  37.8 1.0 %copy-done.26 = f32[27,32,128]{2,1,0:T(8,128)S(1)} copy-done((f32[27,32,128]{2,1,0:T(8,128)S(1)}, f32[27,32,128]{2,1,0:T(8,128)}, u32[]{:S(2)}) %copy-start.26) | copy-done | bytes 442392
  38.8 1.9 %own_cells_high.1.high_ref = f32[4,8,32,256]{3,2,1,0:T(8,128)S(1)} custom-call(f32[16,32,256]{2,1,0:T(8,128)S(1)} %get-tuple-element.44.first_ref, f32[2,16,32,256]{3,2,1,0:T(8,128)S(1)} %get-tuple-element.35.middle_ref, f32[16,32,256]{2,1,0:T(8,128)S(1)} %copy-done.8, f32[27,32,128]{2,1,0:T(8,128)S(1)} %copy-done.26, ...), custom_call_target="tpu_custom_call" | custom-call | flops 8000000000 | tf_op jit(solution)/shard_map/own_cells_high/pallas_call | solution.py:412
  40.8 0.0 copy-start.2
  40.8 1.0 %copy-done.2 = f32[4,8,32,256]{3,2,1,0:T(8,128)} copy-done((f32[4,8,32,256]{3,2,1,0:T(8,128)}, f32[4,8,32,256]{3,2,1,0:T(8,128)S(1)}, u32[]{:S(2)}) %copy-start.2) | copy-done | bytes 1048600
  41.8 2.7 %all-to-all-done.1.data_ref = f32[32,8,128]{2,1,0:T(8,128)S(1)} async-done(((f32[32,8,128]{2,1,0:T(8,128)}), f32[32,8,128]{2,1,0:T(8,128)S(1)}, u32[]{:S(2)}, u32[]{:S(2)}) %all-to-all-start.1) | async-done | bytes 131104 | tf_op jit(solution)/shard_map/all_to_all | solution.py:360
  44.5 0.0 copy-done.12
  44.5 0.0 copy-done.13
  44.5 0.0 copy-done.18
  44.5 0.0 copy-done.19
  44.5 1.8 %middle.1 = f32[32,8,128]{2,1,0:T(8,128)} custom-call(f32[32,8,128]{2,1,0:T(8,128)S(1)} %all-to-all-done.1.data_ref, f32[2,32,32,128]{3,2,1,0:T(8,128)S(1)} %weights.1.weight_ref, bf16[64,256]{1,0:T(8,128)(2,1)S(1)} %copy-done.18, bf16[64,256]{1,0:T(8,128)(2,1)S(1)} %copy-done.19, bf16[256,64]{1,0:T(8,128)(2,1)S(1)} %copy-done.12, bf16[256,64]{1,0:T(8,128)(2,1)S(1)} %copy-done.13), custom_call_target="tpu_custom_call" | custom-call | tf_op jit(solution)/shard_map/middle/pallas_call | solution.py:416
  46.3 6.9 %all-to-all-start.2 = ((f32[32,8,128]{2,1,0:T(8,128)}), f32[32,8,128]{2,1,0:T(8,128)S(1)}, u32[]{:S(2)}, u32[]{:S(2)}) async-start(f32[32,8,128]{2,1,0:T(8,128)} %middle.1), calls=%async_computation.2 | async-start | bytes 262144 | tf_op jit(solution)/shard_map/all_to_all | solution.py:360
  53.2 0.0 copy-start.1
  53.2 0.0 collective-permute-done.before_ref
  53.2 0.0 collective-permute-done.1.after_ref
  53.3 1.1 %copy-done.9 = f32[16,32,256]{2,1,0:T(8,128)S(1)} copy-done((f32[16,32,256]{2,1,0:T(8,128)S(1)}, f32[16,32,256]{2,1,0:T(8,128)}, u32[]{:S(2)}) %copy-start.9) | copy-done | bytes 524312
  54.4 5.2 %rims.1 = (f32[6,32,256]{2,1,0:T(8,128)}, f32[6,32,256]{2,1,0:T(8,128)}) custom-call(f32[16,32,256]{2,1,0:T(8,128)} %collective-permute-done.before_ref, f32[16,32,256]{2,1,0:T(8,128)S(1)} %get-tuple-element.44.first_ref, f32[2,16,32,256]{3,2,1,0:T(8,128)S(1)} %get-tuple-element.35.middle_ref, f32[16,32,256]{2,1,0:T(8,128)S(1)} %copy-done.9, ...), custom_call_target="tpu_custom_call" | custom-call | tf_op jit(solution)/shard_map/rims/pallas_call | solution.py:422
  59.6 1.3 %collective-permute-start.2 = (f32[6,32,256]{2,1,0:T(8,128)}, f32[6,32,256]{2,1,0:T(8,128)S(1)}, u32[]{:S(2)}, u32[]{:S(2)}) collective-permute-start(f32[6,32,256]{2,1,0:T(8,128)} %get-tuple-element.47), channel_id=1, source_target_pairs={{0,1},{1,2},{2,3},{3,4},{4,5},{5,6},{6,7},{7,0},{8,9},{9,10},{10,1... | collective-permute-start | bytes 589832 | tf_op jit(solution)/shard_map/ppermute | solution.py:356
  60.8 3.9 %collective-permute-start.3 = (f32[6,32,256]{2,1,0:T(8,128)}, f32[6,32,256]{2,1,0:T(8,128)S(1)}, u32[]{:S(2)}, u32[]{:S(2)}) collective-permute-start(f32[6,32,256]{2,1,0:T(8,128)} %get-tuple-element.48), channel_id=1, source_target_pairs={{0,7},{1,0},{2,1},{3,2},{4,3},{5,4},{6,5},{7,6},{8,15},{9,8},{10,9... | collective-permute-start | bytes 589832 | tf_op jit(solution)/shard_map/ppermute | solution.py:356
  64.7 0.0 all-to-all-done.2.data_ref
  64.7 1.2 %inverse_y.1 = f32[8,16,8,128]{3,2,1,0:T(8,128)} custom-call(f32[32,8,128]{2,1,0:T(8,128)S(1)} %all-to-all-done.2.data_ref, bf16[256,64]{1,0:T(8,128)(2,1)S(1)} %copy-done.10, bf16[256,64]{1,0:T(8,128)(2,1)S(1)} %copy-done.11), custom_call_target="tpu_custom_call" | custom-call | tf_op jit(solution)/shard_map/inverse_y/pallas_call | solution.py:433
  65.9 3.6 %all-to-all-start.3 = ((f32[8,16,8,128]{3,2,1,0:T(8,128)}), f32[8,16,8,128]{3,2,1,0:T(8,128)S(1)}, u32[]{:S(2)}, u32[]{:S(2)}) async-start(f32[8,16,8,128]{3,2,1,0:T(8,128)} %inverse_y.1), calls=%async_computation.3 | async-start | bytes 1048576 | tf_op jit(solution)/shard_map/all_to_all | solution.py:360
  69.5 0.2 collective-permute-done.2.left_ref
  69.7 1.4 %collective-permute-done.3.right_ref = f32[6,32,256]{2,1,0:T(8,128)S(1)} collective-permute-done((f32[6,32,256]{2,1,0:T(8,128)}, f32[6,32,256]{2,1,0:T(8,128)S(1)}, u32[]{:S(2)}, u32[]{:S(2)}) %collective-permute-start.3) | collective-permute-done | bytes 196640 | tf_op jit(solution)/shard_map/ppermute | solution.py:356
  71.2 0.7 copy-done.23
  71.8 1.2 %copy-done.3 = f32[4,8,32,256]{3,2,1,0:T(8,128)S(1)} copy-done((f32[4,8,32,256]{3,2,1,0:T(8,128)S(1)}, f32[4,8,32,256]{3,2,1,0:T(8,128)}, u32[]{:S(2)}) %copy-start.3) | copy-done | bytes 1048600
  73.1 0.9 %copy-done.24 = f32[6,32,256]{2,1,0:T(8,128)S(1)} copy-done((f32[6,32,256]{2,1,0:T(8,128)S(1)}, f32[6,32,256]{2,1,0:T(8,128)}, u32[]{:S(2)}) %copy-start.24) | copy-done | bytes 196632
  74.0 1.0 %copy-done.27 = f32[27,32,128]{2,1,0:T(8,128)S(1)} copy-done((f32[27,32,128]{2,1,0:T(8,128)S(1)}, f32[27,32,128]{2,1,0:T(8,128)}, u32[]{:S(2)}) %copy-start.27) | copy-done | bytes 442392
  75.0 3.1 %edge_cells.1 = (f32[4,8,32,256]{3,2,1,0:T(8,128)S(1)}, f32[4,8,32,256]{3,2,1,0:T(8,128)S(1)}) custom-call(f32[4,8,32,256]{3,2,1,0:T(8,128)S(1)} %copy-done.1, f32[4,8,32,256]{3,2,1,0:T(8,128)S(1)} %copy-done.3, f32[16,32,256]{2,1,0:T(8,128)} %collective-permute-done.before_ref, ...), custom_call_target="tpu_custom_call", output_to_operand_aliasing={{0}: (0, {}), {1}: (1, {})} | custom-call | flops 40000000000 | tf_op jit(solution)/shard_map/edge_cells/pallas_call | solution.py:437
  78.1 0.0 copy-start.4
  78.1 1.0 %copy-done.4 = f32[4,8,32,256]{3,2,1,0:T(8,128)} copy-done((f32[4,8,32,256]{3,2,1,0:T(8,128)}, f32[4,8,32,256]{3,2,1,0:T(8,128)S(1)}, u32[]{:S(2)}) %copy-start.4) | copy-done | bytes 1048600
  79.1 1.2 %all-to-all-done.3.data_ref = f32[8,16,8,128]{3,2,1,0:T(8,128)S(1)} async-done(((f32[8,16,8,128]{3,2,1,0:T(8,128)}), f32[8,16,8,128]{3,2,1,0:T(8,128)S(1)}, u32[]{:S(2)}, u32[]{:S(2)}) %all-to-all-start.3) | async-done | bytes 524320 | tf_op jit(solution)/shard_map/all_to_all | solution.py:360
  80.3 1.2 %copy-done.5 = f32[4,8,32,256]{3,2,1,0:T(8,128)S(1)} copy-done((f32[4,8,32,256]{3,2,1,0:T(8,128)S(1)}, f32[4,8,32,256]{3,2,1,0:T(8,128)}, u32[]{:S(2)}) %copy-start.5) | copy-done | bytes 1048600
  81.6 3.1 %final.1 = f32[128,16,256]{2,1,0:T(8,128)} custom-call(f32[8,16,8,128]{3,2,1,0:T(8,128)S(1)} %all-to-all-done.3.data_ref, f32[4,8,32,256]{3,2,1,0:T(8,128)S(1)} %get-tuple-element.57.low_ref, f32[4,8,32,256]{3,2,1,0:T(8,128)S(1)} %copy-done.5, bf16[64,256]{1,0:T(8,128)(2,1)S(1)} %copy-done.14, bf16[64,256]{1,0:T(8,128)(2,1)S(1)} %copy-done.15), custom_call_target="tpu_custom_call" | custom-call | tf_op jit(solution)/shard_map/final/pallas_call | solution.py:445
  (32 shorter events, 0.1 us)
Async XLA Ops:
  0.0 13.2 %copy-start.30 = (f32[32]{0:T(128)S(1)}, f32[32]{0:T(128)}, u32[]{:S(2)}) copy-start(f32[32]{0:T(128)} %param.21) | copy-start | bytes 388
  0.0 0.8 copy-start.16
  0.8 0.8 copy-start.17
  1.5 11.3 %copy-start.29 = (f32[32,32]{1,0:T(8,128)S(1)}, f32[32,32]{1,0:T(8,128)}, u32[]{:S(2)}) copy-start(f32[32,32]{1,0:T(8,128)} %param.20) | copy-start | bytes 12292
  1.5 11.8 %copy-start.28 = (f32[32,3,3,3]{0,3,2,1:T(4,128)S(1)}, f32[32,3,3,3]{0,3,2,1:T(4,128)}, u32[]{:S(2)}) copy-start(f32[32,3,3,3]{0,3,2,1:T(4,128)} %param.19) | copy-start | bytes 10372
  5.3 8.1 %copy-start.6 = (f32[16,32,256]{2,1,0:T(8,128)}, f32[16,32,256]{2,1,0:T(8,128)S(1)}, u32[]{:S(2)}) copy-start(f32[16,32,256]{2,1,0:T(8,128)S(1)} %get-tuple-element.43.last_ref) | copy-start | bytes 1572868
  5.3 18.2 %all-to-all-start = ((f32[8,16,8,128]{3,2,1,0:T(8,128)}), f32[8,16,8,128]{3,2,1,0:T(8,128)S(1)}, u32[]{:S(2)}, u32[]{:S(2)}) async-start(f32[8,16,8,128]{3,2,1,0:T(8,128)} %get-tuple-element.32), calls=%async_computation | async-start | bytes 1048576 | tf_op jit(solution)/shard_map/all_to_all | solution.py:360
  13.4 2.2 %copy-start.22 = (f32[2,32,1,4,32,32]{5,4,3,2,1,0:T(8,128)S(1)}, f32[2,32,1,4,32,32]{5,4,3,2,1,0:T(8,128)}, u32[]{:S(2)}) copy-start(f32[2,32,1,4,32,32]{5,4,3,2,1,0:T(8,128)} %param.18) | copy-start | bytes 3145732
  15.6 1.9 %copy-start.7 = (f32[16,32,256]{2,1,0:T(8,128)S(1)}, f32[16,32,256]{2,1,0:T(8,128)}, u32[]{:S(2)}) copy-start(f32[16,32,256]{2,1,0:T(8,128)} %copy-done.6) | copy-start | bytes 1572868
  17.5 6.0 %copy-start.20 = (bf16[64,256]{1,0:T(8,128)(2,1)S(1)}, bf16[64,256]{1,0:T(8,128)(2,1)}, u32[]{:S(2)}) copy-start(bf16[64,256]{1,0:T(8,128)(2,1)} %constant.28.clone.th_ref) | copy-start | bytes 98308
  17.5 6.0 %copy-start.21 = (bf16[64,256]{1,0:T(8,128)(2,1)S(1)}, bf16[64,256]{1,0:T(8,128)(2,1)}, u32[]{:S(2)}) copy-start(bf16[64,256]{1,0:T(8,128)(2,1)} %constant.29.clone.tl_ref) | copy-start | bytes 98308
  19.6 1.0 %copy-start = (f32[4,8,32,256]{3,2,1,0:T(8,128)}, f32[4,8,32,256]{3,2,1,0:T(8,128)S(1)}, u32[]{:S(2)}) copy-start(f32[4,8,32,256]{3,2,1,0:T(8,128)S(1)} %get-tuple-element.50.low_ref) | copy-start | bytes 3145732
  20.6 0.8 copy-start.25
  24.5 20.0 %all-to-all-start.1 = ((f32[32,8,128]{2,1,0:T(8,128)}), f32[32,8,128]{2,1,0:T(8,128)S(1)}, u32[]{:S(2)}, u32[]{:S(2)}) async-start(f32[32,8,128]{2,1,0:T(8,128)} %forward_y.1), calls=%async_computation.1 | async-start | bytes 262144 | tf_op jit(solution)/shard_map/all_to_all | solution.py:360
  35.0 18.2 %collective-permute-start = (f32[16,32,256]{2,1,0:T(8,128)}, f32[16,32,256]{2,1,0:T(8,128)}, u32[]{:S(2)}, u32[]{:S(2)}) collective-permute-start(f32[16,32,256]{2,1,0:T(8,128)} %copy-done.6), channel_id=1, source_target_pairs={{0,8},{8,16},{16,24},{24,32},{32,40},{40,48},{48,56},{56,64},{64,7... | collective-permute-start | bytes 1572872 | tf_op jit(solution)/shard_map/ppermute | solution.py:356
  36.7 16.5 %collective-permute-start.1 = (f32[16,32,256]{2,1,0:T(8,128)S(1)}, f32[16,32,256]{2,1,0:T(8,128)}, u32[]{:S(2)}, u32[]{:S(2)}) collective-permute-start(f32[16,32,256]{2,1,0:T(8,128)S(1)} %get-tuple-element.44.first_ref), channel_id=1, source_target_pairs={{0,248},{8,0},{16,8},{24,16},{32,24},{40,32},{48,40},{56,48},{64,5... | collective-permute-start | bytes 1572872 | tf_op jit(solution)/shard_map/ppermute | solution.py:356
  36.8 1.1 %copy-start.8 = (f32[16,32,256]{2,1,0:T(8,128)S(1)}, f32[16,32,256]{2,1,0:T(8,128)}, u32[]{:S(2)}) copy-start(f32[16,32,256]{2,1,0:T(8,128)} %copy-done.6) | copy-start | bytes 1572868
  37.8 1.0 %copy-start.26 = (f32[27,32,128]{2,1,0:T(8,128)S(1)}, f32[27,32,128]{2,1,0:T(8,128)}, u32[]{:S(2)}) copy-start(f32[27,32,128]{2,1,0:T(8,128)} %copy-done.25) | copy-start | bytes 1327108
  38.8 5.7 %copy-start.12 = (bf16[256,64]{1,0:T(8,128)(2,1)S(1)}, bf16[256,64]{1,0:T(8,128)(2,1)}, u32[]{:S(2)}) copy-start(bf16[256,64]{1,0:T(8,128)(2,1)} %constant.34.clone.ih_ref) | copy-start | bytes 98308
  38.8 5.7 %copy-start.13 = (bf16[256,64]{1,0:T(8,128)(2,1)S(1)}, bf16[256,64]{1,0:T(8,128)(2,1)}, u32[]{:S(2)}) copy-start(bf16[256,64]{1,0:T(8,128)(2,1)} %constant.35.clone.il_ref) | copy-start | bytes 98308
  38.8 5.7 %copy-start.18 = (bf16[64,256]{1,0:T(8,128)(2,1)S(1)}, bf16[64,256]{1,0:T(8,128)(2,1)}, u32[]{:S(2)}) copy-start(bf16[64,256]{1,0:T(8,128)(2,1)} %constant.32.clone.fh_ref) | copy-start | bytes 98308
  38.8 5.7 %copy-start.19 = (bf16[64,256]{1,0:T(8,128)(2,1)S(1)}, bf16[64,256]{1,0:T(8,128)(2,1)}, u32[]{:S(2)}) copy-start(bf16[64,256]{1,0:T(8,128)(2,1)} %constant.33.clone.fl_ref) | copy-start | bytes 98308
  40.8 1.0 %copy-start.2 = (f32[4,8,32,256]{3,2,1,0:T(8,128)}, f32[4,8,32,256]{3,2,1,0:T(8,128)S(1)}, u32[]{:S(2)}) copy-start(f32[4,8,32,256]{3,2,1,0:T(8,128)S(1)} %own_cells_high.1.high_ref) | copy-start | bytes 3145732
  41.8 22.9 %copy-start.10 = (bf16[256,64]{1,0:T(8,128)(2,1)S(1)}, bf16[256,64]{1,0:T(8,128)(2,1)}, u32[]{:S(2)}) copy-start(bf16[256,64]{1,0:T(8,128)(2,1)} %constant.30.clone.th_ref) | copy-start | bytes 98308
  41.8 22.9 %copy-start.11 = (bf16[256,64]{1,0:T(8,128)(2,1)S(1)}, bf16[256,64]{1,0:T(8,128)(2,1)}, u32[]{:S(2)}) copy-start(bf16[256,64]{1,0:T(8,128)(2,1)} %constant.31.clone.tl_ref) | copy-start | bytes 98308
  46.3 18.4 %all-to-all-start.2 = ((f32[32,8,128]{2,1,0:T(8,128)}), f32[32,8,128]{2,1,0:T(8,128)S(1)}, u32[]{:S(2)}, u32[]{:S(2)}) async-start(f32[32,8,128]{2,1,0:T(8,128)} %middle.1), calls=%async_computation.2 | async-start | bytes 262144 | tf_op jit(solution)/shard_map/all_to_all | solution.py:360
  53.2 18.6 %copy-start.1 = (f32[4,8,32,256]{3,2,1,0:T(8,128)S(1)}, f32[4,8,32,256]{3,2,1,0:T(8,128)}, u32[]{:S(2)}) copy-start(f32[4,8,32,256]{3,2,1,0:T(8,128)} %copy-done) | copy-start | bytes 3145732
  53.2 1.1 %copy-start.9 = (f32[16,32,256]{2,1,0:T(8,128)S(1)}, f32[16,32,256]{2,1,0:T(8,128)}, u32[]{:S(2)}) copy-start(f32[16,32,256]{2,1,0:T(8,128)} %copy-done.6) | copy-start | bytes 1572868
  59.6 10.2 %collective-permute-start.2 = (f32[6,32,256]{2,1,0:T(8,128)}, f32[6,32,256]{2,1,0:T(8,128)S(1)}, u32[]{:S(2)}, u32[]{:S(2)}) collective-permute-start(f32[6,32,256]{2,1,0:T(8,128)} %get-tuple-element.47), channel_id=1, source_target_pairs={{0,1},{1,2},{2,3},{3,4},{4,5},{5,6},{6,7},{7,0},{8,9},{9,10},{10,1... | collective-permute-start | bytes 589832 | tf_op jit(solution)/shard_map/ppermute | solution.py:356
  60.8 10.3 %collective-permute-start.3 = (f32[6,32,256]{2,1,0:T(8,128)}, f32[6,32,256]{2,1,0:T(8,128)S(1)}, u32[]{:S(2)}, u32[]{:S(2)}) collective-permute-start(f32[6,32,256]{2,1,0:T(8,128)} %get-tuple-element.48), channel_id=1, source_target_pairs={{0,7},{1,0},{2,1},{3,2},{4,3},{5,4},{6,5},{7,6},{8,15},{9,8},{10,9... | collective-permute-start | bytes 589832 | tf_op jit(solution)/shard_map/ppermute | solution.py:356
  65.9 14.4 %copy-start.14 = (bf16[64,256]{1,0:T(8,128)(2,1)S(1)}, bf16[64,256]{1,0:T(8,128)(2,1)}, u32[]{:S(2)}) copy-start(bf16[64,256]{1,0:T(8,128)(2,1)} %constant.26.clone.th_ref) | copy-start | bytes 98308
  65.9 14.4 %copy-start.15 = (bf16[64,256]{1,0:T(8,128)(2,1)S(1)}, bf16[64,256]{1,0:T(8,128)(2,1)}, u32[]{:S(2)}) copy-start(bf16[64,256]{1,0:T(8,128)(2,1)} %constant.27.clone.tl_ref) | copy-start | bytes 98308
  65.9 14.4 %all-to-all-start.3 = ((f32[8,16,8,128]{3,2,1,0:T(8,128)}), f32[8,16,8,128]{3,2,1,0:T(8,128)S(1)}, u32[]{:S(2)}, u32[]{:S(2)}) async-start(f32[8,16,8,128]{3,2,1,0:T(8,128)} %inverse_y.1), calls=%async_computation.3 | async-start | bytes 1048576 | tf_op jit(solution)/shard_map/all_to_all | solution.py:360
  71.2 0.7 copy-start.23
  71.8 1.2 %copy-start.3 = (f32[4,8,32,256]{3,2,1,0:T(8,128)S(1)}, f32[4,8,32,256]{3,2,1,0:T(8,128)}, u32[]{:S(2)}) copy-start(f32[4,8,32,256]{3,2,1,0:T(8,128)} %copy-done.2) | copy-start | bytes 3145732
  73.1 0.9 %copy-start.24 = (f32[6,32,256]{2,1,0:T(8,128)S(1)}, f32[6,32,256]{2,1,0:T(8,128)}, u32[]{:S(2)}) copy-start(f32[6,32,256]{2,1,0:T(8,128)} %copy-done.23) | copy-start | bytes 589828
  74.0 1.0 %copy-start.27 = (f32[27,32,128]{2,1,0:T(8,128)S(1)}, f32[27,32,128]{2,1,0:T(8,128)}, u32[]{:S(2)}) copy-start(f32[27,32,128]{2,1,0:T(8,128)} %copy-done.25) | copy-start | bytes 1327108
  78.1 1.0 %copy-start.4 = (f32[4,8,32,256]{3,2,1,0:T(8,128)}, f32[4,8,32,256]{3,2,1,0:T(8,128)S(1)}, u32[]{:S(2)}) copy-start(f32[4,8,32,256]{3,2,1,0:T(8,128)S(1)} %get-tuple-element.58.high_ref) | copy-start | bytes 3145732
  80.3 1.2 %copy-start.5 = (f32[4,8,32,256]{3,2,1,0:T(8,128)S(1)}, f32[4,8,32,256]{3,2,1,0:T(8,128)}, u32[]{:S(2)}) copy-start(f32[4,8,32,256]{3,2,1,0:T(8,128)} %copy-done.4) | copy-start | bytes 3145732

commit v4 on v3

v4 whole, which is shorter than its diff:
```python
import functools

import jax
import jax.numpy as jnp
import numpy as np
from jax import lax
from jax.experimental import pallas as pl
from jax.experimental.pallas import tpu as pltpu
from jax.sharding import PartitionSpec as P

F32 = jnp.float32
BF16 = jnp.bfloat16


def halves(table):
    high = np.asarray(table, np.float32).astype(BF16)
    low = (np.asarray(table, np.float64) - high.astype(np.float64)).astype(BF16)
    return high, low


def kept(modes, length):
    index = np.arange(modes)
    return np.where(index < modes // 2, index, index + length - modes)


def angles(freqs, length):
    product = np.outer(freqs, np.arange(length)) % length
    turn = 2.0 * np.pi * product / length
    return np.cos(turn), np.sin(turn)


def tables(modes, full_x, full_y, depth):
    zc, zs = angles(np.arange(modes), depth)
    fz = np.stack([zc, -zs], axis=1).reshape(2 * modes, depth)
    weight = np.where(np.arange(modes) == 0, 1.0, 2.0)[:, None] / depth
    iz = np.stack([weight * zc, -weight * zs], axis=1).reshape(2 * modes, depth)
    yc, ys = angles(kept(modes, full_y), full_y)
    fy = np.block([[yc, ys], [-ys, yc]])
    iy = np.block([[yc.T, -ys.T], [ys.T, yc.T]]) / full_y
    xc, xs = angles(kept(modes, full_x), full_x)
    fx = np.concatenate(
        [np.stack([xc, xs], axis=2), np.stack([-xs, xc], axis=2)], axis=0
    ).reshape(2 * modes, 2 * full_x)
    ix = np.stack(
        [np.concatenate([xc.T, -xs.T], axis=1), np.concatenate([xs.T, xc.T], axis=1)]
    ) / full_x
    ix = ix.reshape(2, full_x // 4, 4, 2 * modes).transpose(2, 0, 1, 3)
    ix = ix.reshape(2 * full_x, 2 * modes)
    return {"fz": fz, "iz": iz, "fy": fy, "iy": iy, "fx": fx, "ix": ix}


def split(value):
    high = value.astype(BF16)
    return high, (value - high.astype(F32)).astype(BF16)


def mm(a, b):
    return jnp.dot(a, b, preferred_element_type=F32)


def mm_nt(a, b):
    return lax.dot_general(a, b, (((1,), (1,)), ((), ())), preferred_element_type=F32)


def mm_tn(a, b):
    return lax.dot_general(a, b, (((0,), (0,)), ((), ())), preferred_element_type=F32)


def table_dot(table_ref, data):
    high, low = split(data)
    return mm(table_ref[0], high) + mm(table_ref[0], low) + mm(table_ref[1], high)


def field_copies(cells_ref, held, sems):
    return [
        [
            pltpu.make_async_copy(
                cells_ref.at[:, pl.ds(8 * half, 8), pl.ds(128 * side, 128)],
                held.at[half, side],
                sems.at[half, side],
            )
            for side in range(2)
        ]
        for half in range(2)
    ]


def field_rows(held, y):
    sides = [held.at[y // 8, side].reshape(1024, 128) for side in range(2)]
    return [
        jnp.concatenate(
            [side[pl.ds(x * 8 + y % 8, 32, stride=32), :] for side in sides], axis=1
        )
        for x in range(4)
    ]


def start_all(copies):
    for copy in copies:
        copy.start()


def wait_all(copies):
    for copy in copies:
        copy.wait()


def forward_z(
    cells_ref, table_ref, out_ref, first_ref, last_ref, held, both, ready, firsts, lasts, sems, done
):
    load = pltpu.make_async_copy(table_ref, both, done.at[6])
    load.start()
    copies = field_copies(cells_ref, held, sems)
    start_all(copies[0] + copies[1])
    load.wait()
    results = []
    for half in range(2):
        wait_all(copies[half])
        span = pl.ds(8 * half, 8)
        for y in range(8 * half, 8 * half + 8):
            parts = field_rows(held, y)
            firsts[y] = parts[0]
            lasts[y] = parts[3]
            high, low = split(jnp.concatenate(parts, axis=0))
            wide = mm_nt(both[...], high)
            total = wide[:64] + wide[64:] + mm_nt(both[:64], low)
            ready[:, y] = total.reshape(8, 8, 128)
        moves = [
            (ready.at[:, span], out_ref.at[:, span]),
            (firsts.at[span], first_ref.at[span]),
            (lasts.at[span], last_ref.at[span]),
        ]
        for i, (src, dst) in enumerate(moves):
            results.append(pltpu.make_async_copy(src, dst, done.at[3 * half + i]))
            results[-1].start()
    wait_all(results)


def forward_y(data_ref, table_ref, out_ref):
    rows = data_ref.reshape(1024, 128)
    results = []
    for k in range(4):
        parts = [rows[pl.ds(2 * k + part, 128, stride=8), :] for part in range(2)]
        results.append(table_dot(table_ref, jnp.concatenate(parts, axis=0)))
    out = out_ref.reshape(256, 128)
    for x in range(4):
        tile = jnp.concatenate([r[:, 32 * x : 32 * x + 32] for r in results], axis=1)
        for part in range(2):
            out[pl.ds(2 * x + part, 32, stride=8), :] = tile[32 * part : 32 * part + 32]


def middle(data_ref, weight_ref, forward_ref, inverse_hbm, out_ref, inverse_ref, sem):
    load = pltpu.make_async_copy(inverse_hbm, inverse_ref, sem)
    load.start()
    spec = table_dot(forward_ref, data_ref[...].reshape(256, 128))
    spec_re, spec_im = spec[:32], spec[32:]
    lane = lax.broadcasted_iota(jnp.int32, (32, 128), 1)
    group = lane - lax.rem(lane, 32)
    mixed_re = jnp.zeros((32, 128), F32)
    mixed_im = jnp.zeros((32, 128), F32)
    for c in range(32):
        index = group + c
        in_re = jnp.take_along_axis(spec_re, index, axis=1)
        in_im = jnp.take_along_axis(spec_im, index, axis=1)
        w_re, w_im = weight_ref[0, c], weight_ref[1, c]
        mixed_re = mixed_re + (in_re * w_re - in_im * w_im)
        mixed_im = mixed_im + (in_re * w_im + in_im * w_re)
    load.wait()
    back = table_dot(inverse_ref, jnp.concatenate([mixed_re, mixed_im], axis=0))
    out = out_ref.reshape(256, 128)
    for k in range(4):
        tile = jnp.concatenate(
            [back[64 * x : 64 * x + 64, 32 * k : 32 * k + 32] for x in range(4)], axis=1
        )
        for part in range(2):
            out[pl.ds(2 * k + part, 32, stride=8), :] = tile[32 * part : 32 * part + 32]


def inverse_y(data_ref, table_ref, out_ref):
    rows = data_ref.reshape(256, 128)
    out = out_ref.reshape(1024, 128)
    for k in range(4):
        parts = [rows[pl.ds(2 * k + part, 32, stride=8), :] for part in range(2)]
        result = table_dot(table_ref, jnp.concatenate(parts, axis=0))
        for part in range(2):
            out[pl.ds(2 * k + part, 128, stride=8), :] = result[128 * part : 128 * part + 128]


def final(data_ref, base_ref, table_ref, out_ref, held, sems):
    table = jnp.concatenate([table_ref[0], table_ref[0], table_ref[1]], axis=0)
    copies = []
    for half in range(2):
        slots = [held.at[half, side] for side in range(2)]
        rows = [slot.reshape(1024, 128) for slot in slots]
        for y in range(8):
            high, low = split(data_ref[:, 8 * half + y].reshape(64, 128))
            stacked = jnp.concatenate([high, low, high], axis=0)
            spectral = mm_tn(stacked, table)
            for x in range(4):
                value = spectral[32 * x : 32 * x + 32] + base_ref[x, 8 * half + y]
                value = jax.nn.gelu(value)
                for side in range(2):
                    rows[side][pl.ds(x * 8 + y, 32, stride=32), :] = value[
                        :, 128 * side : 128 * side + 128
                    ]
        for side in range(2):
            copy = pltpu.make_async_copy(
                slots[side],
                out_ref.at[:, pl.ds(8 * half, 8), pl.ds(128 * side, 128)],
                sems.at[half, side],
            )
            copy.start()
            copies.append(copy)
    for copy in copies:
        copy.wait()


def weights(data_ref, out_ref, held, sems):
    copies = [
        pltpu.make_async_copy(
            data_ref.at[:, pl.ds(4 * i, 4)], held.at[:, pl.ds(4 * i, 4)], sems.at[i]
        )
        for i in range(8)
    ]
    for copy in copies:
        copy.start()
    rows = out_ref.reshape(2048, 128)
    for i in range(8):
        copies[i].wait()
        for m in range(4 * i, 4 * i + 4):
            for part in range(2):
                tile = jnp.concatenate(
                    [held[part, m, 32 * k : 32 * k + 32, :] for k in range(4)], axis=1
                )
                rows[pl.ds(1024 * part + m, 32, stride=32), :] = tile


def rims(rows_ref, before_ref, after_ref, top_ref, bottom_ref, sems):
    copies = []
    for side, out_ref in enumerate((bottom_ref, top_ref)):
        moves = [
            (rows_ref.at[side], out_ref.at[pl.ds(1, 4)]),
            (before_ref.at[15 * side], out_ref.at[0]),
            (after_ref.at[15 * side], out_ref.at[5]),
        ]
        copies += [
            pltpu.make_async_copy(src, dst, sems.at[side, i]) for i, (src, dst) in enumerate(moves)
        ]
    start_all(copies)
    wait_all(copies)


def shift_sum(sums):
    whole = [jnp.concatenate(pair, axis=1) for pair in sums]
    return whole[1] + pltpu.roll(whole[0], 1, 1) + pltpu.roll(whole[2], 255, 1)


def add_taps(sums, tap_ref, chans, first, load):
    cells = [load(slice(128 * side, 128 * side + 128)) for side in range(2)]
    for e in range(3):
        tap = tap_ref[first + e, chans, :]
        for side in range(2):
            term = tap * cells[side]
            old = sums[e][side]
            sums[e][side] = term if old is None else old + term


def spread_taps(dw_ref, tap_ref):
    rows = jnp.concatenate([dw_ref[a, b] for a in range(3) for b in range(3)], axis=0)
    columns = rows.T
    for i in range(27):
        tap_ref[i] = jnp.broadcast_to(columns[:, i : i + 1], (32, 128))


def own_cells(
    cells_ref, dw_ref, point_ref, bias_ref, out_ref, rim_ref, held, planes, tap_ref, sems
):
    copies = field_copies(cells_ref, held, sems)
    start_all(copies[0] + copies[1])
    spread_taps(dw_ref, tap_ref)
    channel_map = jnp.concatenate([jnp.concatenate([point_ref[...].T] * 4, axis=1)] * 4, axis=0)
    row = lax.broadcasted_iota(jnp.int32, (128, 128), 0)
    column = lax.broadcasted_iota(jnp.int32, (128, 128), 1)
    same = lax.div(row, 32) == lax.div(column, 32)
    high, low = split(jnp.where(same, channel_map, 0.0))
    point = jnp.concatenate([high, low, high], axis=1)
    bias = jnp.broadcast_to(bias_ref[...], (32, 32)).T[:, :1]
    bias = jnp.concatenate([bias] * 4, axis=0)
    for half in range(2):
        wait_all(copies[half])
        for y in range(8 * half, 8 * half + 8):
            parts = field_rows(held, y)
            for x in range(4):
                planes[x, y] = parts[x]
                if y % 15 == 0:
                    rim_ref[half, x] = parts[x]

    def line(y, shifts):
        high, low = split(planes[:, y].reshape(128, 256))
        value = mm(point, jnp.concatenate([high, high, low], axis=0)) + bias
        for tile in range(4):
            chans = slice(8 * tile, 8 * tile + 8)
            for x in range(4):
                sums = [[None, None] for _ in range(3)]
                for a in range(max(0, 1 - x), min(3, 5 - x)):
                    for b in shifts:
                        load = lambda lanes: planes[x + a - 1, y + b - 1, chans, lanes]
                        add_taps(sums, tap_ref, chans, 9 * a + 3 * b, load)
                own = 32 * x + 8 * tile
                out_ref[x, y, chans, :] = value[own : own + 8] + shift_sum(sums)

    def body(y, carry):
        line(y, (0, 1, 2))
        return carry

    line(0, (1, 2))
    lax.fori_loop(1, 15, body, 0)
    line(15, (0, 1))


def edge_cells(
    base_ref, before_hbm, after_hbm, left_hbm, right_hbm, dw_ref,
    out_ref, before_ref, after_ref, left_ref, right_ref, tap_ref, sems
):
    moves = [
        (left_hbm, left_ref), (right_hbm, right_ref), (before_hbm, before_ref), (after_hbm, after_ref)
    ]
    copies = [
        pltpu.make_async_copy(src, dst, sems.at[i]) for i, (src, dst) in enumerate(moves)
    ]
    for copy in copies:
        copy.start()
    spread_taps(dw_ref, tap_ref)
    for i, (b, y, source) in enumerate(((0, 0, left_ref), (2, 15, right_ref))):
        copies[i].wait()
        for tile in range(4):
            chans = slice(8 * tile, 8 * tile + 8)
            for x in range(4):
                sums = [[None, None] for _ in range(3)]
                for a in range(max(0, 1 - x), min(3, 5 - x)):
                    load = lambda lanes: source[x + a, chans, lanes]
                    add_taps(sums, tap_ref, chans, 9 * a + 3 * b, load)
                out_ref[x, y, chans, :] = base_ref[x, y, chans, :] + shift_sum(sums)
    copies[2].wait()
    copies[3].wait()

    def line(y, before_rows, after_rows):
        for a, x, rows in ((0, 0, before_rows), (2, 3, after_rows)):
            for tile in range(4):
                chans = slice(8 * tile, 8 * tile + 8)
                sums = [[None, None] for _ in range(3)]
                for b in range(3):
                    plane, at = rows[b]
                    load = lambda lanes: plane[at, chans, lanes]
                    add_taps(sums, tap_ref, chans, 9 * a + 3 * b, load)
                out_ref[x, y, chans, :] = out_ref[x, y, chans, :] + shift_sum(sums)

    def near_rows(plane, edge, y):
        low = (left_ref, edge) if y == 0 else (plane, y - 1)
        high = (right_ref, edge) if y == 15 else (plane, y + 1)
        return [low, (plane, y), high]

    def body(y, carry):
        line(y, *([(plane, y + b - 1) for b in range(3)] for plane in (before_ref, after_ref)))
        return carry

    lax.fori_loop(1, 15, body, 0, unroll=2)
    for y in (0, 15):
        line(y, near_rows(before_ref, 0, y), near_rows(after_ref, 5, y))


VMEM = pl.BlockSpec(memory_space=pltpu.VMEM)
ANY = pl.BlockSpec(memory_space=pl.ANY)
HBM = pl.BlockSpec(memory_space=pltpu.HBM)


def call(body, shapes, inputs, microseconds=0, **kw):
    out_shape = [shape if kind is None else kind(shape, F32) for shape, kind in shapes]
    kw.setdefault("in_specs", [VMEM] * inputs)
    kw.setdefault("out_specs", [VMEM] * len(out_shape))
    kw["compiler_params"] = pltpu.CompilerParams(vmem_limit_bytes=16 * 2**20)
    kw["cost_estimate"] = pl.CostEstimate(
        flops=1_000_000_000 * microseconds, transcendentals=0, bytes_accessed=0
    )
    return pl.pallas_call(body, out_shape=out_shape, name=body.__name__, **kw)


def near(value):
    return pltpu.with_memory_space_constraint(value, pltpu.VMEM)


def after_all(value, *others):
    return lax.optimization_barrier((value, *others))[0]


def shifted(axis, value, step):
    count = lax.axis_size(axis)
    return lax.ppermute(value, axis, [(i, (i + step) % count) for i in range(count)])


def exchange(value, axis):
    return lax.all_to_all(value, axis, split_axis=0, concat_axis=0, tiled=True)


def on_device(field, spec_weight, dw_kernel, point_weight, bias):
    tab = {
        name: np.stack(halves(value)) for name, value in tables(32, 128, 128, 256).items()
    }
    plain, kept_near = jax.ShapeDtypeStruct, pltpu.VMEM
    dma = pltpu.SemaphoreType.DMA
    far = functools.partial(pltpu.with_memory_space_constraint, memory_space=pltpu.HBM)
    cells = far(field.reshape(128, 16, 256))
    zchunks, first, last = call(
        forward_z,
        [((8, 16, 8, 128), plain), ((16, 32, 256), plain), ((16, 32, 256), plain)],
        2,
        in_specs=[HBM] * 2,
        out_specs=[ANY] * 3,
        scratch_shapes=[
            pltpu.VMEM((2, 2, 128, 8, 128), F32),
            pltpu.VMEM((128, 256), BF16),
            pltpu.VMEM((8, 16, 8, 128), F32),
            pltpu.VMEM((16, 32, 256), F32),
            pltpu.VMEM((16, 32, 256), F32),
            dma((2, 2)),
            dma((7,)),
        ],
    )(cells, far(jnp.asarray(tab["fz"].reshape(128, 256))))
    taps = dw_kernel.transpose(1, 2, 3, 0)

    zall = exchange(zchunks, "gy")
    (packed,) = call(
        weights,
        [((2, 32, 32, 128), kept_near)],
        1,
        3,
        in_specs=[HBM],
        scratch_shapes=[pltpu.VMEM((2, 32, 128, 32), F32), dma((8,))],
    )(far(after_all(spec_weight.reshape(2, 32, 128, 32), zchunks)))
    zall, packed = lax.optimization_barrier((zall, packed))
    (ychunks,) = call(forward_y, [((32, 8, 128), plain)], 2)(
        near(zall), near(jnp.asarray(tab["fy"]))
    )

    yall = exchange(ychunks, "gx")
    first, last, taps_now, _ = lax.optimization_barrier((first, last, taps, ychunks))
    before = shifted("gx", last, 1)
    after = shifted("gx", first, -1)
    base, own_rims = call(
        own_cells,
        [((4, 16, 32, 256), kept_near), ((2, 4, 32, 256), plain)],
        4,
        8,
        in_specs=[HBM] + [VMEM] * 3,
        scratch_shapes=[
            pltpu.VMEM((2, 2, 128, 8, 128), F32),
            pltpu.VMEM((4, 16, 32, 256), F32),
            pltpu.VMEM((27, 32, 128), F32),
            dma((2, 2)),
        ],
    )(cells, taps_now, point_weight, bias.reshape(1, 32))
    yall, base = lax.optimization_barrier((yall, base))
    (xchunks,) = call(
        middle,
        [((32, 8, 128), plain)],
        4,
        in_specs=[VMEM] * 3 + [ANY],
        scratch_shapes=[pltpu.VMEM((2, 256, 64), BF16), dma],
    )(near(yall), near(packed), near(jnp.asarray(tab["fx"])), far(jnp.asarray(tab["ix"])))

    xall = exchange(xchunks, "gx")
    before, after, _ = lax.optimization_barrier((before, after, xchunks))
    before, after = far(before), far(after)
    top, bottom = call(
        rims,
        [((6, 32, 256), plain)] * 2,
        3,
        in_specs=[ANY] * 3,
        out_specs=[ANY] * 2,
        scratch_shapes=[dma((2, 3))],
    )(own_rims, before, after)
    left = shifted("gy", top, 1)
    right = shifted("gy", bottom, -1)
    xall, top, bottom = lax.optimization_barrier((xall, top, bottom))
    (back,) = call(inverse_y, [((8, 16, 8, 128), plain)], 2)(
        near(xall), near(jnp.asarray(tab["iy"]))
    )

    ball = exchange(back, "gy")
    left, right, _ = lax.optimization_barrier((left, right, back))
    (base,) = call(
        edge_cells,
        [((4, 16, 32, 256), kept_near)],
        6,
        40,
        in_specs=[VMEM] + [ANY] * 4 + [VMEM],
        scratch_shapes=[
            pltpu.VMEM((16, 32, 256), F32),
            pltpu.VMEM((16, 32, 256), F32),
            pltpu.VMEM((6, 32, 256), F32),
            pltpu.VMEM((6, 32, 256), F32),
            pltpu.VMEM((27, 32, 128), F32),
            dma((4,)),
        ],
        input_output_aliases={0: 0},
    )(near(base), before, after, far(left), far(right), taps)
    ball, base = lax.optimization_barrier((ball, base))
    (out,) = call(
        final,
        [((128, 16, 256), plain)],
        3,
        out_specs=[ANY],
        scratch_shapes=[pltpu.VMEM((2, 2, 128, 8, 128), F32), dma((2, 2))],
    )(near(ball), near(base), near(jnp.asarray(tab["iz"])))
    return out.reshape(field.shape)


def solution(mesh):
    placed = (P(None, "gx", "gy", None), P(None, None, "gx", "gy", None, None), P(), P(), P())
    return jax.shard_map(
        on_device, mesh=mesh, in_specs=placed, out_specs=P(None, "gx", "gy", None), check_vma=False
    )
```

time: 85.9 us -> 86.1 us (level)
  local copies, waits for them, and re-layouts: 16.2 us -> 4.49 us
  waiting for transfers between devices: 7.67 us -> 17.3 us
  starting transfers between devices: 35.4 us -> 38.2 us
    unnamed x62 -> x20, local copies, waits for them, and re-layouts: 15.8 us -> 4.49 us
    all_to_all x4, waiting for transfers between devices: 6.05 us -> 17.3 us  [exchange(): return lax.all_to_all(value, axis, split_axis=0, concat_axis=0, tiled=True)]
    all_to_all x4, starting transfers between devices: 28.5 us -> 31.3 us  [exchange(): return lax.all_to_all(value, axis, split_axis=0, concat_axis=0, tiled=True)]
    ppermute x4, waiting for transfers between devices: 1.61 us -> 0.01 us  [shifted(): lax.ppermute(value, axis, [(i, (i + step) % count) for i in range(count)])]
    pallas_call x10 -> x9, Pallas kernels: 25.1 us -> 25.1 us  [the longest x1 7.07 us: on_device(): call(own_cells, [((4, 16, 32, 256), kept_near), ((2, 4, 32, 256), plain)]...]
  transfers between devices with their start and end apart: 8 -> 8, of which waited for: 5 -> 3; matrix products, arithmetic and copies ran while one was open for 1% -> 0% of each run, Pallas kernels for 20% -> 20%
where the time goes in v4:
time: 86.1 us; the launch traced here: 85.4 us
  starting transfers between devices  38.2 us (44%)
  Pallas kernels  25.1 us (29%)
  waiting for transfers between devices  17.3 us (20%)
  local copies, waits for them, and re-layouts  4.49 us (5%)
    all_to_all x4, starting transfers between devices, exchange(): return lax.all_to_all(value, axis, split_axis=0, concat_axis=0, tiled=True)  31.3 us
    all_to_all x4, waiting for transfers between devices, exchange(): return lax.all_to_all(value, axis, split_axis=0, concat_axis=0, tiled=True)  17.3 us
    pallas_call x1, Pallas kernels, on_device(): call(own_cells, [((4, 16, 32, 256), kept_near), ((2, 4, 32, 256), plain)]...  7.07 us
    ppermute x4, starting transfers between devices, shifted(): lax.ppermute(value, axis, [(i, (i + step) % count) for i in range(count)])  6.87 us
    unnamed x20, local copies, waits for them, and re-layouts  4.49 us
    pallas_call x1, Pallas kernels, on_device(): call(forward_z, [((8, 16, 8, 128), plain), ((16, 32, 256), plain), ((16,...  4.05 us
    pallas_call x1, Pallas kernels, on_device(): call(final, [((128, 16, 256), plain)], 3, out_specs=[ANY], scratch_shapes...  3.08 us
    pallas_call x1, Pallas kernels, on_device(): call(weights, [((2, 32, 32, 128), kept_near)], 1, 3, in_specs=[HBM], scra...  3.03 us
  transfers between devices with their start and end apart: 8, of which 3 were waited for; matrix products, arithmetic and copies ran while one was open for 0% of the time, Pallas kernels for 20%

profile of v4, /device:TPU:1, one launch (start us, length us, event | category | flops | bytes accessed | tf_op | source)
XLA Modules:
  0.0 85.4 jit_solution(9575515391498704417)
XLA Ops:
  0.0 4.0 %forward_z.1 = (f32[8,16,8,128]{3,2,1,0:T(8,128)}, f32[16,32,256]{2,1,0:T(8,128)}, f32[16,32,256]{2,1,0:T(8,128)}) custom-call(f32[128,16,256]{2,1,0:T(8,128)} %bitcast.8, bf16[128,256]{1,0:T(8,128)(2,1)} %constant.12.clone.table_ref), custom_call_target="tpu_custom_call" | custom-call | tf_op jit(solution)/shard_map/forward_z/pallas_call | solution.py:413
  4.1 7.5 %all-to-all-start = ((f32[8,16,8,128]{3,2,1,0:T(8,128)}), f32[8,16,8,128]{3,2,1,0:T(8,128)S(1)}, u32[]{:S(2)}, u32[]{:S(2)}) async-start(f32[8,16,8,128]{3,2,1,0:T(8,128)} %get-tuple-element.27), calls=%async_computation | async-start | bytes 1048576 | tf_op jit(solution)/shard_map/all_to_all | solution.py:402
  11.6 0.0 copy-start.3
  11.6 0.0 copy-start.6
  11.6 3.0 %weights.1.weight_ref = f32[2,32,32,128]{3,2,1,0:T(8,128)S(1)} custom-call(f32[2,32,128,32]{3,2,1,0:T(8,128)} %bitcast.10), custom_call_target="tpu_custom_call" | custom-call | flops 3000000000 | tf_op jit(solution)/shard_map/weights/pallas_call | solution.py:432
  14.6 7.6 %all-to-all-done.data_ref = f32[8,16,8,128]{3,2,1,0:T(8,128)S(1)} async-done(((f32[8,16,8,128]{3,2,1,0:T(8,128)}), f32[8,16,8,128]{3,2,1,0:T(8,128)S(1)}, u32[]{:S(2)}, u32[]{:S(2)}) %all-to-all-start) | async-done | bytes 524320 | tf_op jit(solution)/shard_map/all_to_all | solution.py:402
  22.2 0.0 copy-done.3
  22.2 1.0 %forward_y.1 = f32[32,8,128]{2,1,0:T(8,128)} custom-call(f32[8,16,8,128]{3,2,1,0:T(8,128)S(1)} %all-to-all-done.data_ref, bf16[2,64,256]{2,1,0:T(8,128)(2,1)S(1)} %copy-done.3), custom_call_target="tpu_custom_call" | custom-call | tf_op jit(solution)/shard_map/forward_y/pallas_call | solution.py:441
  23.2 10.5 %all-to-all-start.1 = ((f32[32,8,128]{2,1,0:T(8,128)}), f32[32,8,128]{2,1,0:T(8,128)S(1)}, u32[]{:S(2)}, u32[]{:S(2)}) async-start(f32[32,8,128]{2,1,0:T(8,128)} %forward_y.1), calls=%async_computation.1 | async-start | bytes 262144 | tf_op jit(solution)/shard_map/all_to_all | solution.py:402
  33.8 1.7 %collective-permute-start = (f32[16,32,256]{2,1,0:T(8,128)}, f32[16,32,256]{2,1,0:T(8,128)}, u32[]{:S(2)}, u32[]{:S(2)}) collective-permute-start(f32[16,32,256]{2,1,0:T(8,128)} %get-tuple-element.37), channel_id=1, source_target_pairs={{0,8},{8,16},{16,24},{24,32},{32,40},{40,48},{48,56},{56,64},{64,7... | collective-permute-start | bytes 1572872 | tf_op jit(solution)/shard_map/ppermute | solution.py:398
  35.5 0.0 collective-permute-start.1
  35.5 0.0 copy-done.6
  35.5 0.0 copy-start.4
  35.5 0.7 copy-done.4
  36.2 0.0 copy-start.7
  36.2 0.7 copy-done.7
  36.9 7.1 %own_cells.1 = (f32[4,16,32,256]{3,2,1,0:T(8,128)S(1)}, f32[2,4,32,256]{3,2,1,0:T(8,128)S(1)}) custom-call(f32[128,16,256]{2,1,0:T(8,128)} %bitcast.9, f32[3,3,3,32]{3,2,1,0:T(4,128)S(1)} %bitcast.5, f32[32,32]{1,0:T(8,128)S(1)} %copy-done.6, f32[1,32]{1,0:T(1,128)S(1)} %bitcast.7), custom_call_target="tpu_custom_call" | custom-call | flops 8000000000 | tf_op jit(solution)/shard_map/own_cells/pallas_call | solution.py:449
  43.9 0.0 all-to-all-done.1.data_ref
  44.0 0.0 copy-start.2
  44.0 0.8 copy-done.2
  44.8 1.9 %middle.1 = f32[32,8,128]{2,1,0:T(8,128)} custom-call(f32[32,8,128]{2,1,0:T(8,128)S(1)} %all-to-all-done.1.data_ref, f32[2,32,32,128]{3,2,1,0:T(8,128)S(1)} %weights.1.weight_ref, bf16[2,64,256]{2,1,0:T(8,128)(2,1)S(1)} %copy-done.2, bf16[2,256,64]{2,1,0:T(8,128)(2,1)} %constant.15.clone.inverse_hbm), custom_call_target="tpu_custom_call" | custom-call | tf_op jit(solution)/shard_map/middle/pallas_call | solution.py:463
  46.7 0.0 copy-start.5
  46.7 9.6 %all-to-all-start.2 = ((f32[32,8,128]{2,1,0:T(8,128)}), f32[32,8,128]{2,1,0:T(8,128)S(1)}, u32[]{:S(2)}, u32[]{:S(2)}) async-start(f32[32,8,128]{2,1,0:T(8,128)} %middle.1), calls=%async_computation.2 | async-start | bytes 262144 | tf_op jit(solution)/shard_map/all_to_all | solution.py:402
  56.3 0.0 collective-permute-done.before_ref.before_hbm
  56.4 0.0 collective-permute-done.1.after_ref.after_hbm
  56.4 1.2 %rims.1 = (f32[6,32,256]{2,1,0:T(8,128)S(1)}, f32[6,32,256]{2,1,0:T(8,128)S(1)}) custom-call(f32[2,4,32,256]{3,2,1,0:T(8,128)S(1)} %get-tuple-element.36.rows_ref, f32[16,32,256]{2,1,0:T(8,128)} %collective-permute-done.before_ref.before_hbm, f32[16,32,256]{2,1,0:T(8,128)} %collective-permute-done.1.after_ref.after_hbm), custom_call_target="tpu_custom_call" | custom-call | tf_op jit(solution)/shard_map/rims/pallas_call | solution.py:474
  57.5 1.3 %collective-permute-start.2 = (f32[6,32,256]{2,1,0:T(8,128)S(1)}, f32[6,32,256]{2,1,0:T(8,128)S(1)}, u32[]{:S(2)}, u32[]{:S(2)}) collective-permute-start(f32[6,32,256]{2,1,0:T(8,128)S(1)} %get-tuple-element.41), channel_id=1, source_target_pairs={{0,1},{1,2},{2,3},{3,4},{4,5},{5,6},{6,7},{7,0},{8,9},{9,10},{10,1... | collective-permute-start | bytes 589832 | tf_op jit(solution)/shard_map/ppermute | solution.py:398
  58.8 3.9 %collective-permute-start.3 = (f32[6,32,256]{2,1,0:T(8,128)S(1)}, f32[6,32,256]{2,1,0:T(8,128)S(1)}, u32[]{:S(2)}, u32[]{:S(2)}) collective-permute-start(f32[6,32,256]{2,1,0:T(8,128)S(1)} %get-tuple-element.42), channel_id=1, source_target_pairs={{0,7},{1,0},{2,1},{3,2},{4,3},{5,4},{6,5},{7,6},{8,15},{9,8},{10,9... | collective-permute-start | bytes 589832 | tf_op jit(solution)/shard_map/ppermute | solution.py:398
  62.7 3.0 %all-to-all-done.2.data_ref = f32[32,8,128]{2,1,0:T(8,128)S(1)} async-done(((f32[32,8,128]{2,1,0:T(8,128)}), f32[32,8,128]{2,1,0:T(8,128)S(1)}, u32[]{:S(2)}, u32[]{:S(2)}) %all-to-all-start.2) | async-done | bytes 131104 | tf_op jit(solution)/shard_map/all_to_all | solution.py:402
  65.7 0.0 copy-start
  65.7 0.9 %copy-done = bf16[2,256,64]{2,1,0:T(8,128)(2,1)S(1)} copy-done((bf16[2,256,64]{2,1,0:T(8,128)(2,1)S(1)}, bf16[2,256,64]{2,1,0:T(8,128)(2,1)}, u32[]{:S(2)}) %copy-start) | copy-done | bytes 65560
  66.6 1.2 %inverse_y.1 = f32[8,16,8,128]{3,2,1,0:T(8,128)} custom-call(f32[32,8,128]{2,1,0:T(8,128)S(1)} %all-to-all-done.2.data_ref, bf16[2,256,64]{2,1,0:T(8,128)(2,1)S(1)} %copy-done), custom_call_target="tpu_custom_call" | custom-call | tf_op jit(solution)/shard_map/inverse_y/pallas_call | solution.py:485
  67.8 3.7 %all-to-all-start.3 = ((f32[8,16,8,128]{3,2,1,0:T(8,128)}), f32[8,16,8,128]{3,2,1,0:T(8,128)S(1)}, u32[]{:S(2)}, u32[]{:S(2)}) async-start(f32[8,16,8,128]{3,2,1,0:T(8,128)} %inverse_y.1), calls=%async_computation.3 | async-start | bytes 1048576 | tf_op jit(solution)/shard_map/all_to_all | solution.py:402
  71.5 0.0 copy-start.1
  71.5 0.0 collective-permute-done.2.left_hbm
  71.5 0.0 copy-start.8
  71.5 0.0 collective-permute-done.3.right_hbm
  71.5 0.7 copy-done.8
  72.2 0.0 copy-start.9
  72.2 0.7 copy-done.9
  72.8 0.0 copy-done.5
  72.9 2.6 %edge_cells.1.base_ref = f32[4,16,32,256]{3,2,1,0:T(8,128)S(1)} custom-call(f32[4,16,32,256]{3,2,1,0:T(8,128)S(1)} %get-tuple-element.44.base_ref, f32[16,32,256]{2,1,0:T(8,128)} %collective-permute-done.before_ref.before_hbm, f32[16,32,256]{2,1,0:T(8,128)} %collective-permute-done.1.after_ref.after_hbm, ...), custom_call_target="tpu_custom_call", output_to_operand_aliasing={{}: (0, {})} | custom-call | flops 40000000000 | tf_op jit(solution)/shard_map/edge_cells/pallas_call | solution.py:491
  75.4 6.7 %all-to-all-done.3.data_ref = f32[8,16,8,128]{3,2,1,0:T(8,128)S(1)} async-done(((f32[8,16,8,128]{3,2,1,0:T(8,128)}), f32[8,16,8,128]{3,2,1,0:T(8,128)S(1)}, u32[]{:S(2)}, u32[]{:S(2)}) %all-to-all-start.3) | async-done | bytes 524320 | tf_op jit(solution)/shard_map/all_to_all | solution.py:402
  82.1 0.0 copy-done.1
  82.1 3.1 %final.1 = f32[128,16,256]{2,1,0:T(8,128)} custom-call(f32[8,16,8,128]{3,2,1,0:T(8,128)S(1)} %all-to-all-done.3.data_ref, f32[4,16,32,256]{3,2,1,0:T(8,128)S(1)} %edge_cells.1.base_ref, bf16[2,64,256]{2,1,0:T(8,128)(2,1)S(1)} %copy-done.1), custom_call_target="tpu_custom_call" | custom-call | tf_op jit(solution)/shard_map/final/pallas_call | solution.py:508
Async XLA Ops:
  4.1 18.2 %all-to-all-start = ((f32[8,16,8,128]{3,2,1,0:T(8,128)}), f32[8,16,8,128]{3,2,1,0:T(8,128)S(1)}, u32[]{:S(2)}, u32[]{:S(2)}) async-start(f32[8,16,8,128]{3,2,1,0:T(8,128)} %get-tuple-element.27), calls=%async_computation | async-start | bytes 1048576 | tf_op jit(solution)/shard_map/all_to_all | solution.py:402
  11.6 10.7 %copy-start.3 = (bf16[2,64,256]{2,1,0:T(8,128)(2,1)S(1)}, bf16[2,64,256]{2,1,0:T(8,128)(2,1)}, u32[]{:S(2)}) copy-start(bf16[2,64,256]{2,1,0:T(8,128)(2,1)} %constant.13.clone.table_ref) | copy-start | bytes 196612
  11.6 23.9 %copy-start.6 = (f32[32,32]{1,0:T(8,128)S(1)}, f32[32,32]{1,0:T(8,128)}, u32[]{:S(2)}) copy-start(f32[32,32]{1,0:T(8,128)} %point_ref.1) | copy-start | bytes 12292
  23.2 20.7 %all-to-all-start.1 = ((f32[32,8,128]{2,1,0:T(8,128)}), f32[32,8,128]{2,1,0:T(8,128)S(1)}, u32[]{:S(2)}, u32[]{:S(2)}) async-start(f32[32,8,128]{2,1,0:T(8,128)} %forward_y.1), calls=%async_computation.1 | async-start | bytes 262144 | tf_op jit(solution)/shard_map/all_to_all | solution.py:402
  33.8 22.6 %collective-permute-start = (f32[16,32,256]{2,1,0:T(8,128)}, f32[16,32,256]{2,1,0:T(8,128)}, u32[]{:S(2)}, u32[]{:S(2)}) collective-permute-start(f32[16,32,256]{2,1,0:T(8,128)} %get-tuple-element.37), channel_id=1, source_target_pairs={{0,8},{8,16},{16,24},{24,32},{32,40},{40,48},{48,56},{56,64},{64,7... | collective-permute-start | bytes 1572872 | tf_op jit(solution)/shard_map/ppermute | solution.py:398
  35.5 20.9 %collective-permute-start.1 = (f32[16,32,256]{2,1,0:T(8,128)}, f32[16,32,256]{2,1,0:T(8,128)}, u32[]{:S(2)}, u32[]{:S(2)}) collective-permute-start(f32[16,32,256]{2,1,0:T(8,128)} %get-tuple-element.38), channel_id=1, source_target_pairs={{0,248},{8,0},{16,8},{24,16},{32,24},{40,32},{48,40},{56,48},{64,5... | collective-permute-start | bytes 1572872 | tf_op jit(solution)/shard_map/ppermute | solution.py:398
  35.5 0.7 copy-start.4
  36.2 0.7 copy-start.7
  44.0 0.8 copy-start.2
  46.7 26.1 %copy-start.5 = (f32[32,3,3,3]{0,3,2,1:T(4,128)S(1)}, f32[32,3,3,3]{0,3,2,1:T(4,128)}, u32[]{:S(2)}) copy-start(f32[32,3,3,3]{0,3,2,1:T(4,128)} %param.13) | copy-start | bytes 10372
  46.7 19.0 %all-to-all-start.2 = ((f32[32,8,128]{2,1,0:T(8,128)}), f32[32,8,128]{2,1,0:T(8,128)S(1)}, u32[]{:S(2)}, u32[]{:S(2)}) async-start(f32[32,8,128]{2,1,0:T(8,128)} %middle.1), calls=%async_computation.2 | async-start | bytes 262144 | tf_op jit(solution)/shard_map/all_to_all | solution.py:402
  57.5 13.9 %collective-permute-start.2 = (f32[6,32,256]{2,1,0:T(8,128)S(1)}, f32[6,32,256]{2,1,0:T(8,128)S(1)}, u32[]{:S(2)}, u32[]{:S(2)}) collective-permute-start(f32[6,32,256]{2,1,0:T(8,128)S(1)} %get-tuple-element.41), channel_id=1, source_target_pairs={{0,1},{1,2},{2,3},{3,4},{4,5},{5,6},{6,7},{7,0},{8,9},{9,10},{10,1... | collective-permute-start | bytes 589832 | tf_op jit(solution)/shard_map/ppermute | solution.py:398
  58.8 12.7 %collective-permute-start.3 = (f32[6,32,256]{2,1,0:T(8,128)S(1)}, f32[6,32,256]{2,1,0:T(8,128)S(1)}, u32[]{:S(2)}, u32[]{:S(2)}) collective-permute-start(f32[6,32,256]{2,1,0:T(8,128)S(1)} %get-tuple-element.42), channel_id=1, source_target_pairs={{0,7},{1,0},{2,1},{3,2},{4,3},{5,4},{6,5},{7,6},{8,15},{9,8},{10,9... | collective-permute-start | bytes 589832 | tf_op jit(solution)/shard_map/ppermute | solution.py:398
  65.7 0.9 %copy-start = (bf16[2,256,64]{2,1,0:T(8,128)(2,1)S(1)}, bf16[2,256,64]{2,1,0:T(8,128)(2,1)}, u32[]{:S(2)}) copy-start(bf16[2,256,64]{2,1,0:T(8,128)(2,1)} %constant.16.clone.table_ref) | copy-start | bytes 196612
  67.8 14.4 %all-to-all-start.3 = ((f32[8,16,8,128]{3,2,1,0:T(8,128)}), f32[8,16,8,128]{3,2,1,0:T(8,128)S(1)}, u32[]{:S(2)}, u32[]{:S(2)}) async-start(f32[8,16,8,128]{3,2,1,0:T(8,128)} %inverse_y.1), calls=%async_computation.3 | async-start | bytes 1048576 | tf_op jit(solution)/shard_map/all_to_all | solution.py:402
  71.5 10.7 %copy-start.1 = (bf16[2,64,256]{2,1,0:T(8,128)(2,1)S(1)}, bf16[2,64,256]{2,1,0:T(8,128)(2,1)}, u32[]{:S(2)}) copy-start(bf16[2,64,256]{2,1,0:T(8,128)(2,1)} %constant.17.clone.table_ref) | copy-start | bytes 196612
  71.5 0.7 copy-start.8
  72.2 0.7 copy-start.9

commit v5 on v4

--- a/solution.py
+++ b/solution.py
@@ -105,10 +105,8 @@
         copy.wait()
 
 
-def forward_z(
-    cells_ref, table_ref, out_ref, first_ref, last_ref, held, both, ready, firsts, lasts, sems, done
-):
-    load = pltpu.make_async_copy(table_ref, both, done.at[6])
+def forward_z(cells_ref, table_ref, out_ref, held, both, ready, sems, done):
+    load = pltpu.make_async_copy(table_ref, both, done.at[2])
     load.start()
     copies = field_copies(cells_ref, held, sems)
     start_all(copies[0] + copies[1])
@@ -118,21 +116,14 @@
         wait_all(copies[half])
         span = pl.ds(8 * half, 8)
         for y in range(8 * half, 8 * half + 8):
-            parts = field_rows(held, y)
-            firsts[y] = parts[0]
-            lasts[y] = parts[3]
-            high, low = split(jnp.concatenate(parts, axis=0))
+            high, low = split(jnp.concatenate(field_rows(held, y), axis=0))
             wide = mm_nt(both[...], high)
             total = wide[:64] + wide[64:] + mm_nt(both[:64], low)
             ready[:, y] = total.reshape(8, 8, 128)
-        moves = [
-            (ready.at[:, span], out_ref.at[:, span]),
-            (firsts.at[span], first_ref.at[span]),
-            (lasts.at[span], last_ref.at[span]),
-        ]
-        for i, (src, dst) in enumerate(moves):
-            results.append(pltpu.make_async_copy(src, dst, done.at[3 * half + i]))
-            results[-1].start()
+        results.append(
+            pltpu.make_async_copy(ready.at[:, span], out_ref.at[:, span], done.at[half])
+        )
+        results[-1].start()
     wait_all(results)
 
 
@@ -149,9 +140,14 @@
             out[pl.ds(2 * x + part, 32, stride=8), :] = tile[32 * part : 32 * part + 32]
 
 
-def middle(data_ref, weight_ref, forward_ref, inverse_hbm, out_ref, inverse_ref, sem):
-    load = pltpu.make_async_copy(inverse_hbm, inverse_ref, sem)
+def middle(
+    data_ref, weight_ref, forward_hbm, inverse_hbm, out_ref, forward_ref, inverse_ref, sems
+):
+    first_load = pltpu.make_async_copy(forward_hbm, forward_ref, sems.at[0])
+    load = pltpu.make_async_copy(inverse_hbm, inverse_ref, sems.at[1])
+    first_load.start()
     load.start()
+    first_load.wait()
     spec = table_dot(forward_ref, data_ref[...].reshape(256, 128))
     spec_re, spec_im = spec[:32], spec[32:]
     lane = lax.broadcasted_iota(jnp.int32, (32, 128), 1)
@@ -273,10 +269,18 @@
 
 
 def own_cells(
-    cells_ref, dw_ref, point_ref, bias_ref, out_ref, rim_ref, held, planes, tap_ref, sems
+    cells_ref, dw_hbm, point_hbm, bias_hbm, out_ref, first_ref, last_ref, rim_ref,
+    held, planes, tap_ref, dw_ref, point_ref, bias_ref, sems, small
 ):
+    loads = [
+        pltpu.make_async_copy(src, dst, small.at[i])
+        for i, (src, dst) in enumerate(
+            ((dw_hbm, dw_ref), (point_hbm, point_ref), (bias_hbm, bias_ref))
+        )
+    ]
     copies = field_copies(cells_ref, held, sems)
-    start_all(copies[0] + copies[1])
+    start_all(loads + copies[0] + copies[1])
+    wait_all(loads)
     spread_taps(dw_ref, tap_ref)
     channel_map = jnp.concatenate([jnp.concatenate([point_ref[...].T] * 4, axis=1)] * 4, axis=0)
     row = lax.broadcasted_iota(jnp.int32, (128, 128), 0)
@@ -286,14 +290,6 @@
     point = jnp.concatenate([high, low, high], axis=1)
     bias = jnp.broadcast_to(bias_ref[...], (32, 32)).T[:, :1]
     bias = jnp.concatenate([bias] * 4, axis=0)
-    for half in range(2):
-        wait_all(copies[half])
-        for y in range(8 * half, 8 * half + 8):
-            parts = field_rows(held, y)
-            for x in range(4):
-                planes[x, y] = parts[x]
-                if y % 15 == 0:
-                    rim_ref[half, x] = parts[x]
 
     def line(y, shifts):
         high, low = split(planes[:, y].reshape(128, 256))
@@ -313,26 +309,43 @@
         line(y, (0, 1, 2))
         return carry
 
+    def fill(half):
+        wait_all(copies[half])
+        for y in range(8 * half, 8 * half + 8):
+            for x, part in enumerate(field_rows(held, y)):
+                planes[x, y] = part
+
+    fill(0)
     line(0, (1, 2))
-    lax.fori_loop(1, 15, body, 0)
+    lax.fori_loop(1, 7, body, 0)
+    fill(1)
+    moves = [
+        (planes.at[0], first_ref),
+        (planes.at[3], last_ref),
+        (planes.at[:, 0], rim_ref.at[0]),
+        (planes.at[:, 15], rim_ref.at[1]),
+    ]
+    results = [
+        pltpu.make_async_copy(src, dst, small.at[3 + i]) for i, (src, dst) in enumerate(moves)
+    ]
+    start_all(results)
+    lax.fori_loop(7, 15, body, 0)
     line(15, (0, 1))
+    wait_all(results)
 
 
 def edge_cells(
-    base_ref, before_hbm, after_hbm, left_hbm, right_hbm, dw_ref,
-    out_ref, before_ref, after_ref, left_ref, right_ref, tap_ref, sems
+    base_ref, before_hbm, after_hbm, left_ref, right_ref, dw_hbm,
+    out_ref, before_ref, after_ref, tap_ref, dw_ref, sems
 ):
-    moves = [
-        (left_hbm, left_ref), (right_hbm, right_ref), (before_hbm, before_ref), (after_hbm, after_ref)
-    ]
+    moves = [(dw_hbm, dw_ref), (before_hbm, before_ref), (after_hbm, after_ref)]
     copies = [
         pltpu.make_async_copy(src, dst, sems.at[i]) for i, (src, dst) in enumerate(moves)
     ]
-    for copy in copies:
-        copy.start()
+    start_all(copies)
+    copies[0].wait()
     spread_taps(dw_ref, tap_ref)
-    for i, (b, y, source) in enumerate(((0, 0, left_ref), (2, 15, right_ref))):
-        copies[i].wait()
+    for b, y, source in ((0, 0, left_ref), (2, 15, right_ref)):
         for tile in range(4):
             chans = slice(8 * tile, 8 * tile + 8)
             for x in range(4):
@@ -341,8 +354,7 @@
                     load = lambda lanes: source[x + a, chans, lanes]
                     add_taps(sums, tap_ref, chans, 9 * a + 3 * b, load)
                 out_ref[x, y, chans, :] = base_ref[x, y, chans, :] + shift_sum(sums)
-    copies[2].wait()
-    copies[3].wait()
+    wait_all(copies[1:])
 
     def line(y, before_rows, after_rows):
         for a, x, rows in ((0, 0, before_rows), (2, 3, after_rows)):
@@ -410,75 +422,88 @@
     dma = pltpu.SemaphoreType.DMA
     far = functools.partial(pltpu.with_memory_space_constraint, memory_space=pltpu.HBM)
     cells = far(field.reshape(128, 16, 256))
-    zchunks, first, last = call(
+    (zchunks,) = call(
         forward_z,
-        [((8, 16, 8, 128), plain), ((16, 32, 256), plain), ((16, 32, 256), plain)],
+        [((8, 16, 8, 128), plain)],
         2,
         in_specs=[HBM] * 2,
-        out_specs=[ANY] * 3,
+        out_specs=[ANY],
         scratch_shapes=[
             pltpu.VMEM((2, 2, 128, 8, 128), F32),
             pltpu.VMEM((128, 256), BF16),
             pltpu.VMEM((8, 16, 8, 128), F32),
-            pltpu.VMEM((16, 32, 256), F32),
-            pltpu.VMEM((16, 32, 256), F32),
+            dma((2, 2)),
+            dma((3,)),
+        ],
+    )(cells, far(jnp.asarray(tab["fz"].reshape(128, 256))))
+    taps = dw_kernel.transpose(1, 2, 3, 0)
+
+    zall = exchange(zchunks, "gy")
+    base, first, last, own_rims = call(
+        own_cells,
+        [
+            ((4, 16, 32, 256), kept_near),
+            ((16, 32, 256), pltpu.HBM),
+            ((16, 32, 256), pltpu.HBM),
+            ((2, 4, 32, 256), pltpu.HBM),
+        ],
+        4,
+        8,
+        in_specs=[HBM] * 4,
+        out_specs=[VMEM] + [HBM] * 3,
+        scratch_shapes=[
+            pltpu.VMEM((2, 2, 128, 8, 128), F32),
+            pltpu.VMEM((4, 16, 32, 256), F32),
+            pltpu.VMEM((27, 32, 128), F32),
+            pltpu.VMEM((3, 3, 3, 32), F32),
+            pltpu.VMEM((32, 32), F32),
+            pltpu.VMEM((1, 32), F32),
             dma((2, 2)),
             dma((7,)),
         ],
-    )(cells, far(jnp.asarray(tab["fz"].reshape(128, 256))))
-    taps = dw_kernel.transpose(1, 2, 3, 0)
-
-    zall = exchange(zchunks, "gy")
+    )(far(after_all(cells, zchunks)), far(taps), far(point_weight), far(bias.reshape(1, 32)))
+    zall, base = lax.optimization_barrier((zall, base))
+    (ychunks,) = call(forward_y, [((32, 8, 128), plain)], 2)(
+        near(zall), near(jnp.asarray(tab["fy"]))
+    )
+
+    yall = exchange(ychunks, "gx")
+    first, last, pairs, _ = lax.optimization_barrier((first, last, spec_weight, ychunks))
+    before = shifted("gx", far(last), 1)
+    after = shifted("gx", far(first), -1)
     (packed,) = call(
         weights,
         [((2, 32, 32, 128), kept_near)],
         1,
-        3,
+        8,
         in_specs=[HBM],
         scratch_shapes=[pltpu.VMEM((2, 32, 128, 32), F32), dma((8,))],
-    )(far(after_all(spec_weight.reshape(2, 32, 128, 32), zchunks)))
-    zall, packed = lax.optimization_barrier((zall, packed))
-    (ychunks,) = call(forward_y, [((32, 8, 128), plain)], 2)(
-        near(zall), near(jnp.asarray(tab["fy"]))
-    )
-
-    yall = exchange(ychunks, "gx")
-    first, last, taps_now, _ = lax.optimization_barrier((first, last, taps, ychunks))
-    before = shifted("gx", last, 1)
-    after = shifted("gx", first, -1)
-    base, own_rims = call(
-        own_cells,
-        [((4, 16, 32, 256), kept_near), ((2, 4, 32, 256), plain)],
-        4,
-        8,
-        in_specs=[HBM] + [VMEM] * 3,
-        scratch_shapes=[
-            pltpu.VMEM((2, 2, 128, 8, 128), F32),
-            pltpu.VMEM((4, 16, 32, 256), F32),
-            pltpu.VMEM((27, 32, 128), F32),
-            dma((2, 2)),
-        ],
-    )(cells, taps_now, point_weight, bias.reshape(1, 32))
-    yall, base = lax.optimization_barrier((yall, base))
+    )(far(pairs.reshape(2, 32, 128, 32)))
+    yall, packed = lax.optimization_barrier((yall, packed))
     (xchunks,) = call(
         middle,
         [((32, 8, 128), plain)],
         4,
-        in_specs=[VMEM] * 3 + [ANY],
-        scratch_shapes=[pltpu.VMEM((2, 256, 64), BF16), dma],
-    )(near(yall), near(packed), near(jnp.asarray(tab["fx"])), far(jnp.asarray(tab["ix"])))
+        in_specs=[VMEM] * 2 + [ANY] * 2,
+        scratch_shapes=[
+            pltpu.VMEM((2, 64, 256), BF16),
+            pltpu.VMEM((2, 256, 64), BF16),
+            dma((2,)),
+        ],
+    )(near(yall), near(packed), far(jnp.asarray(tab["fx"])), far(jnp.asarray(tab["ix"])))
 
     xall = exchange(xchunks, "gx")
     before, after, _ = lax.optimization_barrier((before, after, xchunks))
     before, after = far(before), far(after)
     top, bottom = call(
         rims,
-        [((6, 32, 256), plain)] * 2,
+        [((6, 32, 256), pltpu.HBM)] * 2,
         3,
-        in_specs=[ANY] * 3,
-        out_specs=[ANY] * 2,
+        2,
+        in_specs=[HBM] * 3,
+        out_specs=[HBM] * 2,
         scratch_shapes=[dma((2, 3))],
-    )(own_rims, before, after)
+    )(far(own_rims), before, after)
     left = shifted("gy", top, 1)
     right = shifted("gy", bottom, -1)
     xall, top, bottom = lax.optimization_barrier((xall, top, bottom))
@@ -493,17 +518,16 @@
         [((4, 16, 32, 256), kept_near)],
         6,
         40,
-        in_specs=[VMEM] + [ANY] * 4 + [VMEM],
+        in_specs=[VMEM] + [ANY] * 2 + [VMEM] * 2 + [ANY],
         scratch_shapes=[
             pltpu.VMEM((16, 32, 256), F32),
             pltpu.VMEM((16, 32, 256), F32),
-            pltpu.VMEM((6, 32, 256), F32),
-            pltpu.VMEM((6, 32, 256), F32),
             pltpu.VMEM((27, 32, 128), F32),
-            dma((4,)),
+            pltpu.VMEM((3, 3, 3, 32), F32),
+            dma((3,)),
         ],
         input_output_aliases={0: 0},
-    )(near(base), before, after, far(left), far(right), taps)
+    )(near(base), before, after, near(left), near(right), far(taps))
     ball, base = lax.optimization_barrier((ball, base))
     (out,) = call(
         final,

time: 86.1 us -> 88.3 us (1.026)
  Pallas kernels: 25.1 us -> 37.4 us
  starting transfers between devices: 38.2 us -> 33.4 us
  local copies, waits for them, and re-layouts: 4.49 us -> 0.01 us
    pallas_call x5, Pallas kernels: 17.2 us -> 29.7 us  [the longest x1 13.1 us: on_device(): call(rims, [((6, 32, 256), pltpu.HBM)] * 2, 3, 2, in_specs=[HBM] * 3, out...]
    all_to_all x4, starting transfers between devices: 31.3 us -> 26.6 us  [exchange(): return lax.all_to_all(value, axis, split_axis=0, concat_axis=0, tiled=True)]
    unnamed x20 -> x6, local copies, waits for them, and re-layouts: 4.49 us -> 0.01 us
    all_to_all x4, waiting for transfers between devices: 17.3 us -> 14.5 us  [exchange(): return lax.all_to_all(value, axis, split_axis=0, concat_axis=0, tiled=True)]
    ppermute x4, waiting for transfers between devices: 0.01 us -> 2.01 us  [shifted(): lax.ppermute(value, axis, [(i, (i + step) % count) for i in range(count)])]
  transfers between devices with their start and end apart: 8 -> 8, of which waited for: 3 -> 6; matrix products, arithmetic and copies ran while one was open for 0% -> 0% of each run, Pallas kernels for 20% -> 34%
where the time goes in v5:
time: 88.3 us; the launch traced here: 87.6 us
  Pallas kernels  37.4 us (42%)
  starting transfers between devices  33.4 us (38%)
  waiting for transfers between devices  16.5 us (19%)
    all_to_all x4, starting transfers between devices, exchange(): return lax.all_to_all(value, axis, split_axis=0, concat_axis=0, tiled=True)  26.6 us
    all_to_all x4, waiting for transfers between devices, exchange(): return lax.all_to_all(value, axis, split_axis=0, concat_axis=0, tiled=True)  14.5 us
    pallas_call x1, Pallas kernels, on_device(): call(rims, [((6, 32, 256), pltpu.HBM)] * 2, 3, 2, in_specs=[HBM] * 3, out...  13.1 us
    pallas_call x1, Pallas kernels, on_device(): call(own_cells, [((4, 16, 32, 256), kept_near), ((16, 32, 256), pltpu.HBM...  7.22 us
    ppermute x4, starting transfers between devices, shifted(): lax.ppermute(value, axis, [(i, (i + step) % count) for i in range(count)])  6.87 us
    pallas_call x1, Pallas kernels, on_device(): call(forward_z, [((8, 16, 8, 128), plain)], 2, in_specs=[HBM] * 2, out_sp...  3.81 us
    pallas_call x1, Pallas kernels, on_device(): call(final, [((128, 16, 256), plain)], 3, out_specs=[ANY], scratch_shapes...  3.08 us
    pallas_call x1, Pallas kernels, on_device(): call(weights, [((2, 32, 32, 128), kept_near)], 1, 8, in_specs=[HBM], scra...  3 us
  transfers between devices with their start and end apart: 8, of which 6 were waited for; matrix products, arithmetic and copies ran while one was open for 0% of the time, Pallas kernels for 34%

profile of v5, /device:TPU:1, one launch (start us, length us, event | category | flops | bytes accessed | tf_op | source)
XLA Modules:
  0.0 87.6 jit_solution(4450345964392500034)
XLA Ops:
  0.0 3.8 %forward_z.1 = f32[8,16,8,128]{3,2,1,0:T(8,128)} custom-call(f32[128,16,256]{2,1,0:T(8,128)} %bitcast.5, bf16[128,256]{1,0:T(8,128)(2,1)} %constant.12.clone.table_ref), custom_call_target="tpu_custom_call" | custom-call | tf_op jit(solution)/shard_map/forward_z/pallas_call | solution.py:425
  3.8 7.5 %all-to-all-start = ((f32[8,16,8,128]{3,2,1,0:T(8,128)}), f32[8,16,8,128]{3,2,1,0:T(8,128)S(1)}, u32[]{:S(2)}, u32[]{:S(2)}) async-start(f32[8,16,8,128]{3,2,1,0:T(8,128)} %forward_z.1), calls=%async_computation | async-start | bytes 1048576 | tf_op jit(solution)/shard_map/all_to_all | solution.py:414
  11.3 0.0 copy-start.2
  11.3 7.2 %own_cells.1 = (f32[4,16,32,256]{3,2,1,0:T(8,128)S(1)}, f32[16,32,256]{2,1,0:T(8,128)}, f32[16,32,256]{2,1,0:T(8,128)}, f32[2,4,32,256]{3,2,1,0:T(8,128)}) custom-call(f32[128,16,256]{2,1,0:T(8,128)} %bitcast.6, f32[3,3,3,32]{3,2,1,0:T(4,128)} %bitcast.8, f32[32,32]{1,0:T(8,128)} %point_hbm.1, f32[1,32]{1,0:T(1,128)} %bitcast.10), custom_call_target="tpu_custom_call" | custom-call | flops 8000000000 | tf_op jit(solution)/shard_map/own_cells/pallas_call | solution.py:442
  18.5 3.4 %all-to-all-done.data_ref = f32[8,16,8,128]{3,2,1,0:T(8,128)S(1)} async-done(((f32[8,16,8,128]{3,2,1,0:T(8,128)}), f32[8,16,8,128]{3,2,1,0:T(8,128)S(1)}, u32[]{:S(2)}, u32[]{:S(2)}) %all-to-all-start) | async-done | bytes 524320 | tf_op jit(solution)/shard_map/all_to_all | solution.py:414
  22.0 0.0 copy-done.2
  22.0 1.0 %forward_y.1 = f32[32,8,128]{2,1,0:T(8,128)} custom-call(f32[8,16,8,128]{3,2,1,0:T(8,128)S(1)} %all-to-all-done.data_ref, bf16[2,64,256]{2,1,0:T(8,128)(2,1)S(1)} %copy-done.2), custom_call_target="tpu_custom_call" | custom-call | tf_op jit(solution)/shard_map/forward_y/pallas_call | solution.py:466
  23.0 10.5 %all-to-all-start.1 = ((f32[32,8,128]{2,1,0:T(8,128)}), f32[32,8,128]{2,1,0:T(8,128)S(1)}, u32[]{:S(2)}, u32[]{:S(2)}) async-start(f32[32,8,128]{2,1,0:T(8,128)} %forward_y.1), calls=%async_computation.1 | async-start | bytes 262144 | tf_op jit(solution)/shard_map/all_to_all | solution.py:414
  33.5 1.7 %collective-permute-start = (f32[16,32,256]{2,1,0:T(8,128)}, f32[16,32,256]{2,1,0:T(8,128)}, u32[]{:S(2)}, u32[]{:S(2)}) collective-permute-start(f32[16,32,256]{2,1,0:T(8,128)} %get-tuple-element.35), channel_id=1, source_target_pairs={{0,8},{8,16},{16,24},{24,32},{32,40},{40,48},{48,56},{56,64},{64,7... | collective-permute-start | bytes 1572872 | tf_op jit(solution)/shard_map/ppermute | solution.py:410
  35.2 0.0 collective-permute-start.1
  35.2 3.0 %weights.1.weight_ref = f32[2,32,32,128]{3,2,1,0:T(8,128)S(1)} custom-call(f32[2,32,128,32]{3,2,1,0:T(8,128)} %bitcast.7), custom_call_target="tpu_custom_call" | custom-call | flops 8000000000 | tf_op jit(solution)/shard_map/weights/pallas_call | solution.py:474
  38.2 4.8 %all-to-all-done.1.data_ref = f32[32,8,128]{2,1,0:T(8,128)S(1)} async-done(((f32[32,8,128]{2,1,0:T(8,128)}), f32[32,8,128]{2,1,0:T(8,128)S(1)}, u32[]{:S(2)}, u32[]{:S(2)}) %all-to-all-start.1) | async-done | bytes 131104 | tf_op jit(solution)/shard_map/all_to_all | solution.py:414
  43.0 2.6 %middle.1 = f32[32,8,128]{2,1,0:T(8,128)} custom-call(f32[32,8,128]{2,1,0:T(8,128)S(1)} %all-to-all-done.1.data_ref, f32[2,32,32,128]{3,2,1,0:T(8,128)S(1)} %weights.1.weight_ref, bf16[2,64,256]{2,1,0:T(8,128)(2,1)} %constant.14.clone.forward_hbm, bf16[2,256,64]{2,1,0:T(8,128)(2,1)} %constant.15.clone.inverse_hbm), custom_call_target="tpu_custom_call" | custom-call | tf_op jit(solution)/shard_map/middle/pallas_call | solution.py:483
  45.6 4.9 %all-to-all-start.2 = ((f32[32,8,128]{2,1,0:T(8,128)}), f32[32,8,128]{2,1,0:T(8,128)S(1)}, u32[]{:S(2)}, u32[]{:S(2)}) async-start(f32[32,8,128]{2,1,0:T(8,128)} %middle.1), calls=%async_computation.2 | async-start | bytes 262144 | tf_op jit(solution)/shard_map/all_to_all | solution.py:414
  50.5 0.0 collective-permute-done.before_ref.before_hbm
  50.5 0.2 collective-permute-done.1.after_ref.after_hbm
  50.7 0.0 copy-start
  50.7 13.1 %rims.1 = (f32[6,32,256]{2,1,0:T(8,128)}, f32[6,32,256]{2,1,0:T(8,128)}) custom-call(f32[2,4,32,256]{3,2,1,0:T(8,128)} %get-tuple-element.34.rows_ref, f32[16,32,256]{2,1,0:T(8,128)} %collective-permute-done.before_ref.before_hbm, f32[16,32,256]{2,1,0:T(8,128)} %collective-permute-done.1.after_ref.after_hbm), custom_call_target="tpu_custom_call" | custom-call | flops 2000000000 | tf_op jit(solution)/shard_map/rims/pallas_call | solution.py:498
  63.8 1.3 %collective-permute-start.2 = (f32[6,32,256]{2,1,0:T(8,128)}, f32[6,32,256]{2,1,0:T(8,128)S(1)}, u32[]{:S(2)}, u32[]{:S(2)}) collective-permute-start(f32[6,32,256]{2,1,0:T(8,128)} %get-tuple-element.39), channel_id=1, source_target_pairs={{0,1},{1,2},{2,3},{3,4},{4,5},{5,6},{6,7},{7,0},{8,9},{9,10},{10,1... | collective-permute-start | bytes 589832 | tf_op jit(solution)/shard_map/ppermute | solution.py:410
  65.1 3.9 %collective-permute-start.3 = (f32[6,32,256]{2,1,0:T(8,128)}, f32[6,32,256]{2,1,0:T(8,128)S(1)}, u32[]{:S(2)}, u32[]{:S(2)}) collective-permute-start(f32[6,32,256]{2,1,0:T(8,128)} %get-tuple-element.40), channel_id=1, source_target_pairs={{0,7},{1,0},{2,1},{3,2},{4,3},{5,4},{6,5},{7,6},{8,15},{9,8},{10,9... | collective-permute-start | bytes 589832 | tf_op jit(solution)/shard_map/ppermute | solution.py:410
  69.0 0.0 all-to-all-done.2.data_ref
  69.0 0.0 copy-done
  69.0 1.2 %inverse_y.1 = f32[8,16,8,128]{3,2,1,0:T(8,128)} custom-call(f32[32,8,128]{2,1,0:T(8,128)S(1)} %all-to-all-done.2.data_ref, bf16[2,256,64]{2,1,0:T(8,128)(2,1)S(1)} %copy-done), custom_call_target="tpu_custom_call" | custom-call | tf_op jit(solution)/shard_map/inverse_y/pallas_call | solution.py:510
  70.1 3.7 %all-to-all-start.3 = ((f32[8,16,8,128]{3,2,1,0:T(8,128)}), f32[8,16,8,128]{3,2,1,0:T(8,128)S(1)}, u32[]{:S(2)}, u32[]{:S(2)}) async-start(f32[8,16,8,128]{3,2,1,0:T(8,128)} %inverse_y.1), calls=%async_computation.3 | async-start | bytes 1048576 | tf_op jit(solution)/shard_map/all_to_all | solution.py:414
  73.8 0.0 copy-start.1
  73.8 0.4 collective-permute-done.2.left_ref
  74.2 1.4 %collective-permute-done.3.right_ref = f32[6,32,256]{2,1,0:T(8,128)S(1)} collective-permute-done((f32[6,32,256]{2,1,0:T(8,128)}, f32[6,32,256]{2,1,0:T(8,128)S(1)}, u32[]{:S(2)}, u32[]{:S(2)}) %collective-permute-start.3) | collective-permute-done | bytes 196640 | tf_op jit(solution)/shard_map/ppermute | solution.py:410
  75.6 2.4 %edge_cells.1.base_ref = f32[4,16,32,256]{3,2,1,0:T(8,128)S(1)} custom-call(f32[4,16,32,256]{3,2,1,0:T(8,128)S(1)} %get-tuple-element.42.base_ref, f32[16,32,256]{2,1,0:T(8,128)} %collective-permute-done.before_ref.before_hbm, f32[16,32,256]{2,1,0:T(8,128)} %collective-permute-done.1.after_ref.after_hbm, ...), custom_call_target="tpu_custom_call", output_to_operand_aliasing={{}: (0, {})} | custom-call | flops 40000000000 | tf_op jit(solution)/shard_map/edge_cells/pallas_call | solution.py:516
  78.0 6.3 %all-to-all-done.3.data_ref = f32[8,16,8,128]{3,2,1,0:T(8,128)S(1)} async-done(((f32[8,16,8,128]{3,2,1,0:T(8,128)}), f32[8,16,8,128]{3,2,1,0:T(8,128)S(1)}, u32[]{:S(2)}, u32[]{:S(2)}) %all-to-all-start.3) | async-done | bytes 524320 | tf_op jit(solution)/shard_map/all_to_all | solution.py:414
  84.4 0.0 copy-done.1
  84.4 3.1 %final.1 = f32[128,16,256]{2,1,0:T(8,128)} custom-call(f32[8,16,8,128]{3,2,1,0:T(8,128)S(1)} %all-to-all-done.3.data_ref, f32[4,16,32,256]{3,2,1,0:T(8,128)S(1)} %edge_cells.1.base_ref, bf16[2,64,256]{2,1,0:T(8,128)(2,1)S(1)} %copy-done.1), custom_call_target="tpu_custom_call" | custom-call | tf_op jit(solution)/shard_map/final/pallas_call | solution.py:532
Async XLA Ops:
  3.8 18.2 %all-to-all-start = ((f32[8,16,8,128]{3,2,1,0:T(8,128)}), f32[8,16,8,128]{3,2,1,0:T(8,128)S(1)}, u32[]{:S(2)}, u32[]{:S(2)}) async-start(f32[8,16,8,128]{3,2,1,0:T(8,128)} %forward_z.1), calls=%async_computation | async-start | bytes 1048576 | tf_op jit(solution)/shard_map/all_to_all | solution.py:414
  11.3 10.7 %copy-start.2 = (bf16[2,64,256]{2,1,0:T(8,128)(2,1)S(1)}, bf16[2,64,256]{2,1,0:T(8,128)(2,1)}, u32[]{:S(2)}) copy-start(bf16[2,64,256]{2,1,0:T(8,128)(2,1)} %constant.13.clone.table_ref) | copy-start | bytes 196612
  23.0 20.0 %all-to-all-start.1 = ((f32[32,8,128]{2,1,0:T(8,128)}), f32[32,8,128]{2,1,0:T(8,128)S(1)}, u32[]{:S(2)}, u32[]{:S(2)}) async-start(f32[32,8,128]{2,1,0:T(8,128)} %forward_y.1), calls=%async_computation.1 | async-start | bytes 262144 | tf_op jit(solution)/shard_map/all_to_all | solution.py:414
  33.5 17.0 %collective-permute-start = (f32[16,32,256]{2,1,0:T(8,128)}, f32[16,32,256]{2,1,0:T(8,128)}, u32[]{:S(2)}, u32[]{:S(2)}) collective-permute-start(f32[16,32,256]{2,1,0:T(8,128)} %get-tuple-element.35), channel_id=1, source_target_pairs={{0,8},{8,16},{16,24},{24,32},{32,40},{40,48},{48,56},{56,64},{64,7... | collective-permute-start | bytes 1572872 | tf_op jit(solution)/shard_map/ppermute | solution.py:410
  35.2 15.5 %collective-permute-start.1 = (f32[16,32,256]{2,1,0:T(8,128)}, f32[16,32,256]{2,1,0:T(8,128)}, u32[]{:S(2)}, u32[]{:S(2)}) collective-permute-start(f32[16,32,256]{2,1,0:T(8,128)} %get-tuple-element.36), channel_id=1, source_target_pairs={{0,248},{8,0},{16,8},{24,16},{32,24},{40,32},{48,40},{56,48},{64,5... | collective-permute-start | bytes 1572872 | tf_op jit(solution)/shard_map/ppermute | solution.py:410
  45.6 23.3 %all-to-all-start.2 = ((f32[32,8,128]{2,1,0:T(8,128)}), f32[32,8,128]{2,1,0:T(8,128)S(1)}, u32[]{:S(2)}, u32[]{:S(2)}) async-start(f32[32,8,128]{2,1,0:T(8,128)} %middle.1), calls=%async_computation.2 | async-start | bytes 262144 | tf_op jit(solution)/shard_map/all_to_all | solution.py:414
  50.7 18.2 %copy-start = (bf16[2,256,64]{2,1,0:T(8,128)(2,1)S(1)}, bf16[2,256,64]{2,1,0:T(8,128)(2,1)}, u32[]{:S(2)}) copy-start(bf16[2,256,64]{2,1,0:T(8,128)(2,1)} %constant.16.clone.table_ref) | copy-start | bytes 196612
  63.8 10.4 %collective-permute-start.2 = (f32[6,32,256]{2,1,0:T(8,128)}, f32[6,32,256]{2,1,0:T(8,128)S(1)}, u32[]{:S(2)}, u32[]{:S(2)}) collective-permute-start(f32[6,32,256]{2,1,0:T(8,128)} %get-tuple-element.39), channel_id=1, source_target_pairs={{0,1},{1,2},{2,3},{3,4},{4,5},{5,6},{6,7},{7,0},{8,9},{9,10},{10,1... | collective-permute-start | bytes 589832 | tf_op jit(solution)/shard_map/ppermute | solution.py:410
  65.1 10.6 %collective-permute-start.3 = (f32[6,32,256]{2,1,0:T(8,128)}, f32[6,32,256]{2,1,0:T(8,128)S(1)}, u32[]{:S(2)}, u32[]{:S(2)}) collective-permute-start(f32[6,32,256]{2,1,0:T(8,128)} %get-tuple-element.40), channel_id=1, source_target_pairs={{0,7},{1,0},{2,1},{3,2},{4,3},{5,4},{6,5},{7,6},{8,15},{9,8},{10,9... | collective-permute-start | bytes 589832 | tf_op jit(solution)/shard_map/ppermute | solution.py:410
  70.1 14.2 %all-to-all-start.3 = ((f32[8,16,8,128]{3,2,1,0:T(8,128)}), f32[8,16,8,128]{3,2,1,0:T(8,128)S(1)}, u32[]{:S(2)}, u32[]{:S(2)}) async-start(f32[8,16,8,128]{3,2,1,0:T(8,128)} %inverse_y.1), calls=%async_computation.3 | async-start | bytes 1048576 | tf_op jit(solution)/shard_map/all_to_all | solution.py:414
  73.8 10.5 %copy-start.1 = (bf16[2,64,256]{2,1,0:T(8,128)(2,1)S(1)}, bf16[2,64,256]{2,1,0:T(8,128)(2,1)}, u32[]{:S(2)}) copy-start(bf16[2,64,256]{2,1,0:T(8,128)(2,1)} %constant.17.clone.table_ref) | copy-start | bytes 196612

commit v6 on v5

--- a/solution.py
+++ b/solution.py
@@ -497,11 +497,10 @@
     before, after = far(before), far(after)
     top, bottom = call(
         rims,
-        [((6, 32, 256), pltpu.HBM)] * 2,
+        [((6, 32, 256), kept_near)] * 2,
         3,
         2,
         in_specs=[HBM] * 3,
-        out_specs=[HBM] * 2,
         scratch_shapes=[dma((2, 3))],
     )(far(own_rims), before, after)
     left = shifted("gy", top, 1)

time: 88.3 us -> 79.1 us (0.90)
  Pallas kernels: 37.4 us -> 25.4 us
  waiting for transfers between devices: 16.5 us -> 19.5 us
    pallas_call x1, Pallas kernels: 13.1 us -> 1.09 us  [on_device(): call(rims, [((6, 32, 256), kept_near)] * 2, 3, 2, in_specs=[HBM] * 3, scr...]
    all_to_all x4, waiting for transfers between devices: 14.5 us -> 19.3 us  [exchange(): return lax.all_to_all(value, axis, split_axis=0, concat_axis=0, tiled=True)]
    ppermute x4, waiting for transfers between devices: 2.01 us -> 0.23 us  [shifted(): lax.ppermute(value, axis, [(i, (i + step) % count) for i in range(count)])]
  transfers between devices with their start and end apart: 8 -> 8, of which waited for: 6 -> 5; matrix products, arithmetic and copies ran while one was open for 0% -> 0% of each run, Pallas kernels for 34% -> 22%
where the time goes in v6:
time: 79.1 us; the launch traced here: 78.6 us
  starting transfers between devices  33.4 us (42%)
  Pallas kernels  25.4 us (32%)
  waiting for transfers between devices  19.5 us (25%)
    all_to_all x4, starting transfers between devices, exchange(): return lax.all_to_all(value, axis, split_axis=0, concat_axis=0, tiled=True)  26.6 us
    all_to_all x4, waiting for transfers between devices, exchange(): return lax.all_to_all(value, axis, split_axis=0, concat_axis=0, tiled=True)  19.3 us
    pallas_call x1, Pallas kernels, on_device(): call(own_cells, [((4, 16, 32, 256), kept_near), ((16, 32, 256), pltpu.HBM...  7.22 us
    ppermute x4, starting transfers between devices, shifted(): lax.ppermute(value, axis, [(i, (i + step) % count) for i in range(count)])  6.87 us
    pallas_call x1, Pallas kernels, on_device(): call(forward_z, [((8, 16, 8, 128), plain)], 2, in_specs=[HBM] * 2, out_sp...  3.81 us
    pallas_call x1, Pallas kernels, on_device(): call(final, [((128, 16, 256), plain)], 3, out_specs=[ANY], scratch_shapes...  3.08 us
    pallas_call x1, Pallas kernels, on_device(): call(weights, [((2, 32, 32, 128), kept_near)], 1, 8, in_specs=[HBM], scra...  3 us
    pallas_call x1, Pallas kernels, on_device(): call(middle, [((32, 8, 128), plain)], 4, in_specs=[VMEM] * 2 + [ANY] * 2,...  2.63 us
  transfers between devices with their start and end apart: 8, of which 5 were waited for; matrix products, arithmetic and copies ran while one was open for 0% of the time, Pallas kernels for 22%

profile of v6, /device:TPU:1, one launch (start us, length us, event | category | flops | bytes accessed | tf_op | source)
XLA Modules:
  0.0 78.6 jit_solution(15401106567811177471)
XLA Ops:
  0.0 3.8 %forward_z.1 = f32[8,16,8,128]{3,2,1,0:T(8,128)} custom-call(f32[128,16,256]{2,1,0:T(8,128)} %bitcast.5, bf16[128,256]{1,0:T(8,128)(2,1)} %constant.12.clone.table_ref), custom_call_target="tpu_custom_call" | custom-call | tf_op jit(solution)/shard_map/forward_z/pallas_call | solution.py:425
  3.8 7.5 %all-to-all-start = ((f32[8,16,8,128]{3,2,1,0:T(8,128)}), f32[8,16,8,128]{3,2,1,0:T(8,128)S(1)}, u32[]{:S(2)}, u32[]{:S(2)}) async-start(f32[8,16,8,128]{3,2,1,0:T(8,128)} %forward_z.1), calls=%async_computation | async-start | bytes 1048576 | tf_op jit(solution)/shard_map/all_to_all | solution.py:414
  11.3 0.0 copy-start.2
  11.3 7.2 %own_cells.1 = (f32[4,16,32,256]{3,2,1,0:T(8,128)S(1)}, f32[16,32,256]{2,1,0:T(8,128)}, f32[16,32,256]{2,1,0:T(8,128)}, f32[2,4,32,256]{3,2,1,0:T(8,128)}) custom-call(f32[128,16,256]{2,1,0:T(8,128)} %bitcast.6, f32[3,3,3,32]{3,2,1,0:T(4,128)} %bitcast.8, f32[32,32]{1,0:T(8,128)} %point_hbm.1, f32[1,32]{1,0:T(1,128)} %bitcast.10), custom_call_target="tpu_custom_call" | custom-call | flops 8000000000 | tf_op jit(solution)/shard_map/own_cells/pallas_call | solution.py:442
  18.5 3.4 %all-to-all-done.data_ref = f32[8,16,8,128]{3,2,1,0:T(8,128)S(1)} async-done(((f32[8,16,8,128]{3,2,1,0:T(8,128)}), f32[8,16,8,128]{3,2,1,0:T(8,128)S(1)}, u32[]{:S(2)}, u32[]{:S(2)}) %all-to-all-start) | async-done | bytes 524320 | tf_op jit(solution)/shard_map/all_to_all | solution.py:414
  22.0 0.0 copy-done.2
  22.0 1.0 %forward_y.1 = f32[32,8,128]{2,1,0:T(8,128)} custom-call(f32[8,16,8,128]{3,2,1,0:T(8,128)S(1)} %all-to-all-done.data_ref, bf16[2,64,256]{2,1,0:T(8,128)(2,1)S(1)} %copy-done.2), custom_call_target="tpu_custom_call" | custom-call | tf_op jit(solution)/shard_map/forward_y/pallas_call | solution.py:466
  23.0 10.5 %all-to-all-start.1 = ((f32[32,8,128]{2,1,0:T(8,128)}), f32[32,8,128]{2,1,0:T(8,128)S(1)}, u32[]{:S(2)}, u32[]{:S(2)}) async-start(f32[32,8,128]{2,1,0:T(8,128)} %forward_y.1), calls=%async_computation.1 | async-start | bytes 262144 | tf_op jit(solution)/shard_map/all_to_all | solution.py:414
  33.5 1.7 %collective-permute-start = (f32[16,32,256]{2,1,0:T(8,128)}, f32[16,32,256]{2,1,0:T(8,128)}, u32[]{:S(2)}, u32[]{:S(2)}) collective-permute-start(f32[16,32,256]{2,1,0:T(8,128)} %get-tuple-element.35), channel_id=1, source_target_pairs={{0,8},{8,16},{16,24},{24,32},{32,40},{40,48},{48,56},{56,64},{64,7... | collective-permute-start | bytes 1572872 | tf_op jit(solution)/shard_map/ppermute | solution.py:410
  35.2 0.0 collective-permute-start.1
  35.2 3.0 %weights.1.weight_ref = f32[2,32,32,128]{3,2,1,0:T(8,128)S(1)} custom-call(f32[2,32,128,32]{3,2,1,0:T(8,128)} %bitcast.7), custom_call_target="tpu_custom_call" | custom-call | flops 8000000000 | tf_op jit(solution)/shard_map/weights/pallas_call | solution.py:474
  38.2 4.8 %all-to-all-done.1.data_ref = f32[32,8,128]{2,1,0:T(8,128)S(1)} async-done(((f32[32,8,128]{2,1,0:T(8,128)}), f32[32,8,128]{2,1,0:T(8,128)S(1)}, u32[]{:S(2)}, u32[]{:S(2)}) %all-to-all-start.1) | async-done | bytes 131104 | tf_op jit(solution)/shard_map/all_to_all | solution.py:414
  43.0 2.6 %middle.1 = f32[32,8,128]{2,1,0:T(8,128)} custom-call(f32[32,8,128]{2,1,0:T(8,128)S(1)} %all-to-all-done.1.data_ref, f32[2,32,32,128]{3,2,1,0:T(8,128)S(1)} %weights.1.weight_ref, bf16[2,64,256]{2,1,0:T(8,128)(2,1)} %constant.14.clone.forward_hbm, bf16[2,256,64]{2,1,0:T(8,128)(2,1)} %constant.15.clone.inverse_hbm), custom_call_target="tpu_custom_call" | custom-call | tf_op jit(solution)/shard_map/middle/pallas_call | solution.py:483
  45.6 4.9 %all-to-all-start.2 = ((f32[32,8,128]{2,1,0:T(8,128)}), f32[32,8,128]{2,1,0:T(8,128)S(1)}, u32[]{:S(2)}, u32[]{:S(2)}) async-start(f32[32,8,128]{2,1,0:T(8,128)} %middle.1), calls=%async_computation.2 | async-start | bytes 262144 | tf_op jit(solution)/shard_map/all_to_all | solution.py:414
  50.5 0.0 collective-permute-done.before_ref.before_hbm
  50.5 0.2 collective-permute-done.1.after_ref.after_hbm
  50.7 0.0 copy-start
  50.7 1.1 %rims.1 = (f32[6,32,256]{2,1,0:T(8,128)S(1)}, f32[6,32,256]{2,1,0:T(8,128)S(1)}) custom-call(f32[2,4,32,256]{3,2,1,0:T(8,128)} %get-tuple-element.34.rows_ref, f32[16,32,256]{2,1,0:T(8,128)} %collective-permute-done.before_ref.before_hbm, f32[16,32,256]{2,1,0:T(8,128)} %collective-permute-done.1.after_ref.after_hbm), custom_call_target="tpu_custom_call" | custom-call | flops 2000000000 | tf_op jit(solution)/shard_map/rims/pallas_call | solution.py:498
  51.8 1.3 %collective-permute-start.2 = (f32[6,32,256]{2,1,0:T(8,128)S(1)}, f32[6,32,256]{2,1,0:T(8,128)S(1)}, u32[]{:S(2)}, u32[]{:S(2)}) collective-permute-start(f32[6,32,256]{2,1,0:T(8,128)S(1)} %get-tuple-element.39), channel_id=1, source_target_pairs={{0,1},{1,2},{2,3},{3,4},{4,5},{5,6},{6,7},{7,0},{8,9},{9,10},{10,1... | collective-permute-start | bytes 589832 | tf_op jit(solution)/shard_map/ppermute | solution.py:410
  53.1 3.9 %collective-permute-start.3 = (f32[6,32,256]{2,1,0:T(8,128)S(1)}, f32[6,32,256]{2,1,0:T(8,128)S(1)}, u32[]{:S(2)}, u32[]{:S(2)}) collective-permute-start(f32[6,32,256]{2,1,0:T(8,128)S(1)} %get-tuple-element.40), channel_id=1, source_target_pairs={{0,7},{1,0},{2,1},{3,2},{4,3},{5,4},{6,5},{7,6},{8,15},{9,8},{10,9... | collective-permute-start | bytes 589832 | tf_op jit(solution)/shard_map/ppermute | solution.py:410
  57.0 2.9 %all-to-all-done.2.data_ref = f32[32,8,128]{2,1,0:T(8,128)S(1)} async-done(((f32[32,8,128]{2,1,0:T(8,128)}), f32[32,8,128]{2,1,0:T(8,128)S(1)}, u32[]{:S(2)}, u32[]{:S(2)}) %all-to-all-start.2) | async-done | bytes 131104 | tf_op jit(solution)/shard_map/all_to_all | solution.py:414
  59.9 0.0 copy-done
  59.9 1.2 %inverse_y.1 = f32[8,16,8,128]{3,2,1,0:T(8,128)} custom-call(f32[32,8,128]{2,1,0:T(8,128)S(1)} %all-to-all-done.2.data_ref, bf16[2,256,64]{2,1,0:T(8,128)(2,1)S(1)} %copy-done), custom_call_target="tpu_custom_call" | custom-call | tf_op jit(solution)/shard_map/inverse_y/pallas_call | solution.py:509
  61.0 3.7 %all-to-all-start.3 = ((f32[8,16,8,128]{3,2,1,0:T(8,128)}), f32[8,16,8,128]{3,2,1,0:T(8,128)S(1)}, u32[]{:S(2)}, u32[]{:S(2)}) async-start(f32[8,16,8,128]{3,2,1,0:T(8,128)} %inverse_y.1), calls=%async_computation.3 | async-start | bytes 1048576 | tf_op jit(solution)/shard_map/all_to_all | solution.py:414
  64.7 0.0 copy-start.1
  64.7 0.0 collective-permute-done.2.left_ref
  64.7 0.0 collective-permute-done.3.right_ref
  64.8 2.4 %edge_cells.1.base_ref = f32[4,16,32,256]{3,2,1,0:T(8,128)S(1)} custom-call(f32[4,16,32,256]{3,2,1,0:T(8,128)S(1)} %get-tuple-element.42.base_ref, f32[16,32,256]{2,1,0:T(8,128)} %collective-permute-done.before_ref.before_hbm, f32[16,32,256]{2,1,0:T(8,128)} %collective-permute-done.1.after_ref.after_hbm, ...), custom_call_target="tpu_custom_call", output_to_operand_aliasing={{}: (0, {})} | custom-call | flops 40000000000 | tf_op jit(solution)/shard_map/edge_cells/pallas_call | solution.py:515
  67.2 8.2 %all-to-all-done.3.data_ref = f32[8,16,8,128]{3,2,1,0:T(8,128)S(1)} async-done(((f32[8,16,8,128]{3,2,1,0:T(8,128)}), f32[8,16,8,128]{3,2,1,0:T(8,128)S(1)}, u32[]{:S(2)}, u32[]{:S(2)}) %all-to-all-start.3) | async-done | bytes 524320 | tf_op jit(solution)/shard_map/all_to_all | solution.py:414
  75.4 0.0 copy-done.1
  75.4 3.1 %final.1 = f32[128,16,256]{2,1,0:T(8,128)} custom-call(f32[8,16,8,128]{3,2,1,0:T(8,128)S(1)} %all-to-all-done.3.data_ref, f32[4,16,32,256]{3,2,1,0:T(8,128)S(1)} %edge_cells.1.base_ref, bf16[2,64,256]{2,1,0:T(8,128)(2,1)S(1)} %copy-done.1), custom_call_target="tpu_custom_call" | custom-call | tf_op jit(solution)/shard_map/final/pallas_call | solution.py:531
Async XLA Ops:
  3.8 18.2 %all-to-all-start = ((f32[8,16,8,128]{3,2,1,0:T(8,128)}), f32[8,16,8,128]{3,2,1,0:T(8,128)S(1)}, u32[]{:S(2)}, u32[]{:S(2)}) async-start(f32[8,16,8,128]{3,2,1,0:T(8,128)} %forward_z.1), calls=%async_computation | async-start | bytes 1048576 | tf_op jit(solution)/shard_map/all_to_all | solution.py:414
  11.3 10.7 %copy-start.2 = (bf16[2,64,256]{2,1,0:T(8,128)(2,1)S(1)}, bf16[2,64,256]{2,1,0:T(8,128)(2,1)}, u32[]{:S(2)}) copy-start(bf16[2,64,256]{2,1,0:T(8,128)(2,1)} %constant.13.clone.table_ref) | copy-start | bytes 196612
  23.0 20.0 %all-to-all-start.1 = ((f32[32,8,128]{2,1,0:T(8,128)}), f32[32,8,128]{2,1,0:T(8,128)S(1)}, u32[]{:S(2)}, u32[]{:S(2)}) async-start(f32[32,8,128]{2,1,0:T(8,128)} %forward_y.1), calls=%async_computation.1 | async-start | bytes 262144 | tf_op jit(solution)/shard_map/all_to_all | solution.py:414
  33.5 17.0 %collective-permute-start = (f32[16,32,256]{2,1,0:T(8,128)}, f32[16,32,256]{2,1,0:T(8,128)}, u32[]{:S(2)}, u32[]{:S(2)}) collective-permute-start(f32[16,32,256]{2,1,0:T(8,128)} %get-tuple-element.35), channel_id=1, source_target_pairs={{0,8},{8,16},{16,24},{24,32},{32,40},{40,48},{48,56},{56,64},{64,7... | collective-permute-start | bytes 1572872 | tf_op jit(solution)/shard_map/ppermute | solution.py:410
  35.2 15.5 %collective-permute-start.1 = (f32[16,32,256]{2,1,0:T(8,128)}, f32[16,32,256]{2,1,0:T(8,128)}, u32[]{:S(2)}, u32[]{:S(2)}) collective-permute-start(f32[16,32,256]{2,1,0:T(8,128)} %get-tuple-element.36), channel_id=1, source_target_pairs={{0,248},{8,0},{16,8},{24,16},{32,24},{40,32},{48,40},{56,48},{64,5... | collective-permute-start | bytes 1572872 | tf_op jit(solution)/shard_map/ppermute | solution.py:410
  45.6 14.2 %all-to-all-start.2 = ((f32[32,8,128]{2,1,0:T(8,128)}), f32[32,8,128]{2,1,0:T(8,128)S(1)}, u32[]{:S(2)}, u32[]{:S(2)}) async-start(f32[32,8,128]{2,1,0:T(8,128)} %middle.1), calls=%async_computation.2 | async-start | bytes 262144 | tf_op jit(solution)/shard_map/all_to_all | solution.py:414
  50.7 9.1 %copy-start = (bf16[2,256,64]{2,1,0:T(8,128)(2,1)S(1)}, bf16[2,256,64]{2,1,0:T(8,128)(2,1)}, u32[]{:S(2)}) copy-start(bf16[2,256,64]{2,1,0:T(8,128)(2,1)} %constant.16.clone.table_ref) | copy-start | bytes 196612
  51.8 12.9 %collective-permute-start.2 = (f32[6,32,256]{2,1,0:T(8,128)S(1)}, f32[6,32,256]{2,1,0:T(8,128)S(1)}, u32[]{:S(2)}, u32[]{:S(2)}) collective-permute-start(f32[6,32,256]{2,1,0:T(8,128)S(1)} %get-tuple-element.39), channel_id=1, source_target_pairs={{0,1},{1,2},{2,3},{3,4},{4,5},{5,6},{6,7},{7,0},{8,9},{9,10},{10,1... | collective-permute-start | bytes 589832 | tf_op jit(solution)/shard_map/ppermute | solution.py:410
  53.1 11.6 %collective-permute-start.3 = (f32[6,32,256]{2,1,0:T(8,128)S(1)}, f32[6,32,256]{2,1,0:T(8,128)S(1)}, u32[]{:S(2)}, u32[]{:S(2)}) collective-permute-start(f32[6,32,256]{2,1,0:T(8,128)S(1)} %get-tuple-element.40), channel_id=1, source_target_pairs={{0,7},{1,0},{2,1},{3,2},{4,3},{5,4},{6,5},{7,6},{8,15},{9,8},{10,9... | collective-permute-start | bytes 589832 | tf_op jit(solution)/shard_map/ppermute | solution.py:410
  61.0 14.3 %all-to-all-start.3 = ((f32[8,16,8,128]{3,2,1,0:T(8,128)}), f32[8,16,8,128]{3,2,1,0:T(8,128)S(1)}, u32[]{:S(2)}, u32[]{:S(2)}) async-start(f32[8,16,8,128]{3,2,1,0:T(8,128)} %inverse_y.1), calls=%async_computation.3 | async-start | bytes 1048576 | tf_op jit(solution)/shard_map/all_to_all | solution.py:414
  64.7 10.6 %copy-start.1 = (bf16[2,64,256]{2,1,0:T(8,128)(2,1)S(1)}, bf16[2,64,256]{2,1,0:T(8,128)(2,1)}, u32[]{:S(2)}) copy-start(bf16[2,64,256]{2,1,0:T(8,128)(2,1)} %constant.17.clone.table_ref) | copy-start | bytes 196612

commit v7 on v6

--- a/solution.py
+++ b/solution.py
@@ -141,13 +141,10 @@
 
 
 def middle(
-    data_ref, weight_ref, forward_hbm, inverse_hbm, out_ref, forward_ref, inverse_ref, sems
+    data_ref, weight_ref, forward_ref, inverse_hbm, out_ref, inverse_ref, sem
 ):
-    first_load = pltpu.make_async_copy(forward_hbm, forward_ref, sems.at[0])
-    load = pltpu.make_async_copy(inverse_hbm, inverse_ref, sems.at[1])
-    first_load.start()
+    load = pltpu.make_async_copy(inverse_hbm, inverse_ref, sem)
     load.start()
-    first_load.wait()
     spec = table_dot(forward_ref, data_ref[...].reshape(256, 128))
     spec_re, spec_im = spec[:32], spec[32:]
     lane = lax.broadcasted_iota(jnp.int32, (32, 128), 1)
@@ -468,9 +465,6 @@
     )
 
     yall = exchange(ychunks, "gx")
-    first, last, pairs, _ = lax.optimization_barrier((first, last, spec_weight, ychunks))
-    before = shifted("gx", far(last), 1)
-    after = shifted("gx", far(first), -1)
     (packed,) = call(
         weights,
         [((2, 32, 32, 128), kept_near)],
@@ -478,19 +472,19 @@
         8,
         in_specs=[HBM],
         scratch_shapes=[pltpu.VMEM((2, 32, 128, 32), F32), dma((8,))],
-    )(far(pairs.reshape(2, 32, 128, 32)))
+    )(far(after_all(spec_weight, ychunks).reshape(2, 32, 128, 32)))
+    first, last, packed = lax.optimization_barrier((first, last, packed))
+    before = shifted("gx", far(last), 1)
+    after = shifted("gx", far(first), -1)
     yall, packed = lax.optimization_barrier((yall, packed))
     (xchunks,) = call(
         middle,
         [((32, 8, 128), plain)],
         4,
-        in_specs=[VMEM] * 2 + [ANY] * 2,
-        scratch_shapes=[
-            pltpu.VMEM((2, 64, 256), BF16),
-            pltpu.VMEM((2, 256, 64), BF16),
-            dma((2,)),
-        ],
-    )(near(yall), near(packed), far(jnp.asarray(tab["fx"])), far(jnp.asarray(tab["ix"])))
+        3,
+        in_specs=[VMEM] * 3 + [ANY],
+        scratch_shapes=[pltpu.VMEM((2, 256, 64), BF16), dma],
+    )(near(yall), near(packed), near(jnp.asarray(tab["fx"])), far(jnp.asarray(tab["ix"])))
 
     xall = exchange(xchunks, "gx")
     before, after, _ = lax.optimization_barrier((before, after, xchunks))

time: 79.1 us -> 78.7 us (level)
    ppermute x4, waiting for transfers between devices: 0.23 us -> 3.33 us  [shifted(): lax.ppermute(value, axis, [(i, (i + step) % count) for i in range(count)])]
    all_to_all x4, waiting for transfers between devices: 19.3 us -> 16.2 us  [exchange(): return lax.all_to_all(value, axis, split_axis=0, concat_axis=0, tiled=True)]
  transfers between devices with their start and end apart: 8 -> 8, of which waited for: 5 -> 6; matrix products, arithmetic and copies ran while one was open for 0% -> 0% of each run, Pallas kernels for 22% -> 22%
where the time goes in v7:
time: 78.7 us; the launch traced here: 78.2 us
  starting transfers between devices  33.6 us (43%)
  Pallas kernels  24.7 us (31%)
  waiting for transfers between devices  19.5 us (25%)
    all_to_all x4, starting transfers between devices, exchange(): return lax.all_to_all(value, axis, split_axis=0, concat_axis=0, tiled=True)  26.8 us
    all_to_all x4, waiting for transfers between devices, exchange(): return lax.all_to_all(value, axis, split_axis=0, concat_axis=0, tiled=True)  16.2 us
    pallas_call x1, Pallas kernels, on_device(): call(own_cells, [((4, 16, 32, 256), kept_near), ((16, 32, 256), pltpu.HBM...  7.22 us
    ppermute x4, starting transfers between devices, shifted(): lax.ppermute(value, axis, [(i, (i + step) % count) for i in range(count)])  6.87 us
    pallas_call x1, Pallas kernels, on_device(): call(forward_z, [((8, 16, 8, 128), plain)], 2, in_specs=[HBM] * 2, out_sp...  3.81 us
    ppermute x4, waiting for transfers between devices, shifted(): lax.ppermute(value, axis, [(i, (i + step) % count) for i in range(count)])  3.33 us
    pallas_call x1, Pallas kernels, on_device(): call(final, [((128, 16, 256), plain)], 3, out_specs=[ANY], scratch_shapes...  3.08 us
    pallas_call x1, Pallas kernels, on_device(): call(weights, [((2, 32, 32, 128), kept_near)], 1, 8, in_specs=[HBM], scra...  3.03 us
  transfers between devices with their start and end apart: 8, of which 6 were waited for; matrix products, arithmetic and copies ran while one was open for 0% of the time, Pallas kernels for 22%

profile of v7, /device:TPU:1, one launch (start us, length us, event | category | flops | bytes accessed | tf_op | source)
XLA Modules:
  0.0 78.2 jit_solution(16003989988827343037)
XLA Ops:
  0.0 3.8 %forward_z.1 = f32[8,16,8,128]{3,2,1,0:T(8,128)} custom-call(f32[128,16,256]{2,1,0:T(8,128)} %bitcast.5, bf16[128,256]{1,0:T(8,128)(2,1)} %constant.12.clone.table_ref), custom_call_target="tpu_custom_call" | custom-call | tf_op jit(solution)/shard_map/forward_z/pallas_call | solution.py:422
  3.8 7.5 %all-to-all-start = ((f32[8,16,8,128]{3,2,1,0:T(8,128)}), f32[8,16,8,128]{3,2,1,0:T(8,128)S(1)}, u32[]{:S(2)}, u32[]{:S(2)}) async-start(f32[8,16,8,128]{3,2,1,0:T(8,128)} %forward_z.1), calls=%async_computation | async-start | bytes 1048576 | tf_op jit(solution)/shard_map/all_to_all | solution.py:411
  11.3 0.0 copy-start.2
  11.3 7.2 %own_cells.1 = (f32[4,16,32,256]{3,2,1,0:T(8,128)S(1)}, f32[16,32,256]{2,1,0:T(8,128)}, f32[16,32,256]{2,1,0:T(8,128)}, f32[2,4,32,256]{3,2,1,0:T(8,128)}) custom-call(f32[128,16,256]{2,1,0:T(8,128)} %bitcast.6, f32[3,3,3,32]{3,2,1,0:T(4,128)} %bitcast.8, f32[32,32]{1,0:T(8,128)} %point_hbm.1, f32[1,32]{1,0:T(1,128)} %bitcast.10), custom_call_target="tpu_custom_call" | custom-call | flops 8000000000 | tf_op jit(solution)/shard_map/own_cells/pallas_call | solution.py:439
  18.5 3.4 %all-to-all-done.data_ref = f32[8,16,8,128]{3,2,1,0:T(8,128)S(1)} async-done(((f32[8,16,8,128]{3,2,1,0:T(8,128)}), f32[8,16,8,128]{3,2,1,0:T(8,128)S(1)}, u32[]{:S(2)}, u32[]{:S(2)}) %all-to-all-start) | async-done | bytes 524320 | tf_op jit(solution)/shard_map/all_to_all | solution.py:411
  22.0 0.0 copy-done.2
  22.0 1.0 %forward_y.1 = f32[32,8,128]{2,1,0:T(8,128)} custom-call(f32[8,16,8,128]{3,2,1,0:T(8,128)S(1)} %all-to-all-done.data_ref, bf16[2,64,256]{2,1,0:T(8,128)(2,1)S(1)} %copy-done.2), custom_call_target="tpu_custom_call" | custom-call | tf_op jit(solution)/shard_map/forward_y/pallas_call | solution.py:463
  23.0 10.5 %all-to-all-start.1 = ((f32[32,8,128]{2,1,0:T(8,128)}), f32[32,8,128]{2,1,0:T(8,128)S(1)}, u32[]{:S(2)}, u32[]{:S(2)}) async-start(f32[32,8,128]{2,1,0:T(8,128)} %forward_y.1), calls=%async_computation.1 | async-start | bytes 262144 | tf_op jit(solution)/shard_map/all_to_all | solution.py:411
  33.5 0.0 copy-start.3
  33.5 3.0 %weights.1.weight_ref = f32[2,32,32,128]{3,2,1,0:T(8,128)S(1)} custom-call(f32[2,32,128,32]{3,2,1,0:T(8,128)} %bitcast.7), custom_call_target="tpu_custom_call" | custom-call | flops 8000000000 | tf_op jit(solution)/shard_map/weights/pallas_call | solution.py:468
  36.6 1.7 %collective-permute-start = (f32[16,32,256]{2,1,0:T(8,128)}, f32[16,32,256]{2,1,0:T(8,128)}, u32[]{:S(2)}, u32[]{:S(2)}) collective-permute-start(f32[16,32,256]{2,1,0:T(8,128)} %get-tuple-element.37), channel_id=1, source_target_pairs={{0,8},{8,16},{16,24},{24,32},{32,40},{40,48},{48,56},{56,64},{64,7... | collective-permute-start | bytes 1572872 | tf_op jit(solution)/shard_map/ppermute | solution.py:407
  38.3 0.0 collective-permute-start.1
  38.3 4.5 %all-to-all-done.1.data_ref = f32[32,8,128]{2,1,0:T(8,128)S(1)} async-done(((f32[32,8,128]{2,1,0:T(8,128)}), f32[32,8,128]{2,1,0:T(8,128)S(1)}, u32[]{:S(2)}, u32[]{:S(2)}) %all-to-all-start.1) | async-done | bytes 131104 | tf_op jit(solution)/shard_map/all_to_all | solution.py:411
  42.8 0.0 copy-done.3
  42.8 1.9 %middle.1 = f32[32,8,128]{2,1,0:T(8,128)} custom-call(f32[32,8,128]{2,1,0:T(8,128)S(1)} %all-to-all-done.1.data_ref, f32[2,32,32,128]{3,2,1,0:T(8,128)S(1)} %weights.1.weight_ref, bf16[2,64,256]{2,1,0:T(8,128)(2,1)S(1)} %copy-done.3, bf16[2,256,64]{2,1,0:T(8,128)(2,1)} %constant.15.clone.inverse_hbm), custom_call_target="tpu_custom_call" | custom-call | flops 3000000000 | tf_op jit(solution)/shard_map/middle/pallas_call | solution.py:480
  44.8 5.1 %all-to-all-start.2 = ((f32[32,8,128]{2,1,0:T(8,128)}), f32[32,8,128]{2,1,0:T(8,128)S(1)}, u32[]{:S(2)}, u32[]{:S(2)}) async-start(f32[32,8,128]{2,1,0:T(8,128)} %middle.1), calls=%async_computation.2 | async-start | bytes 262144 | tf_op jit(solution)/shard_map/all_to_all | solution.py:411
  49.8 0.8 collective-permute-done.before_ref.before_hbm
  50.6 2.4 %collective-permute-done.1.after_ref.after_hbm = f32[16,32,256]{2,1,0:T(8,128)} collective-permute-done((f32[16,32,256]{2,1,0:T(8,128)}, f32[16,32,256]{2,1,0:T(8,128)}, u32[]{:S(2)}, u32[]{:S(2)}) %collective-permute-start.1) | collective-permute-done | bytes 524320 | tf_op jit(solution)/shard_map/ppermute | solution.py:407
  53.1 0.0 copy-start
  53.1 1.1 %rims.1 = (f32[6,32,256]{2,1,0:T(8,128)S(1)}, f32[6,32,256]{2,1,0:T(8,128)S(1)}) custom-call(f32[2,4,32,256]{3,2,1,0:T(8,128)} %get-tuple-element.36.rows_ref, f32[16,32,256]{2,1,0:T(8,128)} %collective-permute-done.before_ref.before_hbm, f32[16,32,256]{2,1,0:T(8,128)} %collective-permute-done.1.after_ref.after_hbm), custom_call_target="tpu_custom_call" | custom-call | flops 2000000000 | tf_op jit(solution)/shard_map/rims/pallas_call | solution.py:492
  54.2 1.3 %collective-permute-start.2 = (f32[6,32,256]{2,1,0:T(8,128)S(1)}, f32[6,32,256]{2,1,0:T(8,128)S(1)}, u32[]{:S(2)}, u32[]{:S(2)}) collective-permute-start(f32[6,32,256]{2,1,0:T(8,128)S(1)} %get-tuple-element.41), channel_id=1, source_target_pairs={{0,1},{1,2},{2,3},{3,4},{4,5},{5,6},{6,7},{7,0},{8,9},{9,10},{10,1... | collective-permute-start | bytes 589832 | tf_op jit(solution)/shard_map/ppermute | solution.py:407
  55.4 3.9 %collective-permute-start.3 = (f32[6,32,256]{2,1,0:T(8,128)S(1)}, f32[6,32,256]{2,1,0:T(8,128)S(1)}, u32[]{:S(2)}, u32[]{:S(2)}) collective-permute-start(f32[6,32,256]{2,1,0:T(8,128)S(1)} %get-tuple-element.42), channel_id=1, source_target_pairs={{0,7},{1,0},{2,1},{3,2},{4,3},{5,4},{6,5},{7,6},{8,15},{9,8},{10,9... | collective-permute-start | bytes 589832 | tf_op jit(solution)/shard_map/ppermute | solution.py:407
  59.3 0.0 all-to-all-done.2.data_ref
  59.3 0.0 copy-done
  59.3 1.2 %inverse_y.1 = f32[8,16,8,128]{3,2,1,0:T(8,128)} custom-call(f32[32,8,128]{2,1,0:T(8,128)S(1)} %all-to-all-done.2.data_ref, bf16[2,256,64]{2,1,0:T(8,128)(2,1)S(1)} %copy-done), custom_call_target="tpu_custom_call" | custom-call | tf_op jit(solution)/shard_map/inverse_y/pallas_call | solution.py:503
  60.5 3.7 %all-to-all-start.3 = ((f32[8,16,8,128]{3,2,1,0:T(8,128)}), f32[8,16,8,128]{3,2,1,0:T(8,128)S(1)}, u32[]{:S(2)}, u32[]{:S(2)}) async-start(f32[8,16,8,128]{3,2,1,0:T(8,128)} %inverse_y.1), calls=%async_computation.3 | async-start | bytes 1048576 | tf_op jit(solution)/shard_map/all_to_all | solution.py:411
  64.2 0.0 copy-start.1
  64.2 0.1 collective-permute-done.2.left_ref
  64.3 0.0 collective-permute-done.3.right_ref
  64.3 2.4 %edge_cells.1.base_ref = f32[4,16,32,256]{3,2,1,0:T(8,128)S(1)} custom-call(f32[4,16,32,256]{3,2,1,0:T(8,128)S(1)} %get-tuple-element.44.base_ref, f32[16,32,256]{2,1,0:T(8,128)} %collective-permute-done.before_ref.before_hbm, f32[16,32,256]{2,1,0:T(8,128)} %collective-permute-done.1.after_ref.after_hbm, ...), custom_call_target="tpu_custom_call", output_to_operand_aliasing={{}: (0, {})} | custom-call | flops 40000000000 | tf_op jit(solution)/shard_map/edge_cells/pallas_call | solution.py:509
  66.7 8.2 %all-to-all-done.3.data_ref = f32[8,16,8,128]{3,2,1,0:T(8,128)S(1)} async-done(((f32[8,16,8,128]{3,2,1,0:T(8,128)}), f32[8,16,8,128]{3,2,1,0:T(8,128)S(1)}, u32[]{:S(2)}, u32[]{:S(2)}) %all-to-all-start.3) | async-done | bytes 524320 | tf_op jit(solution)/shard_map/all_to_all | solution.py:411
  74.9 0.0 copy-done.1
  74.9 3.1 %final.1 = f32[128,16,256]{2,1,0:T(8,128)} custom-call(f32[8,16,8,128]{3,2,1,0:T(8,128)S(1)} %all-to-all-done.3.data_ref, f32[4,16,32,256]{3,2,1,0:T(8,128)S(1)} %edge_cells.1.base_ref, bf16[2,64,256]{2,1,0:T(8,128)(2,1)S(1)} %copy-done.1), custom_call_target="tpu_custom_call" | custom-call | tf_op jit(solution)/shard_map/final/pallas_call | solution.py:525
Async XLA Ops:
  3.8 18.2 %all-to-all-start = ((f32[8,16,8,128]{3,2,1,0:T(8,128)}), f32[8,16,8,128]{3,2,1,0:T(8,128)S(1)}, u32[]{:S(2)}, u32[]{:S(2)}) async-start(f32[8,16,8,128]{3,2,1,0:T(8,128)} %forward_z.1), calls=%async_computation | async-start | bytes 1048576 | tf_op jit(solution)/shard_map/all_to_all | solution.py:411
  11.3 10.7 %copy-start.2 = (bf16[2,64,256]{2,1,0:T(8,128)(2,1)S(1)}, bf16[2,64,256]{2,1,0:T(8,128)(2,1)}, u32[]{:S(2)}) copy-start(bf16[2,64,256]{2,1,0:T(8,128)(2,1)} %constant.13.clone.table_ref) | copy-start | bytes 196612
  23.0 19.8 %all-to-all-start.1 = ((f32[32,8,128]{2,1,0:T(8,128)}), f32[32,8,128]{2,1,0:T(8,128)S(1)}, u32[]{:S(2)}, u32[]{:S(2)}) async-start(f32[32,8,128]{2,1,0:T(8,128)} %forward_y.1), calls=%async_computation.1 | async-start | bytes 262144 | tf_op jit(solution)/shard_map/all_to_all | solution.py:411
  33.5 9.3 %copy-start.3 = (bf16[2,64,256]{2,1,0:T(8,128)(2,1)S(1)}, bf16[2,64,256]{2,1,0:T(8,128)(2,1)}, u32[]{:S(2)}) copy-start(bf16[2,64,256]{2,1,0:T(8,128)(2,1)} %constant.14.clone.forward_ref) | copy-start | bytes 196612
  36.6 14.0 %collective-permute-start = (f32[16,32,256]{2,1,0:T(8,128)}, f32[16,32,256]{2,1,0:T(8,128)}, u32[]{:S(2)}, u32[]{:S(2)}) collective-permute-start(f32[16,32,256]{2,1,0:T(8,128)} %get-tuple-element.37), channel_id=1, source_target_pairs={{0,8},{8,16},{16,24},{24,32},{32,40},{40,48},{48,56},{56,64},{64,7... | collective-permute-start | bytes 1572872 | tf_op jit(solution)/shard_map/ppermute | solution.py:407
  38.3 14.8 %collective-permute-start.1 = (f32[16,32,256]{2,1,0:T(8,128)}, f32[16,32,256]{2,1,0:T(8,128)}, u32[]{:S(2)}, u32[]{:S(2)}) collective-permute-start(f32[16,32,256]{2,1,0:T(8,128)} %get-tuple-element.38), channel_id=1, source_target_pairs={{0,248},{8,0},{16,8},{24,16},{32,24},{40,32},{48,40},{56,48},{64,5... | collective-permute-start | bytes 1572872 | tf_op jit(solution)/shard_map/ppermute | solution.py:407
  44.8 14.6 %all-to-all-start.2 = ((f32[32,8,128]{2,1,0:T(8,128)}), f32[32,8,128]{2,1,0:T(8,128)S(1)}, u32[]{:S(2)}, u32[]{:S(2)}) async-start(f32[32,8,128]{2,1,0:T(8,128)} %middle.1), calls=%async_computation.2 | async-start | bytes 262144 | tf_op jit(solution)/shard_map/all_to_all | solution.py:411
  53.1 6.3 %copy-start = (bf16[2,256,64]{2,1,0:T(8,128)(2,1)S(1)}, bf16[2,256,64]{2,1,0:T(8,128)(2,1)}, u32[]{:S(2)}) copy-start(bf16[2,256,64]{2,1,0:T(8,128)(2,1)} %constant.16.clone.table_ref) | copy-start | bytes 196612
  54.2 10.1 %collective-permute-start.2 = (f32[6,32,256]{2,1,0:T(8,128)S(1)}, f32[6,32,256]{2,1,0:T(8,128)S(1)}, u32[]{:S(2)}, u32[]{:S(2)}) collective-permute-start(f32[6,32,256]{2,1,0:T(8,128)S(1)} %get-tuple-element.41), channel_id=1, source_target_pairs={{0,1},{1,2},{2,3},{3,4},{4,5},{5,6},{6,7},{7,0},{8,9},{9,10},{10,1... | collective-permute-start | bytes 589832 | tf_op jit(solution)/shard_map/ppermute | solution.py:407
  55.4 8.9 %collective-permute-start.3 = (f32[6,32,256]{2,1,0:T(8,128)S(1)}, f32[6,32,256]{2,1,0:T(8,128)S(1)}, u32[]{:S(2)}, u32[]{:S(2)}) collective-permute-start(f32[6,32,256]{2,1,0:T(8,128)S(1)} %get-tuple-element.42), channel_id=1, source_target_pairs={{0,7},{1,0},{2,1},{3,2},{4,3},{5,4},{6,5},{7,6},{8,15},{9,8},{10,9... | collective-permute-start | bytes 589832 | tf_op jit(solution)/shard_map/ppermute | solution.py:407
  60.5 14.5 %all-to-all-start.3 = ((f32[8,16,8,128]{3,2,1,0:T(8,128)}), f32[8,16,8,128]{3,2,1,0:T(8,128)S(1)}, u32[]{:S(2)}, u32[]{:S(2)}) async-start(f32[8,16,8,128]{3,2,1,0:T(8,128)} %inverse_y.1), calls=%async_computation.3 | async-start | bytes 1048576 | tf_op jit(solution)/shard_map/all_to_all | solution.py:411
  64.2 10.8 %copy-start.1 = (bf16[2,64,256]{2,1,0:T(8,128)(2,1)S(1)}, bf16[2,64,256]{2,1,0:T(8,128)(2,1)}, u32[]{:S(2)}) copy-start(bf16[2,64,256]{2,1,0:T(8,128)(2,1)} %constant.17.clone.table_ref) | copy-start | bytes 196612

commit v8 on v7

--- a/solution.py
+++ b/solution.py
@@ -266,7 +266,7 @@
 
 
 def own_cells(
-    cells_ref, dw_hbm, point_hbm, bias_hbm, out_ref, first_ref, last_ref, rim_ref,
+    cells_ref, dw_hbm, point_hbm, bias_hbm, out_ref, first_ref, third_ref, last_ref, rim_ref,
     held, planes, tap_ref, dw_ref, point_ref, bias_ref, sems, small
 ):
     loads = [
@@ -293,14 +293,15 @@
         value = mm(point, jnp.concatenate([high, high, low], axis=0)) + bias
         for tile in range(4):
             chans = slice(8 * tile, 8 * tile + 8)
-            for x in range(4):
+            for x in range(3):
                 sums = [[None, None] for _ in range(3)]
-                for a in range(max(0, 1 - x), min(3, 5 - x)):
+                for a in range(max(0, 1 - x), 3):
                     for b in shifts:
                         load = lambda lanes: planes[x + a - 1, y + b - 1, chans, lanes]
                         add_taps(sums, tap_ref, chans, 9 * a + 3 * b, load)
                 own = 32 * x + 8 * tile
                 out_ref[x, y, chans, :] = value[own : own + 8] + shift_sum(sums)
+        out_ref[3, y] = value[96:]
 
     def body(y, carry):
         line(y, (0, 1, 2))
@@ -318,6 +319,7 @@
     fill(1)
     moves = [
         (planes.at[0], first_ref),
+        (planes.at[2], third_ref),
         (planes.at[3], last_ref),
         (planes.at[:, 0], rim_ref.at[0]),
         (planes.at[:, 15], rim_ref.at[1]),
@@ -332,10 +334,16 @@
 
 
 def edge_cells(
-    base_ref, before_hbm, after_hbm, left_ref, right_ref, dw_hbm,
-    out_ref, before_ref, after_ref, tap_ref, dw_ref, sems
+    base_ref, before_hbm, third_hbm, last_hbm, after_hbm, left_ref, right_ref, dw_hbm,
+    out_ref, before_ref, third_ref, last_ref, after_ref, tap_ref, dw_ref, sems
 ):
-    moves = [(dw_hbm, dw_ref), (before_hbm, before_ref), (after_hbm, after_ref)]
+    moves = [
+        (dw_hbm, dw_ref),
+        (before_hbm, before_ref),
+        (third_hbm, third_ref),
+        (last_hbm, last_ref),
+        (after_hbm, after_ref),
+    ]
     copies = [
         pltpu.make_async_copy(src, dst, sems.at[i]) for i, (src, dst) in enumerate(moves)
     ]
@@ -353,7 +361,7 @@
                 out_ref[x, y, chans, :] = base_ref[x, y, chans, :] + shift_sum(sums)
     wait_all(copies[1:])
 
-    def line(y, before_rows, after_rows):
+    def line(y, before_rows, after_rows, shifts):
         for a, x, rows in ((0, 0, before_rows), (2, 3, after_rows)):
             for tile in range(4):
                 chans = slice(8 * tile, 8 * tile + 8)
@@ -362,6 +370,10 @@
                     plane, at = rows[b]
                     load = lambda lanes: plane[at, chans, lanes]
                     add_taps(sums, tap_ref, chans, 9 * a + 3 * b, load)
+                for own, plane in enumerate((third_ref, last_ref) if x == 3 else ()):
+                    for b in shifts:
+                        load = lambda lanes: plane[y + b - 1, chans, lanes]
+                        add_taps(sums, tap_ref, chans, 9 * own + 3 * b, load)
                 out_ref[x, y, chans, :] = out_ref[x, y, chans, :] + shift_sum(sums)
 
     def near_rows(plane, edge, y):
@@ -370,12 +382,13 @@
         return [low, (plane, y), high]
 
     def body(y, carry):
-        line(y, *([(plane, y + b - 1) for b in range(3)] for plane in (before_ref, after_ref)))
+        rows = [[(plane, y + b - 1) for b in range(3)] for plane in (before_ref, after_ref)]
+        line(y, *rows, (0, 1, 2))
         return carry
 
     lax.fori_loop(1, 15, body, 0, unroll=2)
-    for y in (0, 15):
-        line(y, near_rows(before_ref, 0, y), near_rows(after_ref, 5, y))
+    for y, shifts in ((0, (1, 2)), (15, (0, 1))):
+        line(y, near_rows(before_ref, 0, y), near_rows(after_ref, 5, y), shifts)
 
 
 VMEM = pl.BlockSpec(memory_space=pltpu.VMEM)
@@ -436,10 +449,11 @@
     taps = dw_kernel.transpose(1, 2, 3, 0)
 
     zall = exchange(zchunks, "gy")
-    base, first, last, own_rims = call(
+    base, first, third, last, own_rims = call(
         own_cells,
         [
             ((4, 16, 32, 256), kept_near),
+            ((16, 32, 256), pltpu.HBM),
             ((16, 32, 256), pltpu.HBM),
             ((16, 32, 256), pltpu.HBM),
             ((2, 4, 32, 256), pltpu.HBM),
@@ -447,7 +461,7 @@
         4,
         8,
         in_specs=[HBM] * 4,
-        out_specs=[VMEM] + [HBM] * 3,
+        out_specs=[VMEM] + [HBM] * 4,
         scratch_shapes=[
             pltpu.VMEM((2, 2, 128, 8, 128), F32),
             pltpu.VMEM((4, 16, 32, 256), F32),
@@ -456,7 +470,7 @@
             pltpu.VMEM((32, 32), F32),
             pltpu.VMEM((1, 32), F32),
             dma((2, 2)),
-            dma((7,)),
+            dma((8,)),
         ],
     )(far(after_all(cells, zchunks)), far(taps), far(point_weight), far(bias.reshape(1, 32)))
     zall, base = lax.optimization_barrier((zall, base))
@@ -509,18 +523,15 @@
     (base,) = call(
         edge_cells,
         [((4, 16, 32, 256), kept_near)],
-        6,
+        8,
         40,
-        in_specs=[VMEM] + [ANY] * 2 + [VMEM] * 2 + [ANY],
-        scratch_shapes=[
-            pltpu.VMEM((16, 32, 256), F32),
-            pltpu.VMEM((16, 32, 256), F32),
-            pltpu.VMEM((27, 32, 128), F32),
-            pltpu.VMEM((3, 3, 3, 32), F32),
-            dma((3,)),
-        ],
+        in_specs=[VMEM] + [ANY] * 4 + [VMEM] * 2 + [ANY],
+        scratch_shapes=[pltpu.VMEM((16, 32, 256), F32)] * 4
+        + [pltpu.VMEM((27, 32, 128), F32), pltpu.VMEM((3, 3, 3, 32), F32), dma((5,))],
         input_output_aliases={0: 0},
-    )(near(base), before, after, near(left), near(right), far(taps))
+    )(
+        near(base), before, far(third), far(last), after, near(left), near(right), far(taps)
+    )
     ball, base = lax.optimization_barrier((ball, base))
     (out,) = call(
         final,

time: 78.7 us -> 77.9 us (0.990)
  no operation moved by 1% of the time
where the time goes in v8:
time: 77.9 us; the launch traced here: 77.4 us
  starting transfers between devices  33.2 us (43%)
  Pallas kernels  24.7 us (32%)
  waiting for transfers between devices  19.3 us (25%)
    all_to_all x4, starting transfers between devices, exchange(): return lax.all_to_all(value, axis, split_axis=0, concat_axis=0, tiled=True)  26.1 us
    all_to_all x4, waiting for transfers between devices, exchange(): return lax.all_to_all(value, axis, split_axis=0, concat_axis=0, tiled=True)  15.6 us
    ppermute x4, starting transfers between devices, shifted(): lax.ppermute(value, axis, [(i, (i + step) % count) for i in range(count)])  7.01 us
    pallas_call x1, Pallas kernels, on_device(): call(own_cells, [((4, 16, 32, 256), kept_near), ((16, 32, 256), pltpu.HBM...  6.44 us
    pallas_call x1, Pallas kernels, on_device(): call(forward_z, [((8, 16, 8, 128), plain)], 2, in_specs=[HBM] * 2, out_sp...  3.81 us
    ppermute x4, waiting for transfers between devices, shifted(): lax.ppermute(value, axis, [(i, (i + step) % count) for i in range(count)])  3.67 us
    pallas_call x1, Pallas kernels, on_device(): call(edge_cells, [((4, 16, 32, 256), kept_near)], 8, 40, in_specs=[VMEM]...  3.16 us
    pallas_call x1, Pallas kernels, on_device(): call(final, [((128, 16, 256), plain)], 3, out_specs=[ANY], scratch_shapes...  3.08 us
  transfers between devices with their start and end apart: 8, of which 6 were waited for; matrix products, arithmetic and copies ran while one was open for 0% of the time, Pallas kernels for 22%

profile of v8, /device:TPU:1, one launch (start us, length us, event | category | flops | bytes accessed | tf_op | source)
XLA Modules:
  0.0 77.4 jit_solution(620537759681354355)
XLA Ops:
  0.0 3.8 %forward_z.1 = f32[8,16,8,128]{3,2,1,0:T(8,128)} custom-call(f32[128,16,256]{2,1,0:T(8,128)} %bitcast.5, bf16[128,256]{1,0:T(8,128)(2,1)} %constant.12.clone.table_ref), custom_call_target="tpu_custom_call" | custom-call | tf_op jit(solution)/shard_map/forward_z/pallas_call | solution.py:435
  3.8 7.5 %all-to-all-start = ((f32[8,16,8,128]{3,2,1,0:T(8,128)}), f32[8,16,8,128]{3,2,1,0:T(8,128)S(1)}, u32[]{:S(2)}, u32[]{:S(2)}) async-start(f32[8,16,8,128]{3,2,1,0:T(8,128)} %forward_z.1), calls=%async_computation | async-start | bytes 1048576 | tf_op jit(solution)/shard_map/all_to_all | solution.py:424
  11.3 0.0 copy-start.2
  11.3 6.4 %own_cells.1 = (f32[4,16,32,256]{3,2,1,0:T(8,128)S(1)}, f32[16,32,256]{2,1,0:T(8,128)}, f32[16,32,256]{2,1,0:T(8,128)}, f32[16,32,256]{2,1,0:T(8,128)}, f32[2,4,32,256]{3,2,1,0:T(8,128)}) custom-call(f32[128,16,256]{2,1,0:T(8,128)} %bitcast.6, f32[3,3,3,32]{3,2,1,0:T(4,128)} %bitcast.8, f32[32,32]{1,0:T(8,128)} %point_hbm.1, f32[1,32]{1,0:T(1,128)} %bitcast.10), custom_call_target="tpu_custom_call" | custom-call | flops 8000000000 | tf_op jit(solution)/shard_map/own_cells/pallas_call | solution.py:452
  17.8 4.2 %all-to-all-done.data_ref = f32[8,16,8,128]{3,2,1,0:T(8,128)S(1)} async-done(((f32[8,16,8,128]{3,2,1,0:T(8,128)}), f32[8,16,8,128]{3,2,1,0:T(8,128)S(1)}, u32[]{:S(2)}, u32[]{:S(2)}) %all-to-all-start) | async-done | bytes 524320 | tf_op jit(solution)/shard_map/all_to_all | solution.py:424
  22.0 0.0 copy-done.2
  22.0 1.0 %forward_y.1 = f32[32,8,128]{2,1,0:T(8,128)} custom-call(f32[8,16,8,128]{3,2,1,0:T(8,128)S(1)} %all-to-all-done.data_ref, bf16[2,64,256]{2,1,0:T(8,128)(2,1)S(1)} %copy-done.2), custom_call_target="tpu_custom_call" | custom-call | tf_op jit(solution)/shard_map/forward_y/pallas_call | solution.py:477
  23.0 10.5 %all-to-all-start.1 = ((f32[32,8,128]{2,1,0:T(8,128)}), f32[32,8,128]{2,1,0:T(8,128)S(1)}, u32[]{:S(2)}, u32[]{:S(2)}) async-start(f32[32,8,128]{2,1,0:T(8,128)} %forward_y.1), calls=%async_computation.1 | async-start | bytes 262144 | tf_op jit(solution)/shard_map/all_to_all | solution.py:424
  33.5 0.0 copy-start.3
  33.5 3.0 %weights.1.weight_ref = f32[2,32,32,128]{3,2,1,0:T(8,128)S(1)} custom-call(f32[2,32,128,32]{3,2,1,0:T(8,128)} %bitcast.7), custom_call_target="tpu_custom_call" | custom-call | flops 8000000000 | tf_op jit(solution)/shard_map/weights/pallas_call | solution.py:482
  36.6 0.3 collective-permute-start.1
  36.9 1.5 %collective-permute-start = (f32[16,32,256]{2,1,0:T(8,128)}, f32[16,32,256]{2,1,0:T(8,128)}, u32[]{:S(2)}, u32[]{:S(2)}) collective-permute-start(f32[16,32,256]{2,1,0:T(8,128)} %get-tuple-element.38.last_hbm), channel_id=1, source_target_pairs={{0,8},{8,16},{16,24},{24,32},{32,40},{40,48},{48,56},{56,64},{64,7... | collective-permute-start | bytes 1572872 | tf_op jit(solution)/shard_map/ppermute | solution.py:420
  38.4 4.5 %all-to-all-done.1.data_ref = f32[32,8,128]{2,1,0:T(8,128)S(1)} async-done(((f32[32,8,128]{2,1,0:T(8,128)}), f32[32,8,128]{2,1,0:T(8,128)S(1)}, u32[]{:S(2)}, u32[]{:S(2)}) %all-to-all-start.1) | async-done | bytes 131104 | tf_op jit(solution)/shard_map/all_to_all | solution.py:424
  42.9 0.0 copy-done.3
  42.9 1.9 %middle.1 = f32[32,8,128]{2,1,0:T(8,128)} custom-call(f32[32,8,128]{2,1,0:T(8,128)S(1)} %all-to-all-done.1.data_ref, f32[2,32,32,128]{3,2,1,0:T(8,128)S(1)} %weights.1.weight_ref, bf16[2,64,256]{2,1,0:T(8,128)(2,1)S(1)} %copy-done.3, bf16[2,256,64]{2,1,0:T(8,128)(2,1)} %constant.15.clone.inverse_hbm), custom_call_target="tpu_custom_call" | custom-call | flops 3000000000 | tf_op jit(solution)/shard_map/middle/pallas_call | solution.py:494
  44.8 4.5 %all-to-all-start.2 = ((f32[32,8,128]{2,1,0:T(8,128)}), f32[32,8,128]{2,1,0:T(8,128)S(1)}, u32[]{:S(2)}, u32[]{:S(2)}) async-start(f32[32,8,128]{2,1,0:T(8,128)} %middle.1), calls=%async_computation.2 | async-start | bytes 262144 | tf_op jit(solution)/shard_map/all_to_all | solution.py:424
  49.3 2.4 %collective-permute-done.1.after_ref.after_hbm = f32[16,32,256]{2,1,0:T(8,128)} collective-permute-done((f32[16,32,256]{2,1,0:T(8,128)}, f32[16,32,256]{2,1,0:T(8,128)}, u32[]{:S(2)}, u32[]{:S(2)}) %collective-permute-start.1) | collective-permute-done | bytes 524320 | tf_op jit(solution)/shard_map/ppermute | solution.py:420
  51.7 0.0 collective-permute-done.before_ref.before_hbm
  51.7 0.0 copy-start
  51.7 1.1 %rims.1 = (f32[6,32,256]{2,1,0:T(8,128)S(1)}, f32[6,32,256]{2,1,0:T(8,128)S(1)}) custom-call(f32[2,4,32,256]{3,2,1,0:T(8,128)} %get-tuple-element.37.rows_ref, f32[16,32,256]{2,1,0:T(8,128)} %collective-permute-done.before_ref.before_hbm, f32[16,32,256]{2,1,0:T(8,128)} %collective-permute-done.1.after_ref.after_hbm), custom_call_target="tpu_custom_call" | custom-call | flops 2000000000 | tf_op jit(solution)/shard_map/rims/pallas_call | solution.py:506
  52.8 1.3 %collective-permute-start.2 = (f32[6,32,256]{2,1,0:T(8,128)S(1)}, f32[6,32,256]{2,1,0:T(8,128)S(1)}, u32[]{:S(2)}, u32[]{:S(2)}) collective-permute-start(f32[6,32,256]{2,1,0:T(8,128)S(1)} %get-tuple-element.42), channel_id=1, source_target_pairs={{0,1},{1,2},{2,3},{3,4},{4,5},{5,6},{6,7},{7,0},{8,9},{9,10},{10,1... | collective-permute-start | bytes 589832 | tf_op jit(solution)/shard_map/ppermute | solution.py:420
  54.0 3.9 %collective-permute-start.3 = (f32[6,32,256]{2,1,0:T(8,128)S(1)}, f32[6,32,256]{2,1,0:T(8,128)S(1)}, u32[]{:S(2)}, u32[]{:S(2)}) collective-permute-start(f32[6,32,256]{2,1,0:T(8,128)S(1)} %get-tuple-element.43), channel_id=1, source_target_pairs={{0,7},{1,0},{2,1},{3,2},{4,3},{5,4},{6,5},{7,6},{8,15},{9,8},{10,9... | collective-permute-start | bytes 589832 | tf_op jit(solution)/shard_map/ppermute | solution.py:420
  57.9 0.7 all-to-all-done.2.data_ref
  58.6 0.0 copy-done
  58.6 1.2 %inverse_y.1 = f32[8,16,8,128]{3,2,1,0:T(8,128)} custom-call(f32[32,8,128]{2,1,0:T(8,128)S(1)} %all-to-all-done.2.data_ref, bf16[2,256,64]{2,1,0:T(8,128)(2,1)S(1)} %copy-done), custom_call_target="tpu_custom_call" | custom-call | tf_op jit(solution)/shard_map/inverse_y/pallas_call | solution.py:517
  59.8 3.7 %all-to-all-start.3 = ((f32[8,16,8,128]{3,2,1,0:T(8,128)}), f32[8,16,8,128]{3,2,1,0:T(8,128)S(1)}, u32[]{:S(2)}, u32[]{:S(2)}) async-start(f32[8,16,8,128]{3,2,1,0:T(8,128)} %inverse_y.1), calls=%async_computation.3 | async-start | bytes 1048576 | tf_op jit(solution)/shard_map/all_to_all | solution.py:424
  63.5 0.0 collective-permute-done.2.left_ref
  63.5 1.3 %collective-permute-done.3.right_ref = f32[6,32,256]{2,1,0:T(8,128)S(1)} collective-permute-done((f32[6,32,256]{2,1,0:T(8,128)S(1)}, f32[6,32,256]{2,1,0:T(8,128)S(1)}, u32[]{:S(2)}, u32[]{:S(2)}) %collective-permute-start.3) | collective-permute-done | bytes 196640 | tf_op jit(solution)/shard_map/ppermute | solution.py:420
  64.8 0.0 copy-start.1
  64.8 3.2 %edge_cells.1.base_ref = f32[4,16,32,256]{3,2,1,0:T(8,128)S(1)} custom-call(f32[4,16,32,256]{3,2,1,0:T(8,128)S(1)} %get-tuple-element.45.base_ref, f32[16,32,256]{2,1,0:T(8,128)} %collective-permute-done.before_ref.before_hbm, f32[16,32,256]{2,1,0:T(8,128)} %get-tuple-element.46.third_hbm, ...), custom_call_target="tpu_custom_call", output_to_operand_aliasing={{}: (0, {})} | custom-call | flops 40000000000 | tf_op jit(solution)/shard_map/edge_cells/pallas_call | solution.py:523
  68.0 6.2 %all-to-all-done.3.data_ref = f32[8,16,8,128]{3,2,1,0:T(8,128)S(1)} async-done(((f32[8,16,8,128]{3,2,1,0:T(8,128)}), f32[8,16,8,128]{3,2,1,0:T(8,128)S(1)}, u32[]{:S(2)}, u32[]{:S(2)}) %all-to-all-start.3) | async-done | bytes 524320 | tf_op jit(solution)/shard_map/all_to_all | solution.py:424
  74.2 0.0 copy-done.1
  74.2 3.1 %final.1 = f32[128,16,256]{2,1,0:T(8,128)} custom-call(f32[8,16,8,128]{3,2,1,0:T(8,128)S(1)} %all-to-all-done.3.data_ref, f32[4,16,32,256]{3,2,1,0:T(8,128)S(1)} %edge_cells.1.base_ref, bf16[2,64,256]{2,1,0:T(8,128)(2,1)S(1)} %copy-done.1), custom_call_target="tpu_custom_call" | custom-call | tf_op jit(solution)/shard_map/final/pallas_call | solution.py:536
Async XLA Ops:
  3.8 18.2 %all-to-all-start = ((f32[8,16,8,128]{3,2,1,0:T(8,128)}), f32[8,16,8,128]{3,2,1,0:T(8,128)S(1)}, u32[]{:S(2)}, u32[]{:S(2)}) async-start(f32[8,16,8,128]{3,2,1,0:T(8,128)} %forward_z.1), calls=%async_computation | async-start | bytes 1048576 | tf_op jit(solution)/shard_map/all_to_all | solution.py:424
  11.3 10.7 %copy-start.2 = (bf16[2,64,256]{2,1,0:T(8,128)(2,1)S(1)}, bf16[2,64,256]{2,1,0:T(8,128)(2,1)}, u32[]{:S(2)}) copy-start(bf16[2,64,256]{2,1,0:T(8,128)(2,1)} %constant.13.clone.table_ref) | copy-start | bytes 196612
  23.0 19.9 %all-to-all-start.1 = ((f32[32,8,128]{2,1,0:T(8,128)}), f32[32,8,128]{2,1,0:T(8,128)S(1)}, u32[]{:S(2)}, u32[]{:S(2)}) async-start(f32[32,8,128]{2,1,0:T(8,128)} %forward_y.1), calls=%async_computation.1 | async-start | bytes 262144 | tf_op jit(solution)/shard_map/all_to_all | solution.py:424
  33.5 9.4 %copy-start.3 = (bf16[2,64,256]{2,1,0:T(8,128)(2,1)S(1)}, bf16[2,64,256]{2,1,0:T(8,128)(2,1)}, u32[]{:S(2)}) copy-start(bf16[2,64,256]{2,1,0:T(8,128)(2,1)} %constant.14.clone.forward_ref) | copy-start | bytes 196612
  36.6 15.1 %collective-permute-start.1 = (f32[16,32,256]{2,1,0:T(8,128)}, f32[16,32,256]{2,1,0:T(8,128)}, u32[]{:S(2)}, u32[]{:S(2)}) collective-permute-start(f32[16,32,256]{2,1,0:T(8,128)} %get-tuple-element.39), channel_id=1, source_target_pairs={{0,248},{8,0},{16,8},{24,16},{32,24},{40,32},{48,40},{56,48},{64,5... | collective-permute-start | bytes 1572872 | tf_op jit(solution)/shard_map/ppermute | solution.py:420
  36.9 14.8 %collective-permute-start = (f32[16,32,256]{2,1,0:T(8,128)}, f32[16,32,256]{2,1,0:T(8,128)}, u32[]{:S(2)}, u32[]{:S(2)}) collective-permute-start(f32[16,32,256]{2,1,0:T(8,128)} %get-tuple-element.38.last_hbm), channel_id=1, source_target_pairs={{0,8},{8,16},{16,24},{24,32},{32,40},{40,48},{48,56},{56,64},{64,7... | collective-permute-start | bytes 1572872 | tf_op jit(solution)/shard_map/ppermute | solution.py:420
  44.8 13.8 %all-to-all-start.2 = ((f32[32,8,128]{2,1,0:T(8,128)}), f32[32,8,128]{2,1,0:T(8,128)S(1)}, u32[]{:S(2)}, u32[]{:S(2)}) async-start(f32[32,8,128]{2,1,0:T(8,128)} %middle.1), calls=%async_computation.2 | async-start | bytes 262144 | tf_op jit(solution)/shard_map/all_to_all | solution.py:424
  51.7 7.0 %copy-start = (bf16[2,256,64]{2,1,0:T(8,128)(2,1)S(1)}, bf16[2,256,64]{2,1,0:T(8,128)(2,1)}, u32[]{:S(2)}) copy-start(bf16[2,256,64]{2,1,0:T(8,128)(2,1)} %constant.16.clone.table_ref) | copy-start | bytes 196612
  52.8 10.7 %collective-permute-start.2 = (f32[6,32,256]{2,1,0:T(8,128)S(1)}, f32[6,32,256]{2,1,0:T(8,128)S(1)}, u32[]{:S(2)}, u32[]{:S(2)}) collective-permute-start(f32[6,32,256]{2,1,0:T(8,128)S(1)} %get-tuple-element.42), channel_id=1, source_target_pairs={{0,1},{1,2},{2,3},{3,4},{4,5},{5,6},{6,7},{7,0},{8,9},{9,10},{10,1... | collective-permute-start | bytes 589832 | tf_op jit(solution)/shard_map/ppermute | solution.py:420
  54.0 10.7 %collective-permute-start.3 = (f32[6,32,256]{2,1,0:T(8,128)S(1)}, f32[6,32,256]{2,1,0:T(8,128)S(1)}, u32[]{:S(2)}, u32[]{:S(2)}) collective-permute-start(f32[6,32,256]{2,1,0:T(8,128)S(1)} %get-tuple-element.43), channel_id=1, source_target_pairs={{0,7},{1,0},{2,1},{3,2},{4,3},{5,4},{6,5},{7,6},{8,15},{9,8},{10,9... | collective-permute-start | bytes 589832 | tf_op jit(solution)/shard_map/ppermute | solution.py:420
  59.8 14.4 %all-to-all-start.3 = ((f32[8,16,8,128]{3,2,1,0:T(8,128)}), f32[8,16,8,128]{3,2,1,0:T(8,128)S(1)}, u32[]{:S(2)}, u32[]{:S(2)}) async-start(f32[8,16,8,128]{3,2,1,0:T(8,128)} %inverse_y.1), calls=%async_computation.3 | async-start | bytes 1048576 | tf_op jit(solution)/shard_map/all_to_all | solution.py:424
  64.8 9.4 %copy-start.1 = (bf16[2,64,256]{2,1,0:T(8,128)(2,1)S(1)}, bf16[2,64,256]{2,1,0:T(8,128)(2,1)}, u32[]{:S(2)}) copy-start(bf16[2,64,256]{2,1,0:T(8,128)(2,1)} %constant.17.clone.table_ref) | copy-start | bytes 196612

commit v9 on v8

--- a/solution.py
+++ b/solution.py
@@ -483,11 +483,11 @@
         weights,
         [((2, 32, 32, 128), kept_near)],
         1,
-        8,
+        0,
         in_specs=[HBM],
         scratch_shapes=[pltpu.VMEM((2, 32, 128, 32), F32), dma((8,))],
     )(far(after_all(spec_weight, ychunks).reshape(2, 32, 128, 32)))
-    first, last, packed = lax.optimization_barrier((first, last, packed))
+    first, last, _ = lax.optimization_barrier((first, last, ychunks))
     before = shifted("gx", far(last), 1)
     after = shifted("gx", far(first), -1)
     yall, packed = lax.optimization_barrier((yall, packed))
@@ -495,7 +495,7 @@
         middle,
         [((32, 8, 128), plain)],
         4,
-        3,
+        1,
         in_specs=[VMEM] * 3 + [ANY],
         scratch_shapes=[pltpu.VMEM((2, 256, 64), BF16), dma],
     )(near(yall), near(packed), near(jnp.asarray(tab["fx"])), far(jnp.asarray(tab["ix"])))

time: 77.9 us -> 80 us (1.027)
  waiting for transfers between devices: 19.3 us -> 21 us
    all_to_all x4, waiting for transfers between devices: 15.6 us -> 21 us  [exchange(): return lax.all_to_all(value, axis, split_axis=0, concat_axis=0, tiled=True)]
    ppermute x4, waiting for transfers between devices: 3.67 us -> 0.01 us  [shifted(): lax.ppermute(value, axis, [(i, (i + step) % count) for i in range(count)])]
  transfers between devices with their start and end apart: 8 -> 8, of which waited for: 6 -> 4; matrix products, arithmetic and copies ran while one was open for 0% -> 0% of each run, Pallas kernels for 22% -> 21%
where the time goes in v9:
time: 80 us; the launch traced here: 79.5 us
  starting transfers between devices  33.4 us (42%)
  Pallas kernels  24.7 us (31%)
  waiting for transfers between devices  21 us (26%)
    all_to_all x4, starting transfers between devices, exchange(): return lax.all_to_all(value, axis, split_axis=0, concat_axis=0, tiled=True)  26.2 us
    all_to_all x4, waiting for transfers between devices, exchange(): return lax.all_to_all(value, axis, split_axis=0, concat_axis=0, tiled=True)  21 us
    ppermute x4, starting transfers between devices, shifted(): lax.ppermute(value, axis, [(i, (i + step) % count) for i in range(count)])  7.22 us
    pallas_call x1, Pallas kernels, on_device(): call(own_cells, [((4, 16, 32, 256), kept_near), ((16, 32, 256), pltpu.HBM...  6.44 us
    pallas_call x1, Pallas kernels, on_device(): call(forward_z, [((8, 16, 8, 128), plain)], 2, in_specs=[HBM] * 2, out_sp...  3.81 us
    pallas_call x1, Pallas kernels, on_device(): call(edge_cells, [((4, 16, 32, 256), kept_near)], 8, 40, in_specs=[VMEM]...  3.17 us
    pallas_call x1, Pallas kernels, on_device(): call(final, [((128, 16, 256), plain)], 3, out_specs=[ANY], scratch_shapes...  3.08 us
    pallas_call x1, Pallas kernels, on_device(): call(weights, [((2, 32, 32, 128), kept_near)], 1, 0, in_specs=[HBM], scra...  3.03 us
  transfers between devices with their start and end apart: 8, of which 4 were waited for; matrix products, arithmetic and copies ran while one was open for 0% of the time, Pallas kernels for 21%

profile of v9, /device:TPU:1, one launch (start us, length us, event | category | flops | bytes accessed | tf_op | source)
XLA Modules:
  0.0 79.5 jit_solution(16074539767162011354)
XLA Ops:
  0.0 3.8 %forward_z.1 = f32[8,16,8,128]{3,2,1,0:T(8,128)} custom-call(f32[128,16,256]{2,1,0:T(8,128)} %bitcast.6, bf16[128,256]{1,0:T(8,128)(2,1)} %constant.12.clone.table_ref), custom_call_target="tpu_custom_call" | custom-call | tf_op jit(solution)/shard_map/forward_z/pallas_call | solution.py:435
  3.8 7.5 %all-to-all-start = ((f32[8,16,8,128]{3,2,1,0:T(8,128)}), f32[8,16,8,128]{3,2,1,0:T(8,128)S(1)}, u32[]{:S(2)}, u32[]{:S(2)}) async-start(f32[8,16,8,128]{3,2,1,0:T(8,128)} %forward_z.1), calls=%async_computation | async-start | bytes 1048576 | tf_op jit(solution)/shard_map/all_to_all | solution.py:424
  11.3 0.0 copy-start.2
  11.3 6.4 %own_cells.1 = (f32[4,16,32,256]{3,2,1,0:T(8,128)S(1)}, f32[16,32,256]{2,1,0:T(8,128)}, f32[16,32,256]{2,1,0:T(8,128)}, f32[16,32,256]{2,1,0:T(8,128)}, f32[2,4,32,256]{3,2,1,0:T(8,128)}) custom-call(f32[128,16,256]{2,1,0:T(8,128)} %bitcast.7, f32[3,3,3,32]{3,2,1,0:T(4,128)} %bitcast.8, f32[32,32]{1,0:T(8,128)} %point_hbm.1, f32[1,32]{1,0:T(1,128)} %bitcast.10), custom_call_target="tpu_custom_call" | custom-call | flops 8000000000 | tf_op jit(solution)/shard_map/own_cells/pallas_call | solution.py:452
  17.8 4.2 %all-to-all-done.data_ref = f32[8,16,8,128]{3,2,1,0:T(8,128)S(1)} async-done(((f32[8,16,8,128]{3,2,1,0:T(8,128)}), f32[8,16,8,128]{3,2,1,0:T(8,128)S(1)}, u32[]{:S(2)}, u32[]{:S(2)}) %all-to-all-start) | async-done | bytes 524320 | tf_op jit(solution)/shard_map/all_to_all | solution.py:424
  22.0 0.0 copy-done.2
  22.0 1.0 %forward_y.1 = f32[32,8,128]{2,1,0:T(8,128)} custom-call(f32[8,16,8,128]{3,2,1,0:T(8,128)S(1)} %all-to-all-done.data_ref, bf16[2,64,256]{2,1,0:T(8,128)(2,1)S(1)} %copy-done.2), custom_call_target="tpu_custom_call" | custom-call | tf_op jit(solution)/shard_map/forward_y/pallas_call | solution.py:477
  23.0 1.9 %collective-permute-start.1 = (f32[16,32,256]{2,1,0:T(8,128)}, f32[16,32,256]{2,1,0:T(8,128)}, u32[]{:S(2)}, u32[]{:S(2)}) collective-permute-start(f32[16,32,256]{2,1,0:T(8,128)} %get-tuple-element.37), channel_id=1, source_target_pairs={{0,248},{8,0},{16,8},{24,16},{32,24},{40,32},{48,40},{56,48},{64,5... | collective-permute-start | bytes 1572872 | tf_op jit(solution)/shard_map/ppermute | solution.py:420
  24.9 0.2 collective-permute-start
  25.1 10.1 %all-to-all-start.1 = ((f32[32,8,128]{2,1,0:T(8,128)}), f32[32,8,128]{2,1,0:T(8,128)S(1)}, u32[]{:S(2)}, u32[]{:S(2)}) async-start(f32[32,8,128]{2,1,0:T(8,128)} %forward_y.1), calls=%async_computation.1 | async-start | bytes 262144 | tf_op jit(solution)/shard_map/all_to_all | solution.py:424
  35.1 0.0 copy-start.3
  35.1 3.0 %weights.1.weight_ref = f32[2,32,32,128]{3,2,1,0:T(8,128)S(1)} custom-call(f32[2,32,128,32]{3,2,1,0:T(8,128)} %bitcast.5), custom_call_target="tpu_custom_call" | custom-call | tf_op jit(solution)/shard_map/weights/pallas_call | solution.py:482
  38.2 6.2 %all-to-all-done.1.data_ref = f32[32,8,128]{2,1,0:T(8,128)S(1)} async-done(((f32[32,8,128]{2,1,0:T(8,128)}), f32[32,8,128]{2,1,0:T(8,128)S(1)}, u32[]{:S(2)}, u32[]{:S(2)}) %all-to-all-start.1) | async-done | bytes 131104 | tf_op jit(solution)/shard_map/all_to_all | solution.py:424
  44.4 0.0 copy-done.3
  44.4 1.9 %middle.1 = f32[32,8,128]{2,1,0:T(8,128)} custom-call(f32[32,8,128]{2,1,0:T(8,128)S(1)} %all-to-all-done.1.data_ref, f32[2,32,32,128]{3,2,1,0:T(8,128)S(1)} %weights.1.weight_ref, bf16[2,64,256]{2,1,0:T(8,128)(2,1)S(1)} %copy-done.3, bf16[2,256,64]{2,1,0:T(8,128)(2,1)} %constant.15.clone.inverse_hbm), custom_call_target="tpu_custom_call" | custom-call | flops 1000000000 | tf_op jit(solution)/shard_map/middle/pallas_call | solution.py:494
  46.3 5.0 %all-to-all-start.2 = ((f32[32,8,128]{2,1,0:T(8,128)}), f32[32,8,128]{2,1,0:T(8,128)S(1)}, u32[]{:S(2)}, u32[]{:S(2)}) async-start(f32[32,8,128]{2,1,0:T(8,128)} %middle.1), calls=%async_computation.2 | async-start | bytes 262144 | tf_op jit(solution)/shard_map/all_to_all | solution.py:424
  51.3 0.0 collective-permute-done.1.after_ref.after_hbm
  51.3 0.0 collective-permute-done.before_ref.before_hbm
  51.4 0.0 copy-start
  51.4 1.1 %rims.1 = (f32[6,32,256]{2,1,0:T(8,128)S(1)}, f32[6,32,256]{2,1,0:T(8,128)S(1)}) custom-call(f32[2,4,32,256]{3,2,1,0:T(8,128)} %get-tuple-element.33.rows_ref, f32[16,32,256]{2,1,0:T(8,128)} %collective-permute-done.before_ref.before_hbm, f32[16,32,256]{2,1,0:T(8,128)} %collective-permute-done.1.after_ref.after_hbm), custom_call_target="tpu_custom_call" | custom-call | flops 2000000000 | tf_op jit(solution)/shard_map/rims/pallas_call | solution.py:506
  52.5 1.1 %collective-permute-start.2 = (f32[6,32,256]{2,1,0:T(8,128)S(1)}, f32[6,32,256]{2,1,0:T(8,128)S(1)}, u32[]{:S(2)}, u32[]{:S(2)}) collective-permute-start(f32[6,32,256]{2,1,0:T(8,128)S(1)} %get-tuple-element.40), channel_id=1, source_target_pairs={{0,1},{1,2},{2,3},{3,4},{4,5},{5,6},{6,7},{7,0},{8,9},{9,10},{10,1... | collective-permute-start | bytes 589832 | tf_op jit(solution)/shard_map/ppermute | solution.py:420
  53.5 4.1 %collective-permute-start.3 = (f32[6,32,256]{2,1,0:T(8,128)S(1)}, f32[6,32,256]{2,1,0:T(8,128)S(1)}, u32[]{:S(2)}, u32[]{:S(2)}) collective-permute-start(f32[6,32,256]{2,1,0:T(8,128)S(1)} %get-tuple-element.41), channel_id=1, source_target_pairs={{0,7},{1,0},{2,1},{3,2},{4,3},{5,4},{6,5},{7,6},{8,15},{9,8},{10,9... | collective-permute-start | bytes 589832 | tf_op jit(solution)/shard_map/ppermute | solution.py:420
  57.6 3.1 %all-to-all-done.2.data_ref = f32[32,8,128]{2,1,0:T(8,128)S(1)} async-done(((f32[32,8,128]{2,1,0:T(8,128)}), f32[32,8,128]{2,1,0:T(8,128)S(1)}, u32[]{:S(2)}, u32[]{:S(2)}) %all-to-all-start.2) | async-done | bytes 131104 | tf_op jit(solution)/shard_map/all_to_all | solution.py:424
  60.7 0.0 copy-done
  60.7 1.2 %inverse_y.1 = f32[8,16,8,128]{3,2,1,0:T(8,128)} custom-call(f32[32,8,128]{2,1,0:T(8,128)S(1)} %all-to-all-done.2.data_ref, bf16[2,256,64]{2,1,0:T(8,128)(2,1)S(1)} %copy-done), custom_call_target="tpu_custom_call" | custom-call | tf_op jit(solution)/shard_map/inverse_y/pallas_call | solution.py:517
  61.9 3.7 %all-to-all-start.3 = ((f32[8,16,8,128]{3,2,1,0:T(8,128)}), f32[8,16,8,128]{3,2,1,0:T(8,128)S(1)}, u32[]{:S(2)}, u32[]{:S(2)}) async-start(f32[8,16,8,128]{3,2,1,0:T(8,128)} %inverse_y.1), calls=%async_computation.3 | async-start | bytes 1048576 | tf_op jit(solution)/shard_map/all_to_all | solution.py:424
  65.5 0.0 collective-permute-done.2.left_ref
  65.5 0.0 collective-permute-done.3.right_ref
  65.6 0.0 copy-start.1
  65.6 3.2 %edge_cells.1.base_ref = f32[4,16,32,256]{3,2,1,0:T(8,128)S(1)} custom-call(f32[4,16,32,256]{3,2,1,0:T(8,128)S(1)} %get-tuple-element.43.base_ref, f32[16,32,256]{2,1,0:T(8,128)} %collective-permute-done.before_ref.before_hbm, f32[16,32,256]{2,1,0:T(8,128)} %get-tuple-element.44.third_hbm, ...), custom_call_target="tpu_custom_call", output_to_operand_aliasing={{}: (0, {})} | custom-call | flops 40000000000 | tf_op jit(solution)/shard_map/edge_cells/pallas_call | solution.py:523
  68.7 7.5 %all-to-all-done.3.data_ref = f32[8,16,8,128]{3,2,1,0:T(8,128)S(1)} async-done(((f32[8,16,8,128]{3,2,1,0:T(8,128)}), f32[8,16,8,128]{3,2,1,0:T(8,128)S(1)}, u32[]{:S(2)}, u32[]{:S(2)}) %all-to-all-start.3) | async-done | bytes 524320 | tf_op jit(solution)/shard_map/all_to_all | solution.py:424
  76.2 0.0 copy-done.1
  76.2 3.1 %final.1 = f32[128,16,256]{2,1,0:T(8,128)} custom-call(f32[8,16,8,128]{3,2,1,0:T(8,128)S(1)} %all-to-all-done.3.data_ref, f32[4,16,32,256]{3,2,1,0:T(8,128)S(1)} %edge_cells.1.base_ref, bf16[2,64,256]{2,1,0:T(8,128)(2,1)S(1)} %copy-done.1), custom_call_target="tpu_custom_call" | custom-call | tf_op jit(solution)/shard_map/final/pallas_call | solution.py:536
Async XLA Ops:
  3.8 18.2 %all-to-all-start = ((f32[8,16,8,128]{3,2,1,0:T(8,128)}), f32[8,16,8,128]{3,2,1,0:T(8,128)S(1)}, u32[]{:S(2)}, u32[]{:S(2)}) async-start(f32[8,16,8,128]{3,2,1,0:T(8,128)} %forward_z.1), calls=%async_computation | async-start | bytes 1048576 | tf_op jit(solution)/shard_map/all_to_all | solution.py:424
  11.3 10.7 %copy-start.2 = (bf16[2,64,256]{2,1,0:T(8,128)(2,1)S(1)}, bf16[2,64,256]{2,1,0:T(8,128)(2,1)}, u32[]{:S(2)}) copy-start(bf16[2,64,256]{2,1,0:T(8,128)(2,1)} %constant.13.clone.table_ref) | copy-start | bytes 196612
  23.0 28.3 %collective-permute-start.1 = (f32[16,32,256]{2,1,0:T(8,128)}, f32[16,32,256]{2,1,0:T(8,128)}, u32[]{:S(2)}, u32[]{:S(2)}) collective-permute-start(f32[16,32,256]{2,1,0:T(8,128)} %get-tuple-element.37), channel_id=1, source_target_pairs={{0,248},{8,0},{16,8},{24,16},{32,24},{40,32},{48,40},{56,48},{64,5... | collective-permute-start | bytes 1572872 | tf_op jit(solution)/shard_map/ppermute | solution.py:420
  24.9 26.5 %collective-permute-start = (f32[16,32,256]{2,1,0:T(8,128)}, f32[16,32,256]{2,1,0:T(8,128)}, u32[]{:S(2)}, u32[]{:S(2)}) collective-permute-start(f32[16,32,256]{2,1,0:T(8,128)} %get-tuple-element.36.last_hbm), channel_id=1, source_target_pairs={{0,8},{8,16},{16,24},{24,32},{32,40},{40,48},{48,56},{56,64},{64,7... | collective-permute-start | bytes 1572872 | tf_op jit(solution)/shard_map/ppermute | solution.py:420
  25.1 19.3 %all-to-all-start.1 = ((f32[32,8,128]{2,1,0:T(8,128)}), f32[32,8,128]{2,1,0:T(8,128)S(1)}, u32[]{:S(2)}, u32[]{:S(2)}) async-start(f32[32,8,128]{2,1,0:T(8,128)} %forward_y.1), calls=%async_computation.1 | async-start | bytes 262144 | tf_op jit(solution)/shard_map/all_to_all | solution.py:424
  35.1 9.3 %copy-start.3 = (bf16[2,64,256]{2,1,0:T(8,128)(2,1)S(1)}, bf16[2,64,256]{2,1,0:T(8,128)(2,1)}, u32[]{:S(2)}) copy-start(bf16[2,64,256]{2,1,0:T(8,128)(2,1)} %constant.14.clone.forward_ref) | copy-start | bytes 196612
  46.3 14.4 %all-to-all-start.2 = ((f32[32,8,128]{2,1,0:T(8,128)}), f32[32,8,128]{2,1,0:T(8,128)S(1)}, u32[]{:S(2)}, u32[]{:S(2)}) async-start(f32[32,8,128]{2,1,0:T(8,128)} %middle.1), calls=%async_computation.2 | async-start | bytes 262144 | tf_op jit(solution)/shard_map/all_to_all | solution.py:424
  51.4 9.3 %copy-start = (bf16[2,256,64]{2,1,0:T(8,128)(2,1)S(1)}, bf16[2,256,64]{2,1,0:T(8,128)(2,1)}, u32[]{:S(2)}) copy-start(bf16[2,256,64]{2,1,0:T(8,128)(2,1)} %constant.16.clone.table_ref) | copy-start | bytes 196612
  52.5 13.1 %collective-permute-start.2 = (f32[6,32,256]{2,1,0:T(8,128)S(1)}, f32[6,32,256]{2,1,0:T(8,128)S(1)}, u32[]{:S(2)}, u32[]{:S(2)}) collective-permute-start(f32[6,32,256]{2,1,0:T(8,128)S(1)} %get-tuple-element.40), channel_id=1, source_target_pairs={{0,1},{1,2},{2,3},{3,4},{4,5},{5,6},{6,7},{7,0},{8,9},{9,10},{10,1... | collective-permute-start | bytes 589832 | tf_op jit(solution)/shard_map/ppermute | solution.py:420
  53.5 12.0 %collective-permute-start.3 = (f32[6,32,256]{2,1,0:T(8,128)S(1)}, f32[6,32,256]{2,1,0:T(8,128)S(1)}, u32[]{:S(2)}, u32[]{:S(2)}) collective-permute-start(f32[6,32,256]{2,1,0:T(8,128)S(1)} %get-tuple-element.41), channel_id=1, source_target_pairs={{0,7},{1,0},{2,1},{3,2},{4,3},{5,4},{6,5},{7,6},{8,15},{9,8},{10,9... | collective-permute-start | bytes 589832 | tf_op jit(solution)/shard_map/ppermute | solution.py:420
  61.9 14.4 %all-to-all-start.3 = ((f32[8,16,8,128]{3,2,1,0:T(8,128)}), f32[8,16,8,128]{3,2,1,0:T(8,128)S(1)}, u32[]{:S(2)}, u32[]{:S(2)}) async-start(f32[8,16,8,128]{3,2,1,0:T(8,128)} %inverse_y.1), calls=%async_computation.3 | async-start | bytes 1048576 | tf_op jit(solution)/shard_map/all_to_all | solution.py:424
  65.6 10.7 %copy-start.1 = (bf16[2,64,256]{2,1,0:T(8,128)(2,1)S(1)}, bf16[2,64,256]{2,1,0:T(8,128)(2,1)}, u32[]{:S(2)}) copy-start(bf16[2,64,256]{2,1,0:T(8,128)(2,1)} %constant.17.clone.table_ref) | copy-start | bytes 196612

commit v10 on v8

--- a/solution.py
+++ b/solution.py
@@ -93,6 +93,10 @@
         )
         for x in range(4)
     ]
+
+
+def odd():
+    return lax.rem(lax.axis_index("gx"), 2)
 
 
 def start_all(copies):
@@ -228,13 +232,13 @@
                 rows[pl.ds(1024 * part + m, 32, stride=32), :] = tile
 
 
-def rims(rows_ref, before_ref, after_ref, top_ref, bottom_ref, sems):
+def rims(rows_ref, inner_ref, outer_ref, top_ref, bottom_ref, sems):
     copies = []
     for side, out_ref in enumerate((bottom_ref, top_ref)):
         moves = [
             (rows_ref.at[side], out_ref.at[pl.ds(1, 4)]),
-            (before_ref.at[15 * side], out_ref.at[0]),
-            (after_ref.at[15 * side], out_ref.at[5]),
+            (inner_ref.at[15 * side], out_ref.at[5 - 5 * odd()]),
+            (outer_ref.at[15 * side], out_ref.at[5 * odd()]),
         ]
         copies += [
             pltpu.make_async_copy(src, dst, sems.at[side, i]) for i, (src, dst) in enumerate(moves)
@@ -266,7 +270,7 @@
 
 
 def own_cells(
-    cells_ref, dw_hbm, point_hbm, bias_hbm, out_ref, first_ref, third_ref, last_ref, rim_ref,
+    cells_ref, dw_hbm, point_hbm, bias_hbm, out_ref, inner_ref, outer_ref, third_ref, last_ref, rim_ref,
     held, planes, tap_ref, dw_ref, point_ref, bias_ref, sems, small
 ):
     loads = [
@@ -318,7 +322,8 @@
     lax.fori_loop(1, 7, body, 0)
     fill(1)
     moves = [
-        (planes.at[0], first_ref),
+        (planes.at[3 - 3 * odd()], inner_ref),
+        (planes.at[3 * odd()], outer_ref),
         (planes.at[2], third_ref),
         (planes.at[3], last_ref),
         (planes.at[:, 0], rim_ref.at[0]),
@@ -334,15 +339,16 @@
 
 
 def edge_cells(
-    base_ref, before_hbm, third_hbm, last_hbm, after_hbm, left_ref, right_ref, dw_hbm,
-    out_ref, before_ref, third_ref, last_ref, after_ref, tap_ref, dw_ref, sems
+    base_ref, inner_hbm, outer_hbm, third_hbm, last_hbm, left_ref, right_ref, dw_hbm,
+    out_ref, halo_ref, third_ref, last_ref, tap_ref, dw_ref, sems
 ):
+    before_ref, after_ref = halo_ref.at[0], halo_ref.at[1]
     moves = [
         (dw_hbm, dw_ref),
-        (before_hbm, before_ref),
+        (inner_hbm, halo_ref.at[1 - odd()]),
+        (outer_hbm, halo_ref.at[odd()]),
         (third_hbm, third_ref),
         (last_hbm, last_ref),
-        (after_hbm, after_ref),
     ]
     copies = [
         pltpu.make_async_copy(src, dst, sems.at[i]) for i, (src, dst) in enumerate(moves)
@@ -418,6 +424,12 @@
 def shifted(axis, value, step):
     count = lax.axis_size(axis)
     return lax.ppermute(value, axis, [(i, (i + step) % count) for i in range(count)])
+
+
+def swapped(axis, value, start):
+    count = lax.axis_size(axis)
+    pairs = [((i + start) % count, (i + start + 1) % count) for i in range(0, count, 2)]
+    return lax.ppermute(value, axis, pairs + [(j, i) for i, j in pairs])
 
 
 def exchange(value, axis):
@@ -449,10 +461,11 @@
     taps = dw_kernel.transpose(1, 2, 3, 0)
 
     zall = exchange(zchunks, "gy")
-    base, first, third, last, own_rims = call(
+    base, inner, outer, third, last, own_rims = call(
         own_cells,
         [
             ((4, 16, 32, 256), kept_near),
+            ((16, 32, 256), pltpu.HBM),
             ((16, 32, 256), pltpu.HBM),
             ((16, 32, 256), pltpu.HBM),
             ((16, 32, 256), pltpu.HBM),
@@ -461,7 +474,7 @@
         4,
         8,
         in_specs=[HBM] * 4,
-        out_specs=[VMEM] + [HBM] * 4,
+        out_specs=[VMEM] + [HBM] * 5,
         scratch_shapes=[
             pltpu.VMEM((2, 2, 128, 8, 128), F32),
             pltpu.VMEM((4, 16, 32, 256), F32),
@@ -470,7 +483,7 @@
             pltpu.VMEM((32, 32), F32),
             pltpu.VMEM((1, 32), F32),
             dma((2, 2)),
-            dma((8,)),
+            dma((9,)),
         ],
     )(far(after_all(cells, zchunks)), far(taps), far(point_weight), far(bias.reshape(1, 32)))
     zall, base = lax.optimization_barrier((zall, base))
@@ -487,9 +500,9 @@
         in_specs=[HBM],
         scratch_shapes=[pltpu.VMEM((2, 32, 128, 32), F32), dma((8,))],
     )(far(after_all(spec_weight, ychunks).reshape(2, 32, 128, 32)))
-    first, last, packed = lax.optimization_barrier((first, last, packed))
-    before = shifted("gx", far(last), 1)
-    after = shifted("gx", far(first), -1)
+    inner, outer, packed = lax.optimization_barrier((inner, outer, packed))
+    inner = swapped("gx", far(inner), 0)
+    outer = swapped("gx", far(outer), 1)
     yall, packed = lax.optimization_barrier((yall, packed))
     (xchunks,) = call(
         middle,
@@ -501,8 +514,8 @@
     )(near(yall), near(packed), near(jnp.asarray(tab["fx"])), far(jnp.asarray(tab["ix"])))
 
     xall = exchange(xchunks, "gx")
-    before, after, _ = lax.optimization_barrier((before, after, xchunks))
-    before, after = far(before), far(after)
+    inner, outer, _ = lax.optimization_barrier((inner, outer, xchunks))
+    inner, outer = far(inner), far(outer)
     top, bottom = call(
         rims,
         [((6, 32, 256), kept_near)] * 2,
@@ -510,7 +523,7 @@
         2,
         in_specs=[HBM] * 3,
         scratch_shapes=[dma((2, 3))],
-    )(far(own_rims), before, after)
+    )(far(own_rims), inner, outer)
     left = shifted("gy", top, 1)
     right = shifted("gy", bottom, -1)
     xall, top, bottom = lax.optimization_barrier((xall, top, bottom))
@@ -526,11 +539,11 @@
         8,
         40,
         in_specs=[VMEM] + [ANY] * 4 + [VMEM] * 2 + [ANY],
-        scratch_shapes=[pltpu.VMEM((16, 32, 256), F32)] * 4
+        scratch_shapes=[pltpu.VMEM((2, 16, 32, 256), F32)] + [pltpu.VMEM((16, 32, 256), F32)] * 2
         + [pltpu.VMEM((27, 32, 128), F32), pltpu.VMEM((3, 3, 3, 32), F32), dma((5,))],
         input_output_aliases={0: 0},
     )(
-        near(base), before, far(third), far(last), after, near(left), near(right), far(taps)
+        near(base), inner, outer, far(third), far(last), near(left), near(right), far(taps)
     )
     ball, base = lax.optimization_barrier((ball, base))
     (out,) = call(

time: 77.9 us -> 77.7 us (level)
    ppermute x4 -> x2, waiting for transfers between devices: 3.67 us -> 0.24 us  [shifted(): lax.ppermute(value, axis, [(i, (i + step) % count) for i in range(count)])]
    ppermute x0 -> x2, waiting for transfers between devices: none -> 3.07 us  [swapped(): return lax.ppermute(value, axis, pairs + [(j, i) for i, j in pairs])]
    ppermute x0 -> x2, starting transfers between devices: none -> 1.87 us  [swapped(): return lax.ppermute(value, axis, pairs + [(j, i) for i, j in pairs])]
    ppermute x4 -> x2, starting transfers between devices: 7.01 us -> 5.16 us  [shifted(): lax.ppermute(value, axis, [(i, (i + step) % count) for i in range(count)])]
where the time goes in v10:
time: 77.7 us; the launch traced here: 77.1 us
  starting transfers between devices  32.8 us (42%)
  Pallas kernels  24.7 us (32%)
  waiting for transfers between devices  19.3 us (25%)
    all_to_all x4, starting transfers between devices, exchange(): return lax.all_to_all(value, axis, split_axis=0, concat_axis=0, tiled=True)  25.8 us
    all_to_all x4, waiting for transfers between devices, exchange(): return lax.all_to_all(value, axis, split_axis=0, concat_axis=0, tiled=True)  16 us
    pallas_call x1, Pallas kernels, on_device(): call(own_cells, [((4, 16, 32, 256), kept_near), ((16, 32, 256), pltpu.HBM...  6.45 us
    ppermute x2, starting transfers between devices, shifted(): lax.ppermute(value, axis, [(i, (i + step) % count) for i in range(count)])  5.16 us
    pallas_call x1, Pallas kernels, on_device(): call(forward_z, [((8, 16, 8, 128), plain)], 2, in_specs=[HBM] * 2, out_sp...  3.81 us
    pallas_call x1, Pallas kernels, on_device(): call(edge_cells, [((4, 16, 32, 256), kept_near)], 8, 40, in_specs=[VMEM]...  3.18 us
    pallas_call x1, Pallas kernels, on_device(): call(final, [((128, 16, 256), plain)], 3, out_specs=[ANY], scratch_shapes...  3.08 us
    ppermute x2, waiting for transfers between devices, swapped(): return lax.ppermute(value, axis, pairs + [(j, i) for i, j in pairs])  3.07 us
  transfers between devices with their start and end apart: 8, of which 6 were waited for; matrix products, arithmetic and copies ran while one was open for 0% of the time, Pallas kernels for 22%

profile of v10, /device:TPU:1, one launch (start us, length us, event | category | flops | bytes accessed | tf_op | source)
XLA Modules:
  0.0 77.1 jit_solution(4160997528242335274)
XLA Ops:
  0.0 3.8 %forward_z.1 = f32[8,16,8,128]{3,2,1,0:T(8,128)} custom-call(f32[128,16,256]{2,1,0:T(8,128)} %bitcast.5, bf16[128,256]{1,0:T(8,128)(2,1)} %constant.12.clone.table_ref), custom_call_target="tpu_custom_call" | custom-call | tf_op jit(solution)/shard_map/forward_z/pallas_call | solution.py:447
  3.8 7.5 %all-to-all-start = ((f32[8,16,8,128]{3,2,1,0:T(8,128)}), f32[8,16,8,128]{3,2,1,0:T(8,128)S(1)}, u32[]{:S(2)}, u32[]{:S(2)}) async-start(f32[8,16,8,128]{3,2,1,0:T(8,128)} %forward_z.1), calls=%async_computation | async-start | bytes 1048576 | tf_op jit(solution)/shard_map/all_to_all | solution.py:436
  11.3 0.0 copy-start.2
  11.3 6.5 %own_cells.1 = (f32[4,16,32,256]{3,2,1,0:T(8,128)S(1)}, f32[16,32,256]{2,1,0:T(8,128)}, f32[16,32,256]{2,1,0:T(8,128)}, f32[16,32,256]{2,1,0:T(8,128)}, f32[16,3...) custom-call(f32[128,16,256]{2,1,0:T(8,128)} %bitcast.6, f32[3,3,3,32]{3,2,1,0:T(4,128)} %bitcast.8, f32[32,32]{1,0:T(8,128)} %point_hbm.1, ...), custom_call_target="tpu_custom_call" | custom-call | flops 8000000000 | tf_op jit(solution)/shard_map/own_cells/pallas_call | solution.py:464
  17.8 4.2 %all-to-all-done.data_ref = f32[8,16,8,128]{3,2,1,0:T(8,128)S(1)} async-done(((f32[8,16,8,128]{3,2,1,0:T(8,128)}), f32[8,16,8,128]{3,2,1,0:T(8,128)S(1)}, u32[]{:S(2)}, u32[]{:S(2)}) %all-to-all-start) | async-done | bytes 524320 | tf_op jit(solution)/shard_map/all_to_all | solution.py:436
  22.0 0.0 copy-done.2
  22.0 1.0 %forward_y.1 = f32[32,8,128]{2,1,0:T(8,128)} custom-call(f32[8,16,8,128]{3,2,1,0:T(8,128)S(1)} %all-to-all-done.data_ref, bf16[2,64,256]{2,1,0:T(8,128)(2,1)S(1)} %copy-done.2), custom_call_target="tpu_custom_call" | custom-call | tf_op jit(solution)/shard_map/forward_y/pallas_call | solution.py:490
  23.0 10.5 %all-to-all-start.1 = ((f32[32,8,128]{2,1,0:T(8,128)}), f32[32,8,128]{2,1,0:T(8,128)S(1)}, u32[]{:S(2)}, u32[]{:S(2)}) async-start(f32[32,8,128]{2,1,0:T(8,128)} %forward_y.1), calls=%async_computation.1 | async-start | bytes 262144 | tf_op jit(solution)/shard_map/all_to_all | solution.py:436
  33.5 0.0 copy-start.3
  33.5 3.0 %weights.1.weight_ref = f32[2,32,32,128]{3,2,1,0:T(8,128)S(1)} custom-call(f32[2,32,128,32]{3,2,1,0:T(8,128)} %bitcast.7), custom_call_target="tpu_custom_call" | custom-call | flops 8000000000 | tf_op jit(solution)/shard_map/weights/pallas_call | solution.py:495
  36.6 0.3 collective-permute-start
  36.9 1.5 %collective-permute-start.1 = (f32[16,32,256]{2,1,0:T(8,128)}, f32[16,32,256]{2,1,0:T(8,128)}, u32[]{:S(2)}, u32[]{:S(2)}) collective-permute-start(f32[16,32,256]{2,1,0:T(8,128)} %get-tuple-element.40), channel_id=1, source_target_pairs={{8,16},{24,32},{40,48},{56,64},{72,80},{88,96},{104,112},{120,128}... | collective-permute-start | bytes 1572872 | tf_op jit(solution)/shard_map/ppermute | solution.py:432
  38.5 4.4 %all-to-all-done.1.data_ref = f32[32,8,128]{2,1,0:T(8,128)S(1)} async-done(((f32[32,8,128]{2,1,0:T(8,128)}), f32[32,8,128]{2,1,0:T(8,128)S(1)}, u32[]{:S(2)}, u32[]{:S(2)}) %all-to-all-start.1) | async-done | bytes 131104 | tf_op jit(solution)/shard_map/all_to_all | solution.py:436
  42.8 0.0 copy-done.3
  42.8 1.9 %middle.1 = f32[32,8,128]{2,1,0:T(8,128)} custom-call(f32[32,8,128]{2,1,0:T(8,128)S(1)} %all-to-all-done.1.data_ref, f32[2,32,32,128]{3,2,1,0:T(8,128)S(1)} %weights.1.weight_ref, bf16[2,64,256]{2,1,0:T(8,128)(2,1)S(1)} %copy-done.3, bf16[2,256,64]{2,1,0:T(8,128)(2,1)} %constant.15.clone.inverse_hbm), custom_call_target="tpu_custom_call" | custom-call | flops 3000000000 | tf_op jit(solution)/shard_map/middle/pallas_call | solution.py:507
  44.7 4.1 %all-to-all-start.2 = ((f32[32,8,128]{2,1,0:T(8,128)}), f32[32,8,128]{2,1,0:T(8,128)S(1)}, u32[]{:S(2)}, u32[]{:S(2)}) async-start(f32[32,8,128]{2,1,0:T(8,128)} %middle.1), calls=%async_computation.2 | async-start | bytes 262144 | tf_op jit(solution)/shard_map/all_to_all | solution.py:436
  48.8 0.0 collective-permute-done.inner_ref.inner_hbm
  48.8 3.1 %collective-permute-done.1.outer_ref.outer_hbm = f32[16,32,256]{2,1,0:T(8,128)} collective-permute-done((f32[16,32,256]{2,1,0:T(8,128)}, f32[16,32,256]{2,1,0:T(8,128)}, u32[]{:S(2)}, u32[]{:S(2)}) %collective-permute-start.1) | collective-permute-done | bytes 524320 | tf_op jit(solution)/shard_map/ppermute | solution.py:432
  51.9 0.0 copy-start
  51.9 1.1 %rims.1 = (f32[6,32,256]{2,1,0:T(8,128)S(1)}, f32[6,32,256]{2,1,0:T(8,128)S(1)}) custom-call(f32[2,4,32,256]{3,2,1,0:T(8,128)} %get-tuple-element.38.rows_ref, f32[16,32,256]{2,1,0:T(8,128)} %collective-permute-done.inner_ref.inner_hbm, f32[16,32,256]{2,1,0:T(8,128)} %collective-permute-done.1.outer_ref.outer_hbm), custom_call_target="tpu_custom_call" | custom-call | flops 2000000000 | tf_op jit(solution)/shard_map/rims/pallas_call | solution.py:519
  53.0 1.3 %collective-permute-start.2 = (f32[6,32,256]{2,1,0:T(8,128)S(1)}, f32[6,32,256]{2,1,0:T(8,128)S(1)}, u32[]{:S(2)}, u32[]{:S(2)}) collective-permute-start(f32[6,32,256]{2,1,0:T(8,128)S(1)} %get-tuple-element.43), channel_id=1, source_target_pairs={{0,1},{1,2},{2,3},{3,4},{4,5},{5,6},{6,7},{7,0},{8,9},{9,10},{10,1... | collective-permute-start | bytes 589832 | tf_op jit(solution)/shard_map/ppermute | solution.py:426
  54.3 3.9 %collective-permute-start.3 = (f32[6,32,256]{2,1,0:T(8,128)S(1)}, f32[6,32,256]{2,1,0:T(8,128)S(1)}, u32[]{:S(2)}, u32[]{:S(2)}) collective-permute-start(f32[6,32,256]{2,1,0:T(8,128)S(1)} %get-tuple-element.44), channel_id=1, source_target_pairs={{0,7},{1,0},{2,1},{3,2},{4,3},{5,4},{6,5},{7,6},{8,15},{9,8},{10,9... | collective-permute-start | bytes 589832 | tf_op jit(solution)/shard_map/ppermute | solution.py:426
  58.2 0.1 all-to-all-done.2.data_ref
  58.3 0.0 copy-done
  58.3 1.2 %inverse_y.1 = f32[8,16,8,128]{3,2,1,0:T(8,128)} custom-call(f32[32,8,128]{2,1,0:T(8,128)S(1)} %all-to-all-done.2.data_ref, bf16[2,256,64]{2,1,0:T(8,128)(2,1)S(1)} %copy-done), custom_call_target="tpu_custom_call" | custom-call | tf_op jit(solution)/shard_map/inverse_y/pallas_call | solution.py:530
  59.5 3.7 %all-to-all-start.3 = ((f32[8,16,8,128]{3,2,1,0:T(8,128)}), f32[8,16,8,128]{3,2,1,0:T(8,128)S(1)}, u32[]{:S(2)}, u32[]{:S(2)}) async-start(f32[8,16,8,128]{3,2,1,0:T(8,128)} %inverse_y.1), calls=%async_computation.3 | async-start | bytes 1048576 | tf_op jit(solution)/shard_map/all_to_all | solution.py:436
  63.1 0.2 collective-permute-done.2.left_ref
  63.4 0.0 collective-permute-done.3.right_ref
  63.4 0.0 copy-start.1
  63.4 3.2 %edge_cells.1.base_ref = f32[4,16,32,256]{3,2,1,0:T(8,128)S(1)} custom-call(f32[4,16,32,256]{3,2,1,0:T(8,128)S(1)} %get-tuple-element.46.base_ref, f32[16,32,256]{2,1,0:T(8,128)} %collective-permute-done.inner_ref.inner_hbm, f32[16,32,256]{2,1,0:T(8,128)} %collective-permute-done.1.outer_ref.outer_hbm, ...), custom_call_target="tpu_custom_call", output_to_operand_aliasing={{}: (0, {})} | custom-call | flops 40000000000 | tf_op jit(solution)/shard_map/edge_cells/pallas_call | solution.py:536
  66.6 7.3 %all-to-all-done.3.data_ref = f32[8,16,8,128]{3,2,1,0:T(8,128)S(1)} async-done(((f32[8,16,8,128]{3,2,1,0:T(8,128)}), f32[8,16,8,128]{3,2,1,0:T(8,128)S(1)}, u32[]{:S(2)}, u32[]{:S(2)}) %all-to-all-start.3) | async-done | bytes 524320 | tf_op jit(solution)/shard_map/all_to_all | solution.py:436
  73.9 0.0 copy-done.1
  73.9 3.1 %final.1 = f32[128,16,256]{2,1,0:T(8,128)} custom-call(f32[8,16,8,128]{3,2,1,0:T(8,128)S(1)} %all-to-all-done.3.data_ref, f32[4,16,32,256]{3,2,1,0:T(8,128)S(1)} %edge_cells.1.base_ref, bf16[2,64,256]{2,1,0:T(8,128)(2,1)S(1)} %copy-done.1), custom_call_target="tpu_custom_call" | custom-call | tf_op jit(solution)/shard_map/final/pallas_call | solution.py:549
Async XLA Ops:
  3.8 18.2 %all-to-all-start = ((f32[8,16,8,128]{3,2,1,0:T(8,128)}), f32[8,16,8,128]{3,2,1,0:T(8,128)S(1)}, u32[]{:S(2)}, u32[]{:S(2)}) async-start(f32[8,16,8,128]{3,2,1,0:T(8,128)} %forward_z.1), calls=%async_computation | async-start | bytes 1048576 | tf_op jit(solution)/shard_map/all_to_all | solution.py:436
  11.3 10.7 %copy-start.2 = (bf16[2,64,256]{2,1,0:T(8,128)(2,1)S(1)}, bf16[2,64,256]{2,1,0:T(8,128)(2,1)}, u32[]{:S(2)}) copy-start(bf16[2,64,256]{2,1,0:T(8,128)(2,1)} %constant.13.clone.table_ref) | copy-start | bytes 196612
  23.0 19.8 %all-to-all-start.1 = ((f32[32,8,128]{2,1,0:T(8,128)}), f32[32,8,128]{2,1,0:T(8,128)S(1)}, u32[]{:S(2)}, u32[]{:S(2)}) async-start(f32[32,8,128]{2,1,0:T(8,128)} %forward_y.1), calls=%async_computation.1 | async-start | bytes 262144 | tf_op jit(solution)/shard_map/all_to_all | solution.py:436
  33.5 9.3 %copy-start.3 = (bf16[2,64,256]{2,1,0:T(8,128)(2,1)S(1)}, bf16[2,64,256]{2,1,0:T(8,128)(2,1)}, u32[]{:S(2)}) copy-start(bf16[2,64,256]{2,1,0:T(8,128)(2,1)} %constant.14.clone.forward_ref) | copy-start | bytes 196612
  36.6 12.3 %collective-permute-start = (f32[16,32,256]{2,1,0:T(8,128)}, f32[16,32,256]{2,1,0:T(8,128)}, u32[]{:S(2)}, u32[]{:S(2)}) collective-permute-start(f32[16,32,256]{2,1,0:T(8,128)} %get-tuple-element.39), channel_id=1, source_target_pairs={{0,8},{16,24},{32,40},{48,56},{64,72},{80,88},{96,104},{112,120},{... | collective-permute-start | bytes 1572872 | tf_op jit(solution)/shard_map/ppermute | solution.py:432
  36.9 15.0 %collective-permute-start.1 = (f32[16,32,256]{2,1,0:T(8,128)}, f32[16,32,256]{2,1,0:T(8,128)}, u32[]{:S(2)}, u32[]{:S(2)}) collective-permute-start(f32[16,32,256]{2,1,0:T(8,128)} %get-tuple-element.40), channel_id=1, source_target_pairs={{8,16},{24,32},{40,48},{56,64},{72,80},{88,96},{104,112},{120,128}... | collective-permute-start | bytes 1572872 | tf_op jit(solution)/shard_map/ppermute | solution.py:432
  44.7 13.6 %all-to-all-start.2 = ((f32[32,8,128]{2,1,0:T(8,128)}), f32[32,8,128]{2,1,0:T(8,128)S(1)}, u32[]{:S(2)}, u32[]{:S(2)}) async-start(f32[32,8,128]{2,1,0:T(8,128)} %middle.1), calls=%async_computation.2 | async-start | bytes 262144 | tf_op jit(solution)/shard_map/all_to_all | solution.py:436
  51.9 6.4 %copy-start = (bf16[2,256,64]{2,1,0:T(8,128)(2,1)S(1)}, bf16[2,256,64]{2,1,0:T(8,128)(2,1)}, u32[]{:S(2)}) copy-start(bf16[2,256,64]{2,1,0:T(8,128)(2,1)} %constant.16.clone.table_ref) | copy-start | bytes 196612
  53.0 10.4 %collective-permute-start.2 = (f32[6,32,256]{2,1,0:T(8,128)S(1)}, f32[6,32,256]{2,1,0:T(8,128)S(1)}, u32[]{:S(2)}, u32[]{:S(2)}) collective-permute-start(f32[6,32,256]{2,1,0:T(8,128)S(1)} %get-tuple-element.43), channel_id=1, source_target_pairs={{0,1},{1,2},{2,3},{3,4},{4,5},{5,6},{6,7},{7,0},{8,9},{9,10},{10,1... | collective-permute-start | bytes 589832 | tf_op jit(solution)/shard_map/ppermute | solution.py:426
  54.3 9.1 %collective-permute-start.3 = (f32[6,32,256]{2,1,0:T(8,128)S(1)}, f32[6,32,256]{2,1,0:T(8,128)S(1)}, u32[]{:S(2)}, u32[]{:S(2)}) collective-permute-start(f32[6,32,256]{2,1,0:T(8,128)S(1)} %get-tuple-element.44), channel_id=1, source_target_pairs={{0,7},{1,0},{2,1},{3,2},{4,3},{5,4},{6,5},{7,6},{8,15},{9,8},{10,9... | collective-permute-start | bytes 589832 | tf_op jit(solution)/shard_map/ppermute | solution.py:426
  59.5 14.4 %all-to-all-start.3 = ((f32[8,16,8,128]{3,2,1,0:T(8,128)}), f32[8,16,8,128]{3,2,1,0:T(8,128)S(1)}, u32[]{:S(2)}, u32[]{:S(2)}) async-start(f32[8,16,8,128]{3,2,1,0:T(8,128)} %inverse_y.1), calls=%async_computation.3 | async-start | bytes 1048576 | tf_op jit(solution)/shard_map/all_to_all | solution.py:436
  63.4 10.5 %copy-start.1 = (bf16[2,64,256]{2,1,0:T(8,128)(2,1)S(1)}, bf16[2,64,256]{2,1,0:T(8,128)(2,1)}, u32[]{:S(2)}) copy-start(bf16[2,64,256]{2,1,0:T(8,128)(2,1)} %constant.17.clone.table_ref) | copy-start | bytes 196612

commit v11 on v10

--- a/solution.py
+++ b/solution.py
@@ -173,14 +173,31 @@
             out[pl.ds(2 * k + part, 32, stride=8), :] = tile[32 * part : 32 * part + 32]
 
 
-def inverse_y(data_ref, table_ref, out_ref):
+def inverse_y(data_ref, table_ref, out_ref, ready, sems):
     rows = data_ref.reshape(256, 128)
-    out = out_ref.reshape(1024, 128)
+    out = ready.reshape(1024, 128)
+    pairs = []
     for k in range(4):
         parts = [rows[pl.ds(2 * k + part, 32, stride=8), :] for part in range(2)]
-        result = table_dot(table_ref, jnp.concatenate(parts, axis=0))
-        for part in range(2):
-            out[pl.ds(2 * k + part, 128, stride=8), :] = result[128 * part : 128 * part + 128]
+        pairs.append(split(jnp.concatenate(parts, axis=0)))
+    copies = []
+    for half in range(2):
+        tables = [
+            jnp.concatenate(
+                [table_ref[i, pl.ds(128 * part + 64 * half, 64)] for part in range(2)], axis=0
+            )
+            for i in range(2)
+        ]
+        for k, (high, low) in enumerate(pairs):
+            result = mm(tables[0], high) + mm(tables[0], low) + mm(tables[1], high)
+            for part in range(2):
+                out[pl.ds(512 * half + 2 * k + part, 64, stride=8), :] = result[
+                    64 * part : 64 * part + 64
+                ]
+        span = pl.ds(4 * half, 4)
+        copies.append(pltpu.make_async_copy(ready.at[span], out_ref.at[span], sems.at[half]))
+        copies[-1].start()
+    wait_all(copies)
 
 
 def final(data_ref, base_ref, table_ref, out_ref, held, sems):
@@ -501,8 +518,8 @@
         scratch_shapes=[pltpu.VMEM((2, 32, 128, 32), F32), dma((8,))],
     )(far(after_all(spec_weight, ychunks).reshape(2, 32, 128, 32)))
     inner, outer, packed = lax.optimization_barrier((inner, outer, packed))
+    outer = swapped("gx", far(outer), 1)
     inner = swapped("gx", far(inner), 0)
-    outer = swapped("gx", far(outer), 1)
     yall, packed = lax.optimization_barrier((yall, packed))
     (xchunks,) = call(
         middle,
@@ -527,9 +544,13 @@
     left = shifted("gy", top, 1)
     right = shifted("gy", bottom, -1)
     xall, top, bottom = lax.optimization_barrier((xall, top, bottom))
-    (back,) = call(inverse_y, [((8, 16, 8, 128), plain)], 2)(
-        near(xall), near(jnp.asarray(tab["iy"]))
-    )
+    (back,) = call(
+        inverse_y,
+        [((8, 16, 8, 128), plain)],
+        2,
+        out_specs=[ANY],
+        scratch_shapes=[pltpu.VMEM((8, 16, 8, 128), F32), dma((2,))],
+    )(near(xall), near(jnp.asarray(tab["iy"])))
 
     ball = exchange(back, "gy")
     left, right, _ = lax.optimization_barrier((left, right, back))

time: 77.7 us -> 77.6 us (level)
  no operation moved by 1% of the time
where the time goes in v11:
time: 77.6 us; the launch traced here: 77 us
  starting transfers between devices  32.8 us (42%)
  Pallas kernels  24.7 us (32%)
  waiting for transfers between devices  19.3 us (25%)
    all_to_all x4, starting transfers between devices, exchange(): return lax.all_to_all(value, axis, split_axis=0, concat_axis=0, tiled=True)  25.8 us
    all_to_all x4, waiting for transfers between devices, exchange(): return lax.all_to_all(value, axis, split_axis=0, concat_axis=0, tiled=True)  15.9 us
    pallas_call x1, Pallas kernels, on_device(): call(own_cells, [((4, 16, 32, 256), kept_near), ((16, 32, 256), pltpu.HBM...  6.45 us
    ppermute x2, starting transfers between devices, shifted(): lax.ppermute(value, axis, [(i, (i + step) % count) for i in range(count)])  5.16 us
    pallas_call x1, Pallas kernels, on_device(): call(forward_z, [((8, 16, 8, 128), plain)], 2, in_specs=[HBM] * 2, out_sp...  3.81 us
    pallas_call x1, Pallas kernels, on_device(): call(edge_cells, [((4, 16, 32, 256), kept_near)], 8, 40, in_specs=[VMEM]...  3.18 us
    pallas_call x1, Pallas kernels, on_device(): call(final, [((128, 16, 256), plain)], 3, out_specs=[ANY], scratch_shapes...  3.08 us
    ppermute x2, waiting for transfers between devices, swapped(): return lax.ppermute(value, axis, pairs + [(j, i) for i, j in pairs])  3.07 us
  transfers between devices with their start and end apart: 8, of which 6 were waited for; matrix products, arithmetic and copies ran while one was open for 0% of the time, Pallas kernels for 22%

profile of v11, /device:TPU:1, one launch (start us, length us, event | category | flops | bytes accessed | tf_op | source)
XLA Modules:
  0.0 77.0 jit_solution(7879910097497256771)
XLA Ops:
  0.0 3.8 %forward_z.1 = f32[8,16,8,128]{3,2,1,0:T(8,128)} custom-call(f32[128,16,256]{2,1,0:T(8,128)} %bitcast.5, bf16[128,256]{1,0:T(8,128)(2,1)} %constant.12.clone.table_ref), custom_call_target="tpu_custom_call" | custom-call | tf_op jit(solution)/shard_map/forward_z/pallas_call | solution.py:464
  3.8 7.5 %all-to-all-start = ((f32[8,16,8,128]{3,2,1,0:T(8,128)}), f32[8,16,8,128]{3,2,1,0:T(8,128)S(1)}, u32[]{:S(2)}, u32[]{:S(2)}) async-start(f32[8,16,8,128]{3,2,1,0:T(8,128)} %forward_z.1), calls=%async_computation | async-start | bytes 1048576 | tf_op jit(solution)/shard_map/all_to_all | solution.py:453
  11.3 0.0 copy-start.2
  11.3 6.5 %own_cells.1 = (f32[4,16,32,256]{3,2,1,0:T(8,128)S(1)}, f32[16,32,256]{2,1,0:T(8,128)}, f32[16,32,256]{2,1,0:T(8,128)}, f32[16,32,256]{2,1,0:T(8,128)}, f32[16,3...) custom-call(f32[128,16,256]{2,1,0:T(8,128)} %bitcast.6, f32[3,3,3,32]{3,2,1,0:T(4,128)} %bitcast.8, f32[32,32]{1,0:T(8,128)} %point_hbm.1, ...), custom_call_target="tpu_custom_call" | custom-call | flops 8000000000 | tf_op jit(solution)/shard_map/own_cells/pallas_call | solution.py:481
  17.8 4.2 %all-to-all-done.data_ref = f32[8,16,8,128]{3,2,1,0:T(8,128)S(1)} async-done(((f32[8,16,8,128]{3,2,1,0:T(8,128)}), f32[8,16,8,128]{3,2,1,0:T(8,128)S(1)}, u32[]{:S(2)}, u32[]{:S(2)}) %all-to-all-start) | async-done | bytes 524320 | tf_op jit(solution)/shard_map/all_to_all | solution.py:453
  22.0 0.0 copy-done.2
  22.0 1.0 %forward_y.1 = f32[32,8,128]{2,1,0:T(8,128)} custom-call(f32[8,16,8,128]{3,2,1,0:T(8,128)S(1)} %all-to-all-done.data_ref, bf16[2,64,256]{2,1,0:T(8,128)(2,1)S(1)} %copy-done.2), custom_call_target="tpu_custom_call" | custom-call | tf_op jit(solution)/shard_map/forward_y/pallas_call | solution.py:507
  23.0 10.5 %all-to-all-start.1 = ((f32[32,8,128]{2,1,0:T(8,128)}), f32[32,8,128]{2,1,0:T(8,128)S(1)}, u32[]{:S(2)}, u32[]{:S(2)}) async-start(f32[32,8,128]{2,1,0:T(8,128)} %forward_y.1), calls=%async_computation.1 | async-start | bytes 262144 | tf_op jit(solution)/shard_map/all_to_all | solution.py:453
  33.5 0.0 copy-start.3
  33.5 3.0 %weights.1.weight_ref = f32[2,32,32,128]{3,2,1,0:T(8,128)S(1)} custom-call(f32[2,32,128,32]{3,2,1,0:T(8,128)} %bitcast.7), custom_call_target="tpu_custom_call" | custom-call | flops 8000000000 | tf_op jit(solution)/shard_map/weights/pallas_call | solution.py:512
  36.6 0.3 collective-permute-start
  36.9 1.5 %collective-permute-start.1 = (f32[16,32,256]{2,1,0:T(8,128)}, f32[16,32,256]{2,1,0:T(8,128)}, u32[]{:S(2)}, u32[]{:S(2)}) collective-permute-start(f32[16,32,256]{2,1,0:T(8,128)} %get-tuple-element.40), channel_id=1, source_target_pairs={{8,16},{24,32},{40,48},{56,64},{72,80},{88,96},{104,112},{120,128}... | collective-permute-start | bytes 1572872 | tf_op jit(solution)/shard_map/ppermute | solution.py:449
  38.5 4.4 %all-to-all-done.1.data_ref = f32[32,8,128]{2,1,0:T(8,128)S(1)} async-done(((f32[32,8,128]{2,1,0:T(8,128)}), f32[32,8,128]{2,1,0:T(8,128)S(1)}, u32[]{:S(2)}, u32[]{:S(2)}) %all-to-all-start.1) | async-done | bytes 131104 | tf_op jit(solution)/shard_map/all_to_all | solution.py:453
  42.8 0.0 copy-done.3
  42.8 1.9 %middle.1 = f32[32,8,128]{2,1,0:T(8,128)} custom-call(f32[32,8,128]{2,1,0:T(8,128)S(1)} %all-to-all-done.1.data_ref, f32[2,32,32,128]{3,2,1,0:T(8,128)S(1)} %weights.1.weight_ref, bf16[2,64,256]{2,1,0:T(8,128)(2,1)S(1)} %copy-done.3, bf16[2,256,64]{2,1,0:T(8,128)(2,1)} %constant.15.clone.inverse_hbm), custom_call_target="tpu_custom_call" | custom-call | flops 3000000000 | tf_op jit(solution)/shard_map/middle/pallas_call | solution.py:524
  44.7 4.1 %all-to-all-start.2 = ((f32[32,8,128]{2,1,0:T(8,128)}), f32[32,8,128]{2,1,0:T(8,128)S(1)}, u32[]{:S(2)}, u32[]{:S(2)}) async-start(f32[32,8,128]{2,1,0:T(8,128)} %middle.1), calls=%async_computation.2 | async-start | bytes 262144 | tf_op jit(solution)/shard_map/all_to_all | solution.py:453
  48.8 0.0 collective-permute-done.inner_ref.inner_hbm
  48.8 3.1 %collective-permute-done.1.outer_ref.outer_hbm = f32[16,32,256]{2,1,0:T(8,128)} collective-permute-done((f32[16,32,256]{2,1,0:T(8,128)}, f32[16,32,256]{2,1,0:T(8,128)}, u32[]{:S(2)}, u32[]{:S(2)}) %collective-permute-start.1) | collective-permute-done | bytes 524320 | tf_op jit(solution)/shard_map/ppermute | solution.py:449
  51.9 0.0 copy-start
  51.9 1.1 %rims.1 = (f32[6,32,256]{2,1,0:T(8,128)S(1)}, f32[6,32,256]{2,1,0:T(8,128)S(1)}) custom-call(f32[2,4,32,256]{3,2,1,0:T(8,128)} %get-tuple-element.38.rows_ref, f32[16,32,256]{2,1,0:T(8,128)} %collective-permute-done.inner_ref.inner_hbm, f32[16,32,256]{2,1,0:T(8,128)} %collective-permute-done.1.outer_ref.outer_hbm), custom_call_target="tpu_custom_call" | custom-call | flops 2000000000 | tf_op jit(solution)/shard_map/rims/pallas_call | solution.py:536
  53.0 1.3 %collective-permute-start.2 = (f32[6,32,256]{2,1,0:T(8,128)S(1)}, f32[6,32,256]{2,1,0:T(8,128)S(1)}, u32[]{:S(2)}, u32[]{:S(2)}) collective-permute-start(f32[6,32,256]{2,1,0:T(8,128)S(1)} %get-tuple-element.43), channel_id=1, source_target_pairs={{0,1},{1,2},{2,3},{3,4},{4,5},{5,6},{6,7},{7,0},{8,9},{9,10},{10,1... | collective-permute-start | bytes 589832 | tf_op jit(solution)/shard_map/ppermute | solution.py:443
  54.3 3.9 %collective-permute-start.3 = (f32[6,32,256]{2,1,0:T(8,128)S(1)}, f32[6,32,256]{2,1,0:T(8,128)S(1)}, u32[]{:S(2)}, u32[]{:S(2)}) collective-permute-start(f32[6,32,256]{2,1,0:T(8,128)S(1)} %get-tuple-element.44), channel_id=1, source_target_pairs={{0,7},{1,0},{2,1},{3,2},{4,3},{5,4},{6,5},{7,6},{8,15},{9,8},{10,9... | collective-permute-start | bytes 589832 | tf_op jit(solution)/shard_map/ppermute | solution.py:443
  58.2 0.1 all-to-all-done.2.data_ref
  58.3 0.0 copy-done
  58.3 1.1 %inverse_y.1 = f32[8,16,8,128]{3,2,1,0:T(8,128)} custom-call(f32[32,8,128]{2,1,0:T(8,128)S(1)} %all-to-all-done.2.data_ref, bf16[2,256,64]{2,1,0:T(8,128)(2,1)S(1)} %copy-done), custom_call_target="tpu_custom_call" | custom-call | tf_op jit(solution)/shard_map/inverse_y/pallas_call | solution.py:547
  59.4 3.7 %all-to-all-start.3 = ((f32[8,16,8,128]{3,2,1,0:T(8,128)}), f32[8,16,8,128]{3,2,1,0:T(8,128)S(1)}, u32[]{:S(2)}, u32[]{:S(2)}) async-start(f32[8,16,8,128]{3,2,1,0:T(8,128)} %inverse_y.1), calls=%async_computation.3 | async-start | bytes 1048576 | tf_op jit(solution)/shard_map/all_to_all | solution.py:453
  63.1 0.3 collective-permute-done.2.left_ref
  63.4 0.0 collective-permute-done.3.right_ref
  63.4 0.0 copy-start.1
  63.4 3.2 %edge_cells.1.base_ref = f32[4,16,32,256]{3,2,1,0:T(8,128)S(1)} custom-call(f32[4,16,32,256]{3,2,1,0:T(8,128)S(1)} %get-tuple-element.46.base_ref, f32[16,32,256]{2,1,0:T(8,128)} %collective-permute-done.inner_ref.inner_hbm, f32[16,32,256]{2,1,0:T(8,128)} %collective-permute-done.1.outer_ref.outer_hbm, ...), custom_call_target="tpu_custom_call", output_to_operand_aliasing={{}: (0, {})} | custom-call | flops 40000000000 | tf_op jit(solution)/shard_map/edge_cells/pallas_call | solution.py:557
  66.6 7.2 %all-to-all-done.3.data_ref = f32[8,16,8,128]{3,2,1,0:T(8,128)S(1)} async-done(((f32[8,16,8,128]{3,2,1,0:T(8,128)}), f32[8,16,8,128]{3,2,1,0:T(8,128)S(1)}, u32[]{:S(2)}, u32[]{:S(2)}) %all-to-all-start.3) | async-done | bytes 524320 | tf_op jit(solution)/shard_map/all_to_all | solution.py:453
  73.8 0.0 copy-done.1
  73.8 3.1 %final.1 = f32[128,16,256]{2,1,0:T(8,128)} custom-call(f32[8,16,8,128]{3,2,1,0:T(8,128)S(1)} %all-to-all-done.3.data_ref, f32[4,16,32,256]{3,2,1,0:T(8,128)S(1)} %edge_cells.1.base_ref, bf16[2,64,256]{2,1,0:T(8,128)(2,1)S(1)} %copy-done.1), custom_call_target="tpu_custom_call" | custom-call | tf_op jit(solution)/shard_map/final/pallas_call | solution.py:570
Async XLA Ops:
  3.8 18.2 %all-to-all-start = ((f32[8,16,8,128]{3,2,1,0:T(8,128)}), f32[8,16,8,128]{3,2,1,0:T(8,128)S(1)}, u32[]{:S(2)}, u32[]{:S(2)}) async-start(f32[8,16,8,128]{3,2,1,0:T(8,128)} %forward_z.1), calls=%async_computation | async-start | bytes 1048576 | tf_op jit(solution)/shard_map/all_to_all | solution.py:453
  11.3 10.7 %copy-start.2 = (bf16[2,64,256]{2,1,0:T(8,128)(2,1)S(1)}, bf16[2,64,256]{2,1,0:T(8,128)(2,1)}, u32[]{:S(2)}) copy-start(bf16[2,64,256]{2,1,0:T(8,128)(2,1)} %constant.13.clone.table_ref) | copy-start | bytes 196612
  23.0 19.8 %all-to-all-start.1 = ((f32[32,8,128]{2,1,0:T(8,128)}), f32[32,8,128]{2,1,0:T(8,128)S(1)}, u32[]{:S(2)}, u32[]{:S(2)}) async-start(f32[32,8,128]{2,1,0:T(8,128)} %forward_y.1), calls=%async_computation.1 | async-start | bytes 262144 | tf_op jit(solution)/shard_map/all_to_all | solution.py:453
  33.5 9.3 %copy-start.3 = (bf16[2,64,256]{2,1,0:T(8,128)(2,1)S(1)}, bf16[2,64,256]{2,1,0:T(8,128)(2,1)}, u32[]{:S(2)}) copy-start(bf16[2,64,256]{2,1,0:T(8,128)(2,1)} %constant.14.clone.forward_ref) | copy-start | bytes 196612
  36.6 12.3 %collective-permute-start = (f32[16,32,256]{2,1,0:T(8,128)}, f32[16,32,256]{2,1,0:T(8,128)}, u32[]{:S(2)}, u32[]{:S(2)}) collective-permute-start(f32[16,32,256]{2,1,0:T(8,128)} %get-tuple-element.39), channel_id=1, source_target_pairs={{0,8},{16,24},{32,40},{48,56},{64,72},{80,88},{96,104},{112,120},{... | collective-permute-start | bytes 1572872 | tf_op jit(solution)/shard_map/ppermute | solution.py:449
  36.9 15.0 %collective-permute-start.1 = (f32[16,32,256]{2,1,0:T(8,128)}, f32[16,32,256]{2,1,0:T(8,128)}, u32[]{:S(2)}, u32[]{:S(2)}) collective-permute-start(f32[16,32,256]{2,1,0:T(8,128)} %get-tuple-element.40), channel_id=1, source_target_pairs={{8,16},{24,32},{40,48},{56,64},{72,80},{88,96},{104,112},{120,128}... | collective-permute-start | bytes 1572872 | tf_op jit(solution)/shard_map/ppermute | solution.py:449
  44.7 13.6 %all-to-all-start.2 = ((f32[32,8,128]{2,1,0:T(8,128)}), f32[32,8,128]{2,1,0:T(8,128)S(1)}, u32[]{:S(2)}, u32[]{:S(2)}) async-start(f32[32,8,128]{2,1,0:T(8,128)} %middle.1), calls=%async_computation.2 | async-start | bytes 262144 | tf_op jit(solution)/shard_map/all_to_all | solution.py:453
  51.9 6.4 %copy-start = (bf16[2,256,64]{2,1,0:T(8,128)(2,1)S(1)}, bf16[2,256,64]{2,1,0:T(8,128)(2,1)}, u32[]{:S(2)}) copy-start(bf16[2,256,64]{2,1,0:T(8,128)(2,1)} %constant.16.clone.table_ref) | copy-start | bytes 196612
  53.0 10.4 %collective-permute-start.2 = (f32[6,32,256]{2,1,0:T(8,128)S(1)}, f32[6,32,256]{2,1,0:T(8,128)S(1)}, u32[]{:S(2)}, u32[]{:S(2)}) collective-permute-start(f32[6,32,256]{2,1,0:T(8,128)S(1)} %get-tuple-element.43), channel_id=1, source_target_pairs={{0,1},{1,2},{2,3},{3,4},{4,5},{5,6},{6,7},{7,0},{8,9},{9,10},{10,1... | collective-permute-start | bytes 589832 | tf_op jit(solution)/shard_map/ppermute | solution.py:443
  54.3 9.1 %collective-permute-start.3 = (f32[6,32,256]{2,1,0:T(8,128)S(1)}, f32[6,32,256]{2,1,0:T(8,128)S(1)}, u32[]{:S(2)}, u32[]{:S(2)}) collective-permute-start(f32[6,32,256]{2,1,0:T(8,128)S(1)} %get-tuple-element.44), channel_id=1, source_target_pairs={{0,7},{1,0},{2,1},{3,2},{4,3},{5,4},{6,5},{7,6},{8,15},{9,8},{10,9... | collective-permute-start | bytes 589832 | tf_op jit(solution)/shard_map/ppermute | solution.py:443
  59.4 14.4 %all-to-all-start.3 = ((f32[8,16,8,128]{3,2,1,0:T(8,128)}), f32[8,16,8,128]{3,2,1,0:T(8,128)S(1)}, u32[]{:S(2)}, u32[]{:S(2)}) async-start(f32[8,16,8,128]{3,2,1,0:T(8,128)} %inverse_y.1), calls=%async_computation.3 | async-start | bytes 1048576 | tf_op jit(solution)/shard_map/all_to_all | solution.py:453
  63.4 10.4 %copy-start.1 = (bf16[2,64,256]{2,1,0:T(8,128)(2,1)S(1)}, bf16[2,64,256]{2,1,0:T(8,128)(2,1)}, u32[]{:S(2)}) copy-start(bf16[2,64,256]{2,1,0:T(8,128)(2,1)} %constant.17.clone.table_ref) | copy-start | bytes 196612

commit v12 on v11

--- a/solution.py
+++ b/solution.py
@@ -95,8 +95,8 @@
     ]
 
 
-def odd():
-    return lax.rem(lax.axis_index("gx"), 2)
+def odd(axis="gx"):
+    return lax.rem(lax.axis_index(axis), 2)
 
 
 def start_all(copies):
@@ -249,16 +249,16 @@
                 rows[pl.ds(1024 * part + m, 32, stride=32), :] = tile
 
 
-def rims(rows_ref, inner_ref, outer_ref, top_ref, bottom_ref, sems):
+def rims(rows_ref, inner_ref, outer_ref, inner_out, outer_out, sems):
     copies = []
-    for side, out_ref in enumerate((bottom_ref, top_ref)):
+    for at, (out_ref, side) in enumerate(((inner_out, 1 - odd("gy")), (outer_out, odd("gy")))):
         moves = [
             (rows_ref.at[side], out_ref.at[pl.ds(1, 4)]),
             (inner_ref.at[15 * side], out_ref.at[5 - 5 * odd()]),
             (outer_ref.at[15 * side], out_ref.at[5 * odd()]),
         ]
         copies += [
-            pltpu.make_async_copy(src, dst, sems.at[side, i]) for i, (src, dst) in enumerate(moves)
+            pltpu.make_async_copy(src, dst, sems.at[at, i]) for i, (src, dst) in enumerate(moves)
         ]
     start_all(copies)
     wait_all(copies)
@@ -356,12 +356,15 @@
 
 
 def edge_cells(
-    base_ref, inner_hbm, outer_hbm, third_hbm, last_hbm, left_ref, right_ref, dw_hbm,
-    out_ref, halo_ref, third_ref, last_ref, tap_ref, dw_ref, sems
+    base_ref, inner_hbm, outer_hbm, third_hbm, last_hbm, inner_rim, outer_rim, dw_hbm,
+    out_ref, halo_ref, rim_ref, third_ref, last_ref, tap_ref, dw_ref, sems
 ):
     before_ref, after_ref = halo_ref.at[0], halo_ref.at[1]
+    left_ref, right_ref = rim_ref.at[0], rim_ref.at[1]
     moves = [
         (dw_hbm, dw_ref),
+        (inner_rim, rim_ref.at[1 - odd("gy")]),
+        (outer_rim, rim_ref.at[odd("gy")]),
         (inner_hbm, halo_ref.at[1 - odd()]),
         (outer_hbm, halo_ref.at[odd()]),
         (third_hbm, third_ref),
@@ -371,7 +374,7 @@
         pltpu.make_async_copy(src, dst, sems.at[i]) for i, (src, dst) in enumerate(moves)
     ]
     start_all(copies)
-    copies[0].wait()
+    wait_all(copies[:3])
     spread_taps(dw_ref, tap_ref)
     for b, y, source in ((0, 0, left_ref), (2, 15, right_ref)):
         for tile in range(4):
@@ -382,7 +385,7 @@
                     load = lambda lanes: source[x + a, chans, lanes]
                     add_taps(sums, tap_ref, chans, 9 * a + 3 * b, load)
                 out_ref[x, y, chans, :] = base_ref[x, y, chans, :] + shift_sum(sums)
-    wait_all(copies[1:])
+    wait_all(copies[3:])
 
     def line(y, before_rows, after_rows, shifts):
         for a, x, rows in ((0, 0, before_rows), (2, 3, after_rows)):
@@ -541,8 +544,8 @@
         in_specs=[HBM] * 3,
         scratch_shapes=[dma((2, 3))],
     )(far(own_rims), inner, outer)
-    left = shifted("gy", top, 1)
-    right = shifted("gy", bottom, -1)
+    left = swapped("gy", top, 0)
+    right = swapped("gy", bottom, 1)
     xall, top, bottom = lax.optimization_barrier((xall, top, bottom))
     (back,) = call(
         inverse_y,
@@ -560,8 +563,9 @@
         8,
         40,
         in_specs=[VMEM] + [ANY] * 4 + [VMEM] * 2 + [ANY],
-        scratch_shapes=[pltpu.VMEM((2, 16, 32, 256), F32)] + [pltpu.VMEM((16, 32, 256), F32)] * 2
-        + [pltpu.VMEM((27, 32, 128), F32), pltpu.VMEM((3, 3, 3, 32), F32), dma((5,))],
+        scratch_shapes=[pltpu.VMEM((2, 16, 32, 256), F32), pltpu.VMEM((2, 6, 32, 256), F32)]
+        + [pltpu.VMEM((16, 32, 256), F32)] * 2
+        + [pltpu.VMEM((27, 32, 128), F32), pltpu.VMEM((3, 3, 3, 32), F32), dma((7,))],
         input_output_aliases={0: 0},
     )(
         near(base), inner, outer, far(third), far(last), near(left), near(right), far(taps)

time: 77.6 us -> 77.6 us (level)
  starting transfers between devices: 32.8 us -> 31 us
  waiting for transfers between devices: 19.3 us -> 20.6 us
    ppermute x2 -> x0, starting transfers between devices: 5.16 us -> none  [shifted(): lax.ppermute(value, axis, [(i, (i + step) % count) for i in range(count)])]
    ppermute x2 -> x4, starting transfers between devices: 1.87 us -> 5.21 us  [swapped(): return lax.ppermute(value, axis, pairs + [(j, i) for i, j in pairs])]
    ppermute x2 -> x4, waiting for transfers between devices: 3.07 us -> 4.14 us  [swapped(): return lax.ppermute(value, axis, pairs + [(j, i) for i, j in pairs])]
where the time goes in v12:
time: 77.6 us; the launch traced here: 77 us
  starting transfers between devices  31 us (40%)
  Pallas kernels  25.1 us (32%)
  waiting for transfers between devices  20.6 us (27%)
    all_to_all x4, starting transfers between devices, exchange(): return lax.all_to_all(value, axis, split_axis=0, concat_axis=0, tiled=True)  25.8 us
    all_to_all x4, waiting for transfers between devices, exchange(): return lax.all_to_all(value, axis, split_axis=0, concat_axis=0, tiled=True)  16.5 us
    pallas_call x1, Pallas kernels, on_device(): call(own_cells, [((4, 16, 32, 256), kept_near), ((16, 32, 256), pltpu.HBM...  6.45 us
    ppermute x4, starting transfers between devices, swapped(): return lax.ppermute(value, axis, pairs + [(j, i) for i, j in pairs])  5.21 us
    ppermute x4, waiting for transfers between devices, swapped(): return lax.ppermute(value, axis, pairs + [(j, i) for i, j in pairs])  4.14 us
    pallas_call x1, Pallas kernels, on_device(): call(forward_z, [((8, 16, 8, 128), plain)], 2, in_specs=[HBM] * 2, out_sp...  3.81 us
    pallas_call x1, Pallas kernels, on_device(): call(edge_cells, [((4, 16, 32, 256), kept_near)], 8, 40, in_specs=[VMEM]...  3.63 us
    pallas_call x1, Pallas kernels, on_device(): call(final, [((128, 16, 256), plain)], 3, out_specs=[ANY], scratch_shapes...  3.08 us
  transfers between devices with their start and end apart: 8, of which 6 were waited for; matrix products, arithmetic and copies ran while one was open for 0% of the time, Pallas kernels for 22%

profile of v12, /device:TPU:1, one launch (start us, length us, event | category | flops | bytes accessed | tf_op | source)
XLA Modules:
  0.0 77.0 jit_solution(17810840129146386812)
XLA Ops:
  0.0 3.8 %forward_z.1 = f32[8,16,8,128]{3,2,1,0:T(8,128)} custom-call(f32[128,16,256]{2,1,0:T(8,128)} %bitcast.5, bf16[128,256]{1,0:T(8,128)(2,1)} %constant.12.clone.table_ref), custom_call_target="tpu_custom_call" | custom-call | tf_op jit(solution)/shard_map/forward_z/pallas_call | solution.py:467
  3.8 7.5 %all-to-all-start = ((f32[8,16,8,128]{3,2,1,0:T(8,128)}), f32[8,16,8,128]{3,2,1,0:T(8,128)S(1)}, u32[]{:S(2)}, u32[]{:S(2)}) async-start(f32[8,16,8,128]{3,2,1,0:T(8,128)} %forward_z.1), calls=%async_computation | async-start | bytes 1048576 | tf_op jit(solution)/shard_map/all_to_all | solution.py:456
  11.3 0.0 copy-start.2
  11.3 6.5 %own_cells.1 = (f32[4,16,32,256]{3,2,1,0:T(8,128)S(1)}, f32[16,32,256]{2,1,0:T(8,128)}, f32[16,32,256]{2,1,0:T(8,128)}, f32[16,32,256]{2,1,0:T(8,128)}, f32[16,3...) custom-call(f32[128,16,256]{2,1,0:T(8,128)} %bitcast.6, f32[3,3,3,32]{3,2,1,0:T(4,128)} %bitcast.8, f32[32,32]{1,0:T(8,128)} %point_hbm.1, ...), custom_call_target="tpu_custom_call" | custom-call | flops 8000000000 | tf_op jit(solution)/shard_map/own_cells/pallas_call | solution.py:484
  17.8 4.2 %all-to-all-done.data_ref = f32[8,16,8,128]{3,2,1,0:T(8,128)S(1)} async-done(((f32[8,16,8,128]{3,2,1,0:T(8,128)}), f32[8,16,8,128]{3,2,1,0:T(8,128)S(1)}, u32[]{:S(2)}, u32[]{:S(2)}) %all-to-all-start) | async-done | bytes 524320 | tf_op jit(solution)/shard_map/all_to_all | solution.py:456
  22.0 0.0 copy-done.2
  22.0 1.0 %forward_y.1 = f32[32,8,128]{2,1,0:T(8,128)} custom-call(f32[8,16,8,128]{3,2,1,0:T(8,128)S(1)} %all-to-all-done.data_ref, bf16[2,64,256]{2,1,0:T(8,128)(2,1)S(1)} %copy-done.2), custom_call_target="tpu_custom_call" | custom-call | tf_op jit(solution)/shard_map/forward_y/pallas_call | solution.py:510
  23.0 10.5 %all-to-all-start.1 = ((f32[32,8,128]{2,1,0:T(8,128)}), f32[32,8,128]{2,1,0:T(8,128)S(1)}, u32[]{:S(2)}, u32[]{:S(2)}) async-start(f32[32,8,128]{2,1,0:T(8,128)} %forward_y.1), calls=%async_computation.1 | async-start | bytes 262144 | tf_op jit(solution)/shard_map/all_to_all | solution.py:456
  33.5 0.0 copy-start.3
  33.5 3.0 %weights.1.weight_ref = f32[2,32,32,128]{3,2,1,0:T(8,128)S(1)} custom-call(f32[2,32,128,32]{3,2,1,0:T(8,128)} %bitcast.7), custom_call_target="tpu_custom_call" | custom-call | flops 8000000000 | tf_op jit(solution)/shard_map/weights/pallas_call | solution.py:515
  36.6 0.3 collective-permute-start
  36.9 1.5 %collective-permute-start.1 = (f32[16,32,256]{2,1,0:T(8,128)}, f32[16,32,256]{2,1,0:T(8,128)}, u32[]{:S(2)}, u32[]{:S(2)}) collective-permute-start(f32[16,32,256]{2,1,0:T(8,128)} %get-tuple-element.40), channel_id=1, source_target_pairs={{8,16},{24,32},{40,48},{56,64},{72,80},{88,96},{104,112},{120,128}... | collective-permute-start | bytes 1572872 | tf_op jit(solution)/shard_map/ppermute | solution.py:452
  38.5 4.4 %all-to-all-done.1.data_ref = f32[32,8,128]{2,1,0:T(8,128)S(1)} async-done(((f32[32,8,128]{2,1,0:T(8,128)}), f32[32,8,128]{2,1,0:T(8,128)S(1)}, u32[]{:S(2)}, u32[]{:S(2)}) %all-to-all-start.1) | async-done | bytes 131104 | tf_op jit(solution)/shard_map/all_to_all | solution.py:456
  42.8 0.0 copy-done.3
  42.8 1.9 %middle.1 = f32[32,8,128]{2,1,0:T(8,128)} custom-call(f32[32,8,128]{2,1,0:T(8,128)S(1)} %all-to-all-done.1.data_ref, f32[2,32,32,128]{3,2,1,0:T(8,128)S(1)} %weights.1.weight_ref, bf16[2,64,256]{2,1,0:T(8,128)(2,1)S(1)} %copy-done.3, bf16[2,256,64]{2,1,0:T(8,128)(2,1)} %constant.15.clone.inverse_hbm), custom_call_target="tpu_custom_call" | custom-call | flops 3000000000 | tf_op jit(solution)/shard_map/middle/pallas_call | solution.py:527
  44.7 4.1 %all-to-all-start.2 = ((f32[32,8,128]{2,1,0:T(8,128)}), f32[32,8,128]{2,1,0:T(8,128)S(1)}, u32[]{:S(2)}, u32[]{:S(2)}) async-start(f32[32,8,128]{2,1,0:T(8,128)} %middle.1), calls=%async_computation.2 | async-start | bytes 262144 | tf_op jit(solution)/shard_map/all_to_all | solution.py:456
  48.8 0.0 collective-permute-done.inner_ref.inner_hbm
  48.8 3.1 %collective-permute-done.1.outer_ref.outer_hbm = f32[16,32,256]{2,1,0:T(8,128)} collective-permute-done((f32[16,32,256]{2,1,0:T(8,128)}, f32[16,32,256]{2,1,0:T(8,128)}, u32[]{:S(2)}, u32[]{:S(2)}) %collective-permute-start.1) | collective-permute-done | bytes 524320 | tf_op jit(solution)/shard_map/ppermute | solution.py:452
  51.9 0.0 copy-start
  51.9 1.1 %rims.1 = (f32[6,32,256]{2,1,0:T(8,128)S(1)}, f32[6,32,256]{2,1,0:T(8,128)S(1)}) custom-call(f32[2,4,32,256]{3,2,1,0:T(8,128)} %get-tuple-element.38.rows_ref, f32[16,32,256]{2,1,0:T(8,128)} %collective-permute-done.inner_ref.inner_hbm, f32[16,32,256]{2,1,0:T(8,128)} %collective-permute-done.1.outer_ref.outer_hbm), custom_call_target="tpu_custom_call" | custom-call | flops 2000000000 | tf_op jit(solution)/shard_map/rims/pallas_call | solution.py:539
  53.0 1.3 %collective-permute-start.2 = (f32[6,32,256]{2,1,0:T(8,128)S(1)}, f32[6,32,256]{2,1,0:T(8,128)S(1)}, u32[]{:S(2)}, u32[]{:S(2)}) collective-permute-start(f32[6,32,256]{2,1,0:T(8,128)S(1)} %get-tuple-element.43), channel_id=1, source_target_pairs={{0,1},{2,3},{4,5},{6,7},{1,0},{3,2},{5,4},{7,6},{8,9},{10,11},{12,... | collective-permute-start | bytes 589832 | tf_op jit(solution)/shard_map/ppermute | solution.py:452
  54.3 2.1 %collective-permute-start.3 = (f32[6,32,256]{2,1,0:T(8,128)S(1)}, f32[6,32,256]{2,1,0:T(8,128)S(1)}, u32[]{:S(2)}, u32[]{:S(2)}) collective-permute-start(f32[6,32,256]{2,1,0:T(8,128)S(1)} %get-tuple-element.44), channel_id=1, source_target_pairs={{1,2},{3,4},{5,6},{7,0},{2,1},{4,3},{6,5},{0,7},{9,10},{11,12},{13... | collective-permute-start | bytes 589832 | tf_op jit(solution)/shard_map/ppermute | solution.py:452
  56.3 1.9 %all-to-all-done.2.data_ref = f32[32,8,128]{2,1,0:T(8,128)S(1)} async-done(((f32[32,8,128]{2,1,0:T(8,128)}), f32[32,8,128]{2,1,0:T(8,128)S(1)}, u32[]{:S(2)}, u32[]{:S(2)}) %all-to-all-start.2) | async-done | bytes 131104 | tf_op jit(solution)/shard_map/all_to_all | solution.py:456
  58.3 0.0 copy-done
  58.3 1.1 %inverse_y.1 = f32[8,16,8,128]{3,2,1,0:T(8,128)} custom-call(f32[32,8,128]{2,1,0:T(8,128)S(1)} %all-to-all-done.2.data_ref, bf16[2,256,64]{2,1,0:T(8,128)(2,1)S(1)} %copy-done), custom_call_target="tpu_custom_call" | custom-call | tf_op jit(solution)/shard_map/inverse_y/pallas_call | solution.py:550
  59.4 3.7 %all-to-all-start.3 = ((f32[8,16,8,128]{3,2,1,0:T(8,128)}), f32[8,16,8,128]{3,2,1,0:T(8,128)S(1)}, u32[]{:S(2)}, u32[]{:S(2)}) async-start(f32[8,16,8,128]{3,2,1,0:T(8,128)} %inverse_y.1), calls=%async_computation.3 | async-start | bytes 1048576 | tf_op jit(solution)/shard_map/all_to_all | solution.py:456
  63.1 0.0 collective-permute-done.2.inner_rim
  63.1 1.1 %collective-permute-done.3.outer_rim = f32[6,32,256]{2,1,0:T(8,128)S(1)} collective-permute-done((f32[6,32,256]{2,1,0:T(8,128)S(1)}, f32[6,32,256]{2,1,0:T(8,128)S(1)}, u32[]{:S(2)}, u32[]{:S(2)}) %collective-permute-start.3) | collective-permute-done | bytes 196640 | tf_op jit(solution)/shard_map/ppermute | solution.py:452
  64.2 0.0 copy-start.1
  64.2 3.6 %edge_cells.1.base_ref = f32[4,16,32,256]{3,2,1,0:T(8,128)S(1)} custom-call(f32[4,16,32,256]{3,2,1,0:T(8,128)S(1)} %get-tuple-element.46.base_ref, f32[16,32,256]{2,1,0:T(8,128)} %collective-permute-done.inner_ref.inner_hbm, f32[16,32,256]{2,1,0:T(8,128)} %collective-permute-done.1.outer_ref.outer_hbm, ...), custom_call_target="tpu_custom_call", output_to_operand_aliasing={{}: (0, {})} | custom-call | flops 40000000000 | tf_op jit(solution)/shard_map/edge_cells/pallas_call | solution.py:560
  67.8 6.0 %all-to-all-done.3.data_ref = f32[8,16,8,128]{3,2,1,0:T(8,128)S(1)} async-done(((f32[8,16,8,128]{3,2,1,0:T(8,128)}), f32[8,16,8,128]{3,2,1,0:T(8,128)S(1)}, u32[]{:S(2)}, u32[]{:S(2)}) %all-to-all-start.3) | async-done | bytes 524320 | tf_op jit(solution)/shard_map/all_to_all | solution.py:456
  73.8 0.0 copy-done.1
  73.8 3.1 %final.1 = f32[128,16,256]{2,1,0:T(8,128)} custom-call(f32[8,16,8,128]{3,2,1,0:T(8,128)S(1)} %all-to-all-done.3.data_ref, f32[4,16,32,256]{3,2,1,0:T(8,128)S(1)} %edge_cells.1.base_ref, bf16[2,64,256]{2,1,0:T(8,128)(2,1)S(1)} %copy-done.1), custom_call_target="tpu_custom_call" | custom-call | tf_op jit(solution)/shard_map/final/pallas_call | solution.py:574
Async XLA Ops:
  3.8 18.2 %all-to-all-start = ((f32[8,16,8,128]{3,2,1,0:T(8,128)}), f32[8,16,8,128]{3,2,1,0:T(8,128)S(1)}, u32[]{:S(2)}, u32[]{:S(2)}) async-start(f32[8,16,8,128]{3,2,1,0:T(8,128)} %forward_z.1), calls=%async_computation | async-start | bytes 1048576 | tf_op jit(solution)/shard_map/all_to_all | solution.py:456
  11.3 10.7 %copy-start.2 = (bf16[2,64,256]{2,1,0:T(8,128)(2,1)S(1)}, bf16[2,64,256]{2,1,0:T(8,128)(2,1)}, u32[]{:S(2)}) copy-start(bf16[2,64,256]{2,1,0:T(8,128)(2,1)} %constant.13.clone.table_ref) | copy-start | bytes 196612
  23.0 19.8 %all-to-all-start.1 = ((f32[32,8,128]{2,1,0:T(8,128)}), f32[32,8,128]{2,1,0:T(8,128)S(1)}, u32[]{:S(2)}, u32[]{:S(2)}) async-start(f32[32,8,128]{2,1,0:T(8,128)} %forward_y.1), calls=%async_computation.1 | async-start | bytes 262144 | tf_op jit(solution)/shard_map/all_to_all | solution.py:456
  33.5 9.3 %copy-start.3 = (bf16[2,64,256]{2,1,0:T(8,128)(2,1)S(1)}, bf16[2,64,256]{2,1,0:T(8,128)(2,1)}, u32[]{:S(2)}) copy-start(bf16[2,64,256]{2,1,0:T(8,128)(2,1)} %constant.14.clone.forward_ref) | copy-start | bytes 196612
  36.6 12.3 %collective-permute-start = (f32[16,32,256]{2,1,0:T(8,128)}, f32[16,32,256]{2,1,0:T(8,128)}, u32[]{:S(2)}, u32[]{:S(2)}) collective-permute-start(f32[16,32,256]{2,1,0:T(8,128)} %get-tuple-element.39), channel_id=1, source_target_pairs={{0,8},{16,24},{32,40},{48,56},{64,72},{80,88},{96,104},{112,120},{... | collective-permute-start | bytes 1572872 | tf_op jit(solution)/shard_map/ppermute | solution.py:452
  36.9 15.0 %collective-permute-start.1 = (f32[16,32,256]{2,1,0:T(8,128)}, f32[16,32,256]{2,1,0:T(8,128)}, u32[]{:S(2)}, u32[]{:S(2)}) collective-permute-start(f32[16,32,256]{2,1,0:T(8,128)} %get-tuple-element.40), channel_id=1, source_target_pairs={{8,16},{24,32},{40,48},{56,64},{72,80},{88,96},{104,112},{120,128}... | collective-permute-start | bytes 1572872 | tf_op jit(solution)/shard_map/ppermute | solution.py:452
  44.7 13.6 %all-to-all-start.2 = ((f32[32,8,128]{2,1,0:T(8,128)}), f32[32,8,128]{2,1,0:T(8,128)S(1)}, u32[]{:S(2)}, u32[]{:S(2)}) async-start(f32[32,8,128]{2,1,0:T(8,128)} %middle.1), calls=%async_computation.2 | async-start | bytes 262144 | tf_op jit(solution)/shard_map/all_to_all | solution.py:456
  51.9 6.4 %copy-start = (bf16[2,256,64]{2,1,0:T(8,128)(2,1)S(1)}, bf16[2,256,64]{2,1,0:T(8,128)(2,1)}, u32[]{:S(2)}) copy-start(bf16[2,256,64]{2,1,0:T(8,128)(2,1)} %constant.16.clone.table_ref) | copy-start | bytes 196612
  53.0 10.1 %collective-permute-start.2 = (f32[6,32,256]{2,1,0:T(8,128)S(1)}, f32[6,32,256]{2,1,0:T(8,128)S(1)}, u32[]{:S(2)}, u32[]{:S(2)}) collective-permute-start(f32[6,32,256]{2,1,0:T(8,128)S(1)} %get-tuple-element.43), channel_id=1, source_target_pairs={{0,1},{2,3},{4,5},{6,7},{1,0},{3,2},{5,4},{7,6},{8,9},{10,11},{12,... | collective-permute-start | bytes 589832 | tf_op jit(solution)/shard_map/ppermute | solution.py:452
  54.3 9.9 %collective-permute-start.3 = (f32[6,32,256]{2,1,0:T(8,128)S(1)}, f32[6,32,256]{2,1,0:T(8,128)S(1)}, u32[]{:S(2)}, u32[]{:S(2)}) collective-permute-start(f32[6,32,256]{2,1,0:T(8,128)S(1)} %get-tuple-element.44), channel_id=1, source_target_pairs={{1,2},{3,4},{5,6},{7,0},{2,1},{4,3},{6,5},{0,7},{9,10},{11,12},{13... | collective-permute-start | bytes 589832 | tf_op jit(solution)/shard_map/ppermute | solution.py:452
  59.4 14.4 %all-to-all-start.3 = ((f32[8,16,8,128]{3,2,1,0:T(8,128)}), f32[8,16,8,128]{3,2,1,0:T(8,128)S(1)}, u32[]{:S(2)}, u32[]{:S(2)}) async-start(f32[8,16,8,128]{3,2,1,0:T(8,128)} %inverse_y.1), calls=%async_computation.3 | async-start | bytes 1048576 | tf_op jit(solution)/shard_map/all_to_all | solution.py:456
  64.2 9.6 %copy-start.1 = (bf16[2,64,256]{2,1,0:T(8,128)(2,1)S(1)}, bf16[2,64,256]{2,1,0:T(8,128)(2,1)}, u32[]{:S(2)}) copy-start(bf16[2,64,256]{2,1,0:T(8,128)(2,1)} %constant.17.clone.table_ref) | copy-start | bytes 196612
